TPU v7x, 256 devices: a whole 4x4x8 slice. The times are simulated.
256 devices in a mesh: dp: 8 (over y, x_lo), expert: 32 (over x_hi, z, core).
Axes of the slice: x: 4 (x_hi: 2, x_lo: 2; x = x_hi * 2 + x_lo), y: 4, z: 8, core: 2. Of those that a mesh axis runs over, the one named last changes fastest.
Arguments:
- tokens: bfloat16 [32, 8, 12, 7168], P('expert', 'dp'), may hold values from -6 to 6
- cotangent: bfloat16 [32, 8, 12, 7168], P('expert', 'dp'), may hold values from -6 to 6
- w_gate: bfloat16 [32, 7168, 1024], P('expert', None, 'dp'), may hold values from -0.0625 to 0.0625
- w_up: bfloat16 [32, 7168, 1024], P('expert', None, 'dp'), may hold values from -0.0625 to 0.0625
- w_down: bfloat16 [32, 1024, 7168], P('expert', 'dp'), may hold values from -0.1875 to 0.1875
- routes: int32 [32, 8, 12, 2], P('expert', 'dp'), may hold values from 0 to 31, all different within a row; in each aligned block of 96 rows (0 to 95, 96 to 191, ..., all dimensions but the last counted through in order) at most 9 rows name the same one
- gates: int32 [32, 8, 12, 2], P('expert', 'dp'), may hold values from 4096 to 65535
- matching: int32 [32], replicated, may hold values from 0 to 31, as said below
Outputs:
- grad_input: bfloat16 [32, 8, 12, 7168], P('expert', 'dp')
- grad_gate: bfloat16 [32, 7168, 1024], P('expert', None, 'dp')
- grad_up: bfloat16 [32, 7168, 1024], P('expert', None, 'dp')
- grad_down: bfloat16 [32, 1024, 7168], P('expert', 'dp')
Inputs may be any that keep to these rules, and one draw needn't show every extreme that they name: Each token names 2 different experts. Within routes[c] for any c no expert is named more than 9 times. matching[j] is j, or j + 16 for j below 16, or j - 16 above; matching[matching[j]] = j, and the pair of slot 31 always differs from it.
All inputs are finite; a program needn't handle non-finite values.
Results may differ from a plain program's by a relative error of at most 0.019.
Values may be sent and summed in bfloat16 or wider, within the bound.
No kernel may reach another device: no remote copies, remote signals or barrier semaphores. Data moves between devices by JAX's collectives and lax.ppermute only.
A program may use at most 192 MiB of HBM per device.

v0:
```python
import jax
import jax.numpy as jnp
from jax import lax
from jax.sharding import PartitionSpec as P


def from_partner(x, axis, distance):
    return lax.ppermute(x, axis, [(i, i ^ 1 << distance) for i in range(lax.axis_size(axis))])


def column_places(route_flat, owner_table, expert_count, cap_col):
    choices_iota = jnp.arange(expert_count, dtype=jnp.int32)
    onehot = (route_flat[:, None] == choices_iota[None, :]).astype(jnp.int32)
    ranking = jnp.sum(jnp.cumsum(onehot, axis=0) * onehot, axis=1) - 1
    target = jnp.sum(onehot * owner_table[None, :], axis=1)
    position = target * cap_col + ranking
    slot_iota = jnp.arange(expert_count * cap_col, dtype=jnp.int32)
    return slot_iota[:, None] == position[None, :]


def contract_rows(left, right):
    return lax.dot_general(
        left, right, (((0,), (0,)), ((), ())), preferred_element_type=jnp.float32
    )


def contract_units(left, right):
    return lax.dot_general(
        left, right, (((1,), (1,)), ((), ())), preferred_element_type=jnp.float32
    )


def shards(tokens, cotangent, w_gate, w_up, w_down, routes, gates, matching):
    rows_here = tokens.shape[2]
    width = tokens.shape[3]
    topk = routes.shape[3]
    expert_count = lax.axis_size("expert")
    group_count = lax.axis_size("dp")
    cap_col = 3 * group_count * rows_here * topk // (2 * expert_count)
    slot_count = expert_count * cap_col
    column_tok = group_count * rows_here
    self_index = lax.axis_index("expert")
    pair_bit = expert_count.bit_length() - 2
    expert_iota = jnp.arange(expert_count, dtype=jnp.int32)
    partner = jnp.sum(jnp.where(expert_iota == self_index, matching, 0))
    flipped = partner != self_index
    weight_gate = w_gate[0]
    weight_up = w_up[0]
    weight_down = w_down[0]
    swapped = from_partner((weight_gate, weight_up, weight_down), "expert", pair_bit)
    weight_gate = jnp.where(flipped, swapped[0], weight_gate)
    weight_up = jnp.where(flipped, swapped[1], weight_up)
    weight_down = jnp.where(flipped, swapped[2], weight_down)
    labels = (
        lax.all_gather(routes, "dp", axis=1, tiled=True),
        lax.all_gather(gates, "dp", axis=1, tiled=True),
    )
    route_col = labels[0].reshape(column_tok * topk)
    gate_col = labels[1].reshape(column_tok, topk).astype(jnp.float32) / 65536.0
    places = column_places(route_col, matching, expert_count, cap_col)
    place_pick = places.astype(jnp.bfloat16)
    place_tok = jnp.any(places.reshape(slot_count, column_tok, topk), axis=2).astype(jnp.bfloat16)
    column = (
        lax.all_gather(tokens, "dp", axis=1, tiled=True),
        lax.all_gather(cotangent, "dp", axis=1, tiled=True),
    )
    col_in = column[0].reshape(column_tok, width)
    col_cot = column[1].reshape(column_tok, width)
    send_in = jnp.dot(place_tok, col_in, preferred_element_type=jnp.float32).astype(jnp.bfloat16)
    dy_pick = (gate_col[:, :, None] * col_cot[:, None, :].astype(jnp.float32)).astype(jnp.bfloat16)
    send_cot = jnp.dot(
        place_pick, dy_pick.reshape(column_tok * topk, width), preferred_element_type=jnp.float32
    ).astype(jnp.bfloat16)
    arrived = (
        lax.all_to_all(
            send_in.reshape(expert_count, cap_col, width),
            "expert",
            split_axis=0,
            concat_axis=0,
            tiled=True,
        ),
        lax.all_to_all(
            send_cot.reshape(expert_count, cap_col, width),
            "expert",
            split_axis=0,
            concat_axis=0,
            tiled=True,
        ),
    )
    routed_rows = arrived[0].reshape(slot_count, width)
    routed_cot = arrived[1].reshape(slot_count, width)
    gate_act = jnp.dot(routed_rows, weight_gate, preferred_element_type=jnp.float32)
    up_act = jnp.dot(routed_rows, weight_up, preferred_element_type=jnp.float32)
    sigmoid_gate = jax.nn.sigmoid(gate_act)
    hidden = (gate_act * sigmoid_gate * up_act).astype(jnp.bfloat16)
    grad_down_here = contract_rows(hidden, routed_cot).astype(jnp.bfloat16)
    d_hidden = contract_units(routed_cot, weight_down)
    d_gate = (d_hidden * up_act * sigmoid_gate * (1.0 + gate_act * (1.0 - sigmoid_gate))).astype(
        jnp.bfloat16
    )
    d_up = (d_hidden * gate_act * sigmoid_gate).astype(jnp.bfloat16)
    grad_gate_here = contract_rows(routed_rows, d_gate).astype(jnp.bfloat16)
    grad_up_here = contract_rows(routed_rows, d_up).astype(jnp.bfloat16)
    partial_terms = contract_units(d_gate, weight_gate) + contract_units(d_up, weight_up)
    parts = partial_terms.astype(jnp.bfloat16).reshape(expert_count, cap_col, width)
    back = lax.all_to_all(parts, "expert", split_axis=0, concat_axis=0, tiled=True)
    col_sum = contract_rows(place_tok, back.reshape(slot_count, width))
    total = lax.psum_scatter(
        col_sum.reshape(group_count, rows_here, width).astype(jnp.bfloat16),
        "dp",
        scatter_dimension=0,
        tiled=True,
    )
    return (
        total.reshape(1, 1, rows_here, width),
        grad_gate_here[None],
        grad_up_here[None],
        grad_down_here[None],
    )


def solution(mesh):
    placed = (
        P("expert", "dp", None, None),
        P("expert", "dp", None, None),
        P("expert", None, "dp"),
        P("expert", None, "dp"),
        P("expert", "dp", None),
        P("expert", "dp", None, None),
        P("expert", "dp", None, None),
        P(),
    )
    return jax.shard_map(
        shards,
        mesh=mesh,
        in_specs=placed,
        out_specs=(
            P("expert", "dp", None, None),
            P("expert", None, "dp"),
            P("expert", None, "dp"),
            P("expert", "dp", None),
        ),
        check_vma=False,
    )
```

profile of v0, /device:TPU:6, one launch (start us, length us, event | category | flops | bytes accessed | tf_op | source)
XLA Modules:
  0.0 709.9 jit_solution(8011210042714407718)
XLA Ops:
  7.9 16.5 %all_gather.12 = s32[1,8,12,2]{2,3,0,1:T(2,128)S(1)} all-gather(s32[1,1,12,2]{2,3,0,1:T(2,128)} %bitcast.72), channel_id=1, replica_groups=mesh['dp'=8,'expert'=32] {'dp'}, dimensions={1}, use_global_device_ids=true | all-gather | bytes 864 | tf_op jit(solution)/shard_map/all_gather | solution.py:55
  26.6 34.4 %all-gather.5.cloned.1.call-done = bf16[1,8,12,7168]{3,2,0,1:T(8,128)(2,1)} async-done(((bf16[1,1,12,7168]{3,2,0,1:T(8,128)(2,1)}), bf16[1,8,12,7168]{3,2,0,1:T(8,128)(2,1)}) %all-gather.5.cloned.1.call-update) | async-done | bytes 1376272 | tf_op jit(solution)/shard_map/all_gather | solution.py:64
  65.8 6.4 reshape.98
  72.2 10.4 %all-to-all-start.1 = ((bf16[32,9,7168]{2,1,0:T(8,128)(2,1)}), bf16[32,9,7168]{2,1,0:T(8,128)(2,1)}, u32[]{:S(2)}, u32[]{:S(2)}) async-start(bf16[32,9,7168]{2,1,0:T(8,128)(2,1)} %reshape.98), calls=%async_computation.1 | async-start | bytes 14680064 | tf_op jit(solution)/shard_map/all_to_all | solution.py:75
  83.3 25.7 %all_gather.13 = s32[1,8,12,2]{2,3,0,1:T(2,128)S(1)} all-gather(s32[1,1,12,2]{2,3,0,1:T(2,128)S(1)} %bitcast.73), channel_id=1, replica_groups=mesh['dp'=8,'expert'=32] {'dp'}, dimensions={1}, use_global_device_ids=true | all-gather | bytes 864 | tf_op jit(solution)/shard_map/all_gather | solution.py:56
  109.3 55.0 %all-gather.3.cloned.1.call-done = bf16[1,8,12,7168]{3,2,0,1:T(8,128)(2,1)} async-done(((bf16[1,1,12,7168]{3,2,0,1:T(8,128)(2,1)}), bf16[1,8,12,7168]{3,2,0,1:T(8,128)(2,1)}) %all-gather.3.cloned.1.call-update) | async-done | bytes 1376272 | tf_op jit(solution)/shard_map/all_gather | solution.py:65
  165.9 4.3 mul.69
  170.2 7.8 %mul.70 = f32[192,7168]{1,0:T(8,128)} reshape(f32[96,2,7168]{2,1,0:T(2,128)} %mul.69) | data formatting | bytes 11010048 | tf_op jit(solution)/shard_map/mul | solution.py:70
  177.9 5.9 convolution_convert_fusion.1
  183.8 6.4 reshape.95
  190.2 54.7 %all-to-all-done.1 = bf16[32,9,7168]{2,1,0:T(8,128)(2,1)} async-done(((bf16[32,9,7168]{2,1,0:T(8,128)(2,1)}), bf16[32,9,7168]{2,1,0:T(8,128)(2,1)}, u32[]{:S(2)}, u32[]{:S(2)}) %all-to-all-start.1) | async-done | bytes 4128800 | tf_op jit(solution)/shard_map/all_to_all | solution.py:75
  244.8 10.6 %all-to-all-start = ((bf16[32,9,7168]{2,1,0:T(8,128)(2,1)}), bf16[32,9,7168]{2,1,0:T(8,128)(2,1)}, u32[]{:S(2)}, u32[]{:S(2)}) async-start(bf16[32,9,7168]{2,1,0:T(8,128)(2,1)} %reshape.95), calls=%async_computation | async-start | bytes 14680064 | tf_op jit(solution)/shard_map/all_to_all | solution.py:82
  260.6 6.4 reshape.99
  267.0 150.7 %all-to-all-done = bf16[32,9,7168]{2,1,0:T(8,128)(2,1)} async-done(((bf16[32,9,7168]{2,1,0:T(8,128)(2,1)}), bf16[32,9,7168]{2,1,0:T(8,128)(2,1)}, u32[]{:S(2)}, u32[]{:S(2)}) %all-to-all-start) | async-done | bytes 4128800 | tf_op jit(solution)/shard_map/all_to_all | solution.py:82
  417.7 6.4 reshape.96
  424.1 3.6 fusion.10
  429.4 24.2 %collective-permute-done = bf16[128,7168]{1,0:T(8,128)(2,1)} collective-permute-done((bf16[128,7168]{1,0:T(8,128)(2,1)}, bf16[128,7168]{1,0:T(8,128)(2,1)}, u32[]{:S(2)}, u32[]{:S(2)}) %collective-permute-start) | collective-permute-done | bytes 1835040 | tf_op jit(solution)/shard_map/ppermute | solution.py:8
  459.4 6.4 reshape.100
  465.7 14.5 %all-to-all-start.2 = ((bf16[32,9,7168]{2,1,0:T(8,128)(2,1)}), bf16[32,9,7168]{2,1,0:T(8,128)(2,1)}, u32[]{:S(2)}, u32[]{:S(2)}) async-start(bf16[32,9,7168]{2,1,0:T(8,128)(2,1)} %reshape.100), calls=%async_computation.2 | async-start | bytes 14680064 | tf_op jit(solution)/shard_map/all_to_all | solution.py:106
  480.7 161.8 %all-to-all-done.2 = bf16[32,9,7168]{2,1,0:T(8,128)(2,1)} async-done(((bf16[32,9,7168]{2,1,0:T(8,128)(2,1)}), bf16[32,9,7168]{2,1,0:T(8,128)(2,1)}, u32[]{:S(2)}, u32[]{:S(2)}) %all-to-all-start.2) | async-done | bytes 4128800 | tf_op jit(solution)/shard_map/all_to_all | solution.py:106
  642.5 6.3 reshape.105
  648.8 4.6 convolution_convert_fusion.5
  653.5 4.7 fusion.3
  664.1 39.3 %reduce-scatter.2.cloned.1.call-done = bf16[1,12,7168]{2,1,0:T(8,128)(2,1)} async-done(((bf16[8,12,7168]{2,1,0:T(8,128)(2,1)}), bf16[1,12,7168]{2,1,0:T(8,128)(2,1)}) %reduce-scatter.2.cloned.1.call-update) | async-done | bytes 172048 | tf_op jit(solution)/shard_map/reduce_scatter | solution.py:108
  (56 shorter events, 28.7 us)
Async XLA Ops:
  7.2 53.9 %all-gather.5.cloned.1.call-start = ((), (), s32[]{:S(2)}) async-start(), calls=%async_computation.5 | async-start | bytes 2064384 | tf_op jit(solution)/shard_map/all_gather | solution.py:64
  72.2 11.1 %copy-start.5 = (s32[1,1,12,2]{2,3,1,0:T(2,128)S(1)}, s32[1,1,12,2]{2,3,1,0:T(2,128)}, u32[]{:S(2)}) copy-start(s32[1,1,12,2]{2,3,1,0:T(2,128)} %param.14) | copy-start | bytes 292
  72.2 172.7 %all-to-all-start.1 = ((bf16[32,9,7168]{2,1,0:T(8,128)(2,1)}), bf16[32,9,7168]{2,1,0:T(8,128)(2,1)}, u32[]{:S(2)}, u32[]{:S(2)}) async-start(bf16[32,9,7168]{2,1,0:T(8,128)(2,1)} %reshape.98), calls=%async_computation.1 | async-start | bytes 14680064 | tf_op jit(solution)/shard_map/all_to_all | solution.py:75
  82.5 81.7 %all-gather.3.cloned.1.call-start = ((), (), s32[]{:S(2)}) async-start(), calls=%async_computation.4 | async-start | bytes 2064384 | tf_op jit(solution)/shard_map/all_gather | solution.py:65
  190.2 65.2 %copy-start.3 = (bf16[1,7168,128]{2,1,0:T(8,128)(2,1)S(1)}, bf16[1,7168,128]{2,1,0:T(8,128)(2,1)}, u32[]{:S(2)}) copy-start(bf16[1,7168,128]{2,1,0:T(8,128)(2,1)} %param.10) | copy-start | bytes 5505028
  190.2 69.2 %copy-start.6 = (s32[32]{0:T(128)S(1)}, s32[32]{0:T(128)}, u32[]{:S(2)}) copy-start(s32[32]{0:T(128)} %param.15) | copy-start | bytes 388
  244.8 172.9 %all-to-all-start = ((bf16[32,9,7168]{2,1,0:T(8,128)(2,1)}), bf16[32,9,7168]{2,1,0:T(8,128)(2,1)}, u32[]{:S(2)}, u32[]{:S(2)}) async-start(bf16[32,9,7168]{2,1,0:T(8,128)(2,1)} %reshape.95), calls=%async_computation | async-start | bytes 14680064 | tf_op jit(solution)/shard_map/all_to_all | solution.py:82
  255.4 168.7 %collective-permute-start.2 = (bf16[7168,128]{1,0:T(8,128)(2,1)S(1)}, bf16[7168,128]{1,0:T(8,128)(2,1)}, u32[]{:S(2)}, u32[]{:S(2)}) collective-permute-start(bf16[7168,128]{1,0:T(8,128)(2,1)S(1)} %bitcast.67), channel_id=1, source_target_pairs={{0,16},{1,17},{2,18},{3,19},{4,20},{5,21},{6,22},{7,23},{8,24},{9,... | collective-permute-start | bytes 5505032 | tf_op jit(solution)/shard_map/ppermute | solution.py:8
  255.8 171.9 %collective-permute-start.1 = (bf16[7168,128]{1,0:T(8,128)(2,1)}, bf16[7168,128]{1,0:T(8,128)(2,1)}, u32[]{:S(2)}, u32[]{:S(2)}) collective-permute-start(bf16[7168,128]{1,0:T(8,128)(2,1)} %bitcast.68), channel_id=1, source_target_pairs={{0,16},{1,17},{2,18},{3,19},{4,20},{5,21},{6,22},{7,23},{8,24},{9,... | collective-permute-start | bytes 5505032 | tf_op jit(solution)/shard_map/ppermute | solution.py:8
  259.0 194.5 %collective-permute-start = (bf16[128,7168]{1,0:T(8,128)(2,1)}, bf16[128,7168]{1,0:T(8,128)(2,1)}, u32[]{:S(2)}, u32[]{:S(2)}) collective-permute-start(bf16[128,7168]{1,0:T(8,128)(2,1)} %bitcast.74), channel_id=1, source_target_pairs={{0,16},{1,17},{2,18},{3,19},{4,20},{5,21},{6,22},{7,23},{8,24},{9,... | collective-permute-start | bytes 5505032 | tf_op jit(solution)/shard_map/ppermute | solution.py:8
  424.1 3.6 copy-start
  424.1 4.0 copy-start.4
  427.7 25.9 %copy-start.2 = (bf16[288,7168]{1,0:T(8,128)(2,1)S(1)}, bf16[288,7168]{1,0:T(8,128)(2,1)}, u32[]{:S(2)}) copy-start(bf16[288,7168]{1,0:T(8,128)(2,1)} %reshape.96) | copy-start | bytes 12386308
  427.7 25.9 %copy-start.7 = (bf16[1,128,7168]{2,1,0:T(8,128)(2,1)S(1)}, bf16[1,128,7168]{2,1,0:T(8,128)(2,1)}, u32[]{:S(2)}) copy-start(bf16[1,128,7168]{2,1,0:T(8,128)(2,1)} %param.12) | copy-start | bytes 5505028
  465.7 176.8 %all-to-all-start.2 = ((bf16[32,9,7168]{2,1,0:T(8,128)(2,1)}), bf16[32,9,7168]{2,1,0:T(8,128)(2,1)}, u32[]{:S(2)}, u32[]{:S(2)}) async-start(bf16[32,9,7168]{2,1,0:T(8,128)(2,1)} %reshape.100), calls=%async_computation.2 | async-start | bytes 14680064 | tf_op jit(solution)/shard_map/all_to_all | solution.py:106
  480.3 223.2 %reduce-scatter.2.cloned.1.call-start = ((), (), s32[]{:S(2)}) async-start(), calls=%async_computation.6 | async-start | bytes 2064384 | tf_op jit(solution)/shard_map/reduce_scatter | solution.py:108
  653.4 4.8 copy-start.1
Sparse Core Ops, SparseCore 0:
  9.8 51.2 all-gather.4
  85.2 79.0 all-gather.2
  653.6 49.7 reduce-scatter.1
where the time goes:
time: 713 us; the launch traced here: 710 us
  waiting for transfers between devices  521 us (73%)
  local copies, waits for them, and re-layouts  55 us (8%)
  blocking collectives  42.1 us (6%)
  starting transfers between devices  39.7 us (6%)
  matrix products  34.9 us (5%)
  between operations  14.6 us (2%)
    all_to_all x1, waiting for transfers between devices, shards(): lax.all_to_all(parts, 'expert', split_axis=0, concat_axis=0, tiled=True)  162 us
    all_to_all x1, waiting for transfers between devices, shards(): lax.all_to_all(send_cot.reshape(expert_count, cap_col, width), 'expert',...  151 us
    all_gather x1, waiting for transfers between devices, shards(): lax.all_gather(cotangent, 'dp', axis=1, tiled=True)  55 us
    all_to_all x1, waiting for transfers between devices, shards(): lax.all_to_all(send_in.reshape(expert_count, cap_col, width), 'expert', s...  54.7 us
    reduce_scatter x1, waiting for transfers between devices, shards(): lax.psum_scatter(col_sum.reshape(group_count, rows_here, width).astype(jn...  39.3 us
    all_gather x1, waiting for transfers between devices, shards(): lax.all_gather(tokens, 'dp', axis=1, tiled=True)  34.4 us
    all_gather x1, blocking collectives, shards(): lax.all_gather(gates, 'dp', axis=1, tiled=True)  25.7 us
    ppermute x3, waiting for transfers between devices, from_partner(): lax.ppermute(x, axis, [(i, i ^ 1 << distance) for i in range(lax.axis_siz...  24.2 us
  transfers between devices with their start and end apart: 9, of which 7 were waited for; matrix products, arithmetic and copies ran while one was open for 8% of the time, Pallas kernels for 0%

commit v1 on v0

v1 whole, which is shorter than its diff:
```python
import jax
import jax.numpy as jnp
from jax import lax
from jax.experimental import pallas as pl
from jax.experimental.pallas import tpu as pltpu
from jax.sharding import PartitionSpec as P

LANES = 128
BF = jnp.bfloat16
F32 = jnp.float32


def dot(a, b, dims):
    return lax.dot_general(a, b, (dims, ((), ())), preferred_element_type=F32)


def hop(x, axis, step, size):
    return lax.ppermute(x, axis, [(i, (i + step) % size) for i in range(size)])


def flip(x, axis, bit, size):
    return lax.ppermute(x, axis, [(i, i ^ bit) for i in range(size)])


def to_chunks(x, experts, low):
    parts = x.shape[1] // LANES
    head = x[: experts * low].reshape(experts, low, parts, LANES)
    head = head.transpose(0, 2, 1, 3).reshape(experts, low * parts, LANES)
    last = x[experts * low :].reshape(experts, parts, LANES)
    pad = -(low + 1) * parts % 16
    return jnp.concatenate([head, last, jnp.zeros((experts, pad, LANES), x.dtype)], axis=1)


def from_chunks(y, experts, low, parts):
    head = y[:, : low * parts].reshape(experts, parts, low, LANES)
    head = head.transpose(0, 2, 1, 3).reshape(experts * low, parts * LANES)
    last = y[:, low * parts : (low + 1) * parts].reshape(experts, parts * LANES)
    return jnp.concatenate([head, last], axis=0)


def gather_slices(x, me, size):
    mate = flip(x, "dp", 1, size)
    own_up, own_down = hop(x, "dp", 2, size), hop(x, "dp", -2, size)
    mate_up, mate_down = hop(mate, "dp", 2, size), hop(mate, "dp", -2, size)
    own_far, mate_far = hop(own_up, "dp", 2, size), hop(mate_down, "dp", -2, size)
    return (x, mate, own_up, own_down, mate_up, mate_down, own_far, mate_far)


def slice_ids(me, size):
    mate = me ^ 1
    wrap = lambda v: v % size
    return jnp.stack(
        [me, mate, wrap(me + size - 2), wrap(me + 2), wrap(mate + size - 2), wrap(mate + 2),
         wrap(me + size - 4), wrap(mate + 4)]
    ).astype(jnp.int32)


def act_kernel(ids, *refs):
    ins, (wg, wu, gate_ref, up_ref) = refs[:8], refs[8:]
    part = ins[0].shape[1]
    for k in range(8):
        at = pl.ds(pl.multiple_of(ids[k] * part, part), part)
        rows = ins[k][...]
        g = dot(rows, wg[at, :], ((1,), (0,)))
        u = dot(rows, wu[at, :], ((1,), (0,)))
        if k == 0:
            gate_ref[...] = g
            up_ref[...] = u
        else:
            gate_ref[...] += g
            up_ref[...] += u


def share_kernel(ids, *refs):
    cots = refs[:8]
    wg, wu, wd, gate_ref, up_ref, hid_ref, dg_ref, du_ref, share_ref, acc = refs[8:]
    part = cots[0].shape[1]
    for k in range(8):
        at = pl.ds(pl.multiple_of(ids[k] * part, part), part)
        h = dot(cots[k][...], wd[:, at], ((1,), (1,)))
        if k == 0:
            acc[...] = h
        else:
            acc[...] += h
    gate, up, d_hidden = gate_ref[...], up_ref[...], acc[...]
    s = jax.nn.sigmoid(gate)
    hid_ref[...] = (gate * s * up).astype(BF)
    dg_ref[...] = (d_hidden * up * s * (1.0 + gate * (1.0 - s))).astype(BF)
    du_ref[...] = (d_hidden * gate * s).astype(BF)
    for k in range(8):
        at = pl.ds(k * part, part)
        total = dot(dg_ref[...], wg[at, :], ((1,), (1,))) + dot(du_ref[...], wu[at, :], ((1,), (1,)))
        share_ref[k] = total.astype(BF)


def grad_kernel(ids, *refs):
    ins, cots = refs[:8], refs[8:16]
    hid, dg, du, gg_ref, gu_ref, gd_ref = refs[16:]
    part = ins[0].shape[1]
    for k in range(8):
        at = pl.ds(pl.multiple_of(ids[k] * part, part), part)
        rows = ins[k][...]
        gg_ref[at, :] = dot(rows, dg[...], ((0,), (0,))).astype(BF)
        gu_ref[at, :] = dot(rows, du[...], ((0,), (0,))).astype(BF)
        gd_ref[:, at] = dot(hid[...], cots[k][...], ((0,), (0,))).astype(BF)


def call(kernel, ids, args, outs, flops, scratch=()):
    vm = pl.BlockSpec(memory_space=pltpu.VMEM)
    size = lambda a: a.size * a.dtype.itemsize
    return pl.pallas_call(
        kernel,
        out_shape=outs,
        in_specs=[pl.BlockSpec(memory_space=pltpu.SMEM)] + [vm] * len(args),
        out_specs=jax.tree.map(lambda _: vm, outs),
        scratch_shapes=list(scratch),
        compiler_params=pltpu.CompilerParams(vmem_limit_bytes=48 << 20),
        cost_estimate=pl.CostEstimate(
            flops=flops, bytes_accessed=sum(map(size, args)) + sum(map(size, outs)), transcendentals=0
        ),
    )(ids, *args)


def shards(tokens, cotangent, w_gate, w_up, w_down, routes, gates, matching):
    n_tok, width = tokens.shape[2], tokens.shape[3]
    topk = routes.shape[3]
    experts, groups = lax.axis_size("expert"), lax.axis_size("dp")
    cap = 3 * groups * n_tok * topk // (2 * experts)
    low = cap - 1
    part = width // groups
    parts = part // LANES
    hidden = w_gate.shape[2]
    me_e, me_d = lax.axis_index("expert"), lax.axis_index("dp")
    expert_iota = jnp.arange(experts, dtype=jnp.int32)
    ids = slice_ids(me_d, groups)

    flipped = jnp.sum(jnp.where(expert_iota == me_e, matching, 0)) != me_e
    swap = lambda w: jnp.where(flipped, flip(w, "expert", experts // 2, experts), w)
    wg, wu, wd = swap(w_gate[0]), swap(w_up[0]), swap(w_down[0])

    split = lambda x: x.reshape(n_tok, groups, part).transpose(1, 0, 2)
    flat_gates = gates.reshape(-1)
    meta = jnp.concatenate([routes.reshape(-1), flat_gates // 256, flat_gates % 256]).astype(F32)
    meta = jnp.pad(meta, (0, part - meta.shape[0])).astype(BF)
    meta = jnp.broadcast_to(meta[None, None], (groups, 1, part))
    stride = 32
    pad = jnp.zeros((groups, stride - 2 * n_tok - 1, part), BF)
    packed = jnp.concatenate([split(tokens[0, 0]), split(cotangent[0, 0]), meta, pad], axis=1)
    column = lax.all_to_all(packed, "dp", split_axis=0, concat_axis=0, tiled=True)
    picks = n_tok * topk
    told = column[:, 2 * n_tok, : 3 * picks].astype(F32).reshape(groups, 3, picks)
    route = told[:, 0].reshape(-1).astype(jnp.int32)
    gate_of = (told[:, 1] * 256.0 + told[:, 2]).reshape(-1) / 65536.0
    count = groups * picks

    onehot = (route[:, None] == expert_iota[None, :]).astype(BF)
    order = jnp.arange(count, dtype=jnp.int32)
    before = (order[:, None] > order[None, :]).astype(BF)
    earlier = dot(before, onehot, ((1,), (0,)))
    rank = jnp.sum(earlier * onehot.astype(F32), axis=1).astype(jnp.int32)
    target = jnp.sum(jnp.where(route[:, None] == expert_iota[None, :], matching[None, :], 0), axis=1)
    slot = jnp.where(rank < low, target * low + rank, experts * low + target)
    slot_count = experts * cap
    slots = jnp.arange(slot_count, dtype=jnp.int32)
    gate_slot = jnp.sum(jnp.where(slots[:, None] == slot[None, :], gate_of[None, :], 0.0), axis=1)
    by_tok = slot.reshape(groups, n_tok, topk)

    def places(step, first):
        spread = jnp.pad(by_tok, ((0, 0), (first, step - first - n_tok), (0, 0)), constant_values=-1)
        spread = spread.reshape(groups * step, topk)
        hit = slots[:, None] == spread[None, :, 0]
        for k in range(1, topk):
            hit = hit | (slots[:, None] == spread[None, :, k])
        return hit.astype(BF)

    rows = column.reshape(groups * stride, part)
    send_in = dot(places(stride, 0), rows, ((1,), (0,))).astype(BF)
    send_cot = (dot(places(stride, n_tok), rows, ((1,), (0,))) * gate_slot[:, None]).astype(BF)

    def exchange(x):
        x = to_chunks(x, experts, low)
        x = lax.all_to_all(x, "expert", split_axis=0, concat_axis=0, tiled=True)
        return from_chunks(x, experts, low, parts)

    ins = gather_slices(exchange(send_in), me_d, groups)
    cots = gather_slices(exchange(send_cot), me_d, groups)

    unit = 2 * slot_count * width * hidden
    act = jax.ShapeDtypeStruct((slot_count, hidden), F32)
    narrow = jax.ShapeDtypeStruct((slot_count, hidden), BF)
    gate_act, up_act = call(act_kernel, ids, (*ins, wg, wu), (act, act), 2 * unit)
    hid, dg, du, share = call(
        share_kernel,
        ids,
        (*cots, wg, wu, wd, gate_act, up_act),
        (narrow, narrow, narrow, jax.ShapeDtypeStruct((groups, slot_count, part), BF)),
        3 * unit,
        [pltpu.VMEM((slot_count, hidden), F32)],
    )
    shapes = (jax.ShapeDtypeStruct(wg.shape, BF), jax.ShapeDtypeStruct(wu.shape, BF), jax.ShapeDtypeStruct(wd.shape, BF))
    grads = call(grad_kernel, ids, (*ins, *cots, hid, dg, du), shapes, 3 * unit)

    spread = lax.all_to_all(share, "dp", split_axis=0, concat_axis=0, tiled=True)
    summed = jnp.sum(spread.astype(F32), axis=0).astype(BF)
    back = exchange(summed)
    tok_rows = 16
    total = dot(places(tok_rows, 0), back, ((0,), (0,))).astype(BF)
    home = lax.all_to_all(total.reshape(groups, tok_rows, part), "dp", split_axis=0, concat_axis=0, tiled=True)
    grad_input = home[:, :n_tok].transpose(1, 0, 2).reshape(1, 1, n_tok, width)
    return grad_input, grads[0][None], grads[1][None], grads[2][None]


def solution(mesh):
    placed = (
        P("expert", "dp", None, None),
        P("expert", "dp", None, None),
        P("expert", None, "dp"),
        P("expert", None, "dp"),
        P("expert", "dp", None),
        P("expert", "dp", None, None),
        P("expert", "dp", None, None),
        P(),
    )
    return jax.shard_map(
        shards,
        mesh=mesh,
        in_specs=placed,
        out_specs=(
            P("expert", "dp", None, None),
            P("expert", None, "dp"),
            P("expert", None, "dp"),
            P("expert", "dp", None),
        ),
        check_vma=False,
    )
```

time: 713 us -> 351 us (0.49)
  waiting for transfers between devices: 521 us -> 184 us
  local copies, waits for them, and re-layouts: 55 us -> 15 us
  matrix products: 34.9 us -> 1.9 us
  Pallas kernels: 0 us -> 21.2 us
  starting transfers between devices: 39.7 us -> 56.6 us
  other arithmetic: 2.2 us -> 15.3 us
  between operations: 14.6 us -> 1.81 us
  blocking collectives: 42.1 us -> 52.1 us
    all_to_all x3 -> x5, waiting for transfers between devices: 367 us -> 105 us  [the longest x3 96.6 us: exchange(): x = lax.all_to_all(x, 'expert', split_axis=0, concat_axis=0, tiled=True)]
    all_gather x2 -> x0, waiting for transfers between devices: 89.4 us -> none  [the longest x1 55 us: shards(): lax.all_gather(cotangent, 'dp', axis=1, tiled=True)]
    ppermute x3 -> x17, waiting for transfers between devices: 24.2 us -> 79.3 us  [the longest x5 51 us: flip(): return lax.ppermute(x, axis, [(i, i ^ bit) for i in range(size)])]
    all_to_all x0 -> x1, blocking collectives: none -> 52.1 us  [shards(): lax.all_to_all(share, 'dp', split_axis=0, concat_axis=0, tiled=True)]
    all_gather x2 -> x0, blocking collectives: 42.1 us -> none  [the longest x1 25.7 us: shards(): lax.all_gather(gates, 'dp', axis=1, tiled=True)]
    reduce_scatter x1 -> x0, waiting for transfers between devices: 39.3 us -> none  [shards(): lax.psum_scatter(col_sum.reshape(group_count, rows_here, width).astype(jn...]
    reshape x7 -> x12, local copies, waits for them, and re-layouts: 39.8 us -> 2.5 us  [the longest x3 1.13 us: from_chunks(): head = head.transpose(0, 2, 1, 3).reshape(experts * low, parts * LANES)]
    dot_general x11 -> x4, matrix products: 34.9 us -> 1.9 us  [dot(): return lax.dot_general(a, b, (dims, ((), ())), preferred_element_type=F32)]
  transfers between devices with their start and end apart: 9 -> 22, of which waited for: 7 -> 10; matrix products, arithmetic and copies ran while one was open for 8% -> 3% of each run, Pallas kernels for 0% -> 4%
where the time goes in v1:
time: 351 us; the launch traced here: 348 us
  waiting for transfers between devices  184 us (52%)
  starting transfers between devices  56.6 us (16%)
  blocking collectives  52.1 us (15%)
  Pallas kernels  21.2 us (6%)
  other arithmetic  15.3 us (4%)
  local copies, waits for them, and re-layouts  15 us (4%)
    all_to_all x3, waiting for transfers between devices, exchange(): x = lax.all_to_all(x, 'expert', split_axis=0, concat_axis=0, tiled=True)  96.6 us
    all_to_all x1, blocking collectives, shards(): lax.all_to_all(share, 'dp', split_axis=0, concat_axis=0, tiled=True)  52.1 us
    ppermute x5, waiting for transfers between devices, flip(): return lax.ppermute(x, axis, [(i, i ^ bit) for i in range(size)])  51 us
    all_to_all x3, starting transfers between devices, exchange(): x = lax.all_to_all(x, 'expert', split_axis=0, concat_axis=0, tiled=True)  28.6 us
    ppermute x12, waiting for transfers between devices, hop(): return lax.ppermute(x, axis, [(i, (i + step) % size) for i in range(size)])  28.3 us
    pallas_call x3, Pallas kernels, call(): pl.pallas_call(kernel, out_shape=outs, in_specs=[pl.BlockSpec(memory_spac...  21.2 us
    ppermute x12, starting transfers between devices, hop(): return lax.ppermute(x, axis, [(i, (i + step) % size) for i in range(size)])  11.5 us
    unnamed x51, local copies, waits for them, and re-layouts  9.81 us
  transfers between devices with their start and end apart: 22, of which 10 were waited for; matrix products, arithmetic and copies ran while one was open for 3% of the time, Pallas kernels for 4%

profile of v1, /device:TPU:6, one launch (start us, length us, event | category | flops | bytes accessed | tf_op | source)
XLA Modules:
  0.0 347.9 jit_solution(6978285016101713151)
XLA Ops:
  5.5 5.9 %all-to-all-start = ((bf16[8,32,896]{2,1,0:T(8,128)(2,1)}), bf16[8,32,896]{2,1,0:T(8,128)(2,1)S(1)}, u32[]{:S(2)}, u32[]{:S(2)}) async-start(bf16[8,32,896]{2,1,0:T(8,128)(2,1)} %copy.42), calls=%async_computation | async-start | bytes 917504 | tf_op jit(solution)/shard_map/all_to_all | solution.py:149
  11.5 8.1 %all-to-all-done = bf16[8,32,896]{2,1,0:T(8,128)(2,1)S(1)} async-done(((bf16[8,32,896]{2,1,0:T(8,128)(2,1)}), bf16[8,32,896]{2,1,0:T(8,128)(2,1)S(1)}, u32[]{:S(2)}, u32[]{:S(2)}) %all-to-all-start) | async-done | bytes 458784 | tf_op jit(solution)/shard_map/all_to_all | solution.py:149
  23.4 11.6 %all-to-all-start.2 = ((bf16[32,64,128]{2,1,0:T(8,128)(2,1)}), bf16[32,64,128]{2,1,0:T(8,128)(2,1)S(1)}, u32[]{:S(2)}, u32[]{:S(2)}) async-start(bf16[32,64,128]{2,1,0:T(8,128)(2,1)} %get-tuple-element.30), calls=%async_computation.2 | async-start | bytes 1048576 | tf_op jit(solution)/shard_map/all_to_all | solution.py:182
  35.3 3.3 collective-permute-start.8
  38.6 13.6 %all-to-all-done.2 = bf16[32,64,128]{2,1,0:T(8,128)(2,1)S(1)} async-done(((bf16[32,64,128]{2,1,0:T(8,128)(2,1)}), bf16[32,64,128]{2,1,0:T(8,128)(2,1)S(1)}, u32[]{:S(2)}, u32[]{:S(2)}) %all-to-all-start.2) | async-done | bytes 524320 | tf_op jit(solution)/shard_map/all_to_all | solution.py:182
  52.2 6.6 %all-to-all-start.1 = ((bf16[32,64,128]{2,1,0:T(8,128)(2,1)}), bf16[32,64,128]{2,1,0:T(8,128)(2,1)S(1)}, u32[]{:S(2)}, u32[]{:S(2)}) async-start(bf16[32,64,128]{2,1,0:T(8,128)(2,1)} %get-tuple-element.31), calls=%async_computation.1 | async-start | bytes 1048576 | tf_op jit(solution)/shard_map/all_to_all | solution.py:182
  62.8 66.0 %all-to-all-done.1 = bf16[32,64,128]{2,1,0:T(8,128)(2,1)S(1)} async-done(((bf16[32,64,128]{2,1,0:T(8,128)(2,1)}), bf16[32,64,128]{2,1,0:T(8,128)(2,1)S(1)}, u32[]{:S(2)}, u32[]{:S(2)}) %all-to-all-start.1) | async-done | bytes 524320 | tf_op jit(solution)/shard_map/all_to_all | solution.py:182
  131.1 2.9 broadcast_select_fusion.refs_10_
  134.1 34.2 %collective-permute-done.7 = bf16[7168,128]{1,0:T(8,128)(2,1)} collective-permute-done((bf16[7168,128]{1,0:T(8,128)(2,1)}, bf16[7168,128]{1,0:T(8,128)(2,1)}, u32[]{:S(2)}, u32[]{:S(2)}) %collective-permute-start.7) | collective-permute-done | bytes 1835040 | tf_op jit(solution)/shard_map/ppermute | solution.py:22
  168.9 9.1 %collective-permute-done.10.refs_1_ = bf16[288,896]{1,0:T(8,128)(2,1)S(1)} collective-permute-done((bf16[288,896]{1,0:T(8,128)(2,1)S(1)}, bf16[288,896]{1,0:T(8,128)(2,1)S(1)}, u32[]{:S(2)}, u32[]{:S(2)}) %collective-permute-start.10) | collective-permute-done | bytes 516128 | tf_op jit(solution)/shard_map/ppermute | solution.py:22
  181.0 7.6 %collective-permute-done.refs_1_.refs_9_ = bf16[288,896]{1,0:T(8,128)(2,1)S(1)} collective-permute-done((bf16[288,896]{1,0:T(8,128)(2,1)S(1)}, bf16[288,896]{1,0:T(8,128)(2,1)S(1)}, u32[]{:S(2)}, u32[]{:S(2)}) %collective-permute-start) | collective-permute-done | bytes 516128 | tf_op jit(solution)/shard_map/ppermute | solution.py:22
  193.0 11.6 %collective-permute-done.15.refs_6_ = bf16[288,896]{1,0:T(8,128)(2,1)S(1)} collective-permute-done((bf16[288,896]{1,0:T(8,128)(2,1)}, bf16[288,896]{1,0:T(8,128)(2,1)S(1)}, u32[]{:S(2)}, u32[]{:S(2)}) %collective-permute-start.15) | collective-permute-done | bytes 516128 | tf_op jit(solution)/shard_map/ppermute | solution.py:18
  204.8 3.1 collective-permute-start.16
  209.8 2.9 broadcast_select_fusion.2.refs_8_
  212.7 12.7 %collective-permute-done.16.refs_7_ = bf16[288,896]{1,0:T(8,128)(2,1)S(1)} collective-permute-done((bf16[288,896]{1,0:T(8,128)(2,1)S(1)}, bf16[288,896]{1,0:T(8,128)(2,1)S(1)}, u32[]{:S(2)}, u32[]{:S(2)}) %collective-permute-start.16) | collective-permute-done | bytes 516128 | tf_op jit(solution)/shard_map/ppermute | solution.py:18
  225.4 4.8 %shard_map.111 = (f32[288,128]{1,0:T(8,128)S(1)}, f32[288,128]{1,0:T(8,128)S(1)}) custom-call(s32[8]{0:T(128)S(1)} %stack.35.ids, bf16[288,896]{1,0:T(8,128)(2,1)S(1)} %pad_maximum_fusion.1.refs_0_, bf16[288,896]{1,0:T(8,128)(2,1)S(1)} %collective-permute-done.10.refs_1_, bf16[288,896]{1,0:T(8,128)(2,1)} %collective-permute-done.11.refs_2_, ...), custom_call_target="tpu_custom_call" | custom-call | flops 1056964608 | bytes 8093696 | tf_op jit(solution)/shard_map/pallas_call | solution.py:111
  231.1 4.0 %collective-permute-done.6.refs_7_.refs_15_ = bf16[288,896]{1,0:T(8,128)(2,1)S(1)} collective-permute-done((bf16[288,896]{1,0:T(8,128)(2,1)S(1)}, bf16[288,896]{1,0:T(8,128)(2,1)S(1)}, u32[]{:S(2)}, u32[]{:S(2)}) %collective-permute-start.6) | collective-permute-done | bytes 516128 | tf_op jit(solution)/shard_map/ppermute | solution.py:18
  235.1 8.3 %shard_map.112 = (bf16[288,128]{1,0:T(8,128)(2,1)S(1)}, bf16[288,128]{1,0:T(8,128)(2,1)S(1)}, bf16[288,128]{1,0:T(8,128)(2,1)S(1)}, bf16[8,288,896]{2,1,0:T(8,128)(2,1)}) custom-call(s32[8]{0:T(128)S(1)} %stack.35.ids, bf16[288,896]{1,0:T(8,128)(2,1)S(1)} %pad_maximum_fusion.refs_0_.refs_8_, bf16[288,896]{1,0:T(8,128)(2,1)S(1)} %collective-permute-done.refs_1_.refs_9_, ...), custom_call_target="tpu_custom_call" | custom-call | flops 1585446912 | bytes 14278656 | tf_op jit(solution)/shard_map/pallas_call | solution.py:111
  243.4 52.1 %all_to_all.30 = bf16[8,288,896]{2,1,0:T(8,128)(2,1)} all-to-all(bf16[8,288,896]{2,1,0:T(8,128)(2,1)} %get-tuple-element.15), channel_id=1, replica_groups=mesh['dp'=8,'expert'=32] {'dp'}, dimensions={0} | all-to-all | bytes 8257536 | tf_op jit(solution)/shard_map/all_to_all | solution.py:203
  295.5 3.0 reduce_sum.52
  299.6 10.3 %all-to-all-start.4 = ((bf16[32,64,128]{2,1,0:T(8,128)(2,1)}), bf16[32,64,128]{2,1,0:T(8,128)(2,1)}, u32[]{:S(2)}, u32[]{:S(2)}) async-start(bf16[32,64,128]{2,1,0:T(8,128)(2,1)} %maximum_maximum_fusion.2), calls=%async_computation.4 | async-start | bytes 1048576 | tf_op jit(solution)/shard_map/all_to_all | solution.py:182
  310.2 17.0 %all-to-all-done.4 = bf16[32,64,128]{2,1,0:T(8,128)(2,1)} async-done(((bf16[32,64,128]{2,1,0:T(8,128)(2,1)}), bf16[32,64,128]{2,1,0:T(8,128)(2,1)}, u32[]{:S(2)}, u32[]{:S(2)}) %all-to-all-start.4) | async-done | bytes 524320 | tf_op jit(solution)/shard_map/all_to_all | solution.py:182
  330.1 4.5 %all-to-all-start.5 = ((bf16[8,16,896]{2,1,0:T(8,128)(2,1)}), bf16[8,16,896]{2,1,0:T(8,128)(2,1)S(1)}, u32[]{:S(2)}, u32[]{:S(2)}) async-start(bf16[8,16,896]{2,1,0:T(8,128)(2,1)} %bitcast.105), calls=%async_computation.5 | async-start | bytes 458752 | tf_op jit(solution)/shard_map/all_to_all | solution.py:208
  338.8 8.2 %shard_map.113 = (bf16[7168,128]{1,0:T(8,128)(2,1)}, bf16[7168,128]{1,0:T(8,128)(2,1)}, bf16[128,7168]{1,0:T(8,128)(2,1)}) custom-call(s32[8]{0:T(128)S(1)} %stack.35.ids, bf16[288,896]{1,0:T(8,128)(2,1)S(1)} %pad_maximum_fusion.1.refs_0_, bf16[288,896]{1,0:T(8,128)(2,1)S(1)} %copy-done.9, bf16[288,896]{1,0:T(8,128)(2,1)} %collective-permute-done.11.refs_2_, ...), custom_call_target="tpu_custom_call" | custom-call | flops 1585446912 | bytes 13983744 | tf_op jit(solution)/shard_map/pallas_call | solution.py:111
  (134 shorter events, 34.6 us)
Async XLA Ops:
  5.5 14.1 %all-to-all-start = ((bf16[8,32,896]{2,1,0:T(8,128)(2,1)}), bf16[8,32,896]{2,1,0:T(8,128)(2,1)S(1)}, u32[]{:S(2)}, u32[]{:S(2)}) async-start(bf16[8,32,896]{2,1,0:T(8,128)(2,1)} %copy.42), calls=%async_computation | async-start | bytes 917504 | tf_op jit(solution)/shard_map/all_to_all | solution.py:149
  23.4 28.8 %all-to-all-start.2 = ((bf16[32,64,128]{2,1,0:T(8,128)(2,1)}), bf16[32,64,128]{2,1,0:T(8,128)(2,1)S(1)}, u32[]{:S(2)}, u32[]{:S(2)}) async-start(bf16[32,64,128]{2,1,0:T(8,128)(2,1)} %get-tuple-element.30), calls=%async_computation.2 | async-start | bytes 1048576 | tf_op jit(solution)/shard_map/all_to_all | solution.py:182
  35.0 94.0 %collective-permute-start.9 = (bf16[128,7168]{1,0:T(8,128)(2,1)}, bf16[128,7168]{1,0:T(8,128)(2,1)}, u32[]{:S(2)}, u32[]{:S(2)}) collective-permute-start(bf16[128,7168]{1,0:T(8,128)(2,1)} %bitcast.25), channel_id=1, source_target_pairs={{0,16},{1,17},{2,18},{3,19},{4,20},{5,21},{6,22},{7,23},{8,24},{9,... | collective-permute-start | bytes 5505032 | tf_op jit(solution)/shard_map/ppermute | solution.py:22
  35.3 95.0 %collective-permute-start.8 = (bf16[7168,128]{1,0:T(8,128)(2,1)}, bf16[7168,128]{1,0:T(8,128)(2,1)}, u32[]{:S(2)}, u32[]{:S(2)}) collective-permute-start(bf16[7168,128]{1,0:T(8,128)(2,1)} %bitcast.24), channel_id=1, source_target_pairs={{0,16},{1,17},{2,18},{3,19},{4,20},{5,21},{6,22},{7,23},{8,24},{9,... | collective-permute-start | bytes 5505032 | tf_op jit(solution)/shard_map/ppermute | solution.py:22
  52.2 76.7 %all-to-all-start.1 = ((bf16[32,64,128]{2,1,0:T(8,128)(2,1)}), bf16[32,64,128]{2,1,0:T(8,128)(2,1)S(1)}, u32[]{:S(2)}, u32[]{:S(2)}) async-start(bf16[32,64,128]{2,1,0:T(8,128)(2,1)} %get-tuple-element.31), calls=%async_computation.1 | async-start | bytes 1048576 | tf_op jit(solution)/shard_map/all_to_all | solution.py:182
  58.8 109.5 %collective-permute-start.7 = (bf16[7168,128]{1,0:T(8,128)(2,1)}, bf16[7168,128]{1,0:T(8,128)(2,1)}, u32[]{:S(2)}, u32[]{:S(2)}) collective-permute-start(bf16[7168,128]{1,0:T(8,128)(2,1)} %bitcast.23), channel_id=1, source_target_pairs={{0,16},{1,17},{2,18},{3,19},{4,20},{5,21},{6,22},{7,23},{8,24},{9,... | collective-permute-start | bytes 5505032 | tf_op jit(solution)/shard_map/ppermute | solution.py:22
  60.7 118.1 %collective-permute-start.12 = (bf16[288,896]{1,0:T(8,128)(2,1)S(1)}, bf16[288,896]{1,0:T(8,128)(2,1)S(1)}, u32[]{:S(2)}, u32[]{:S(2)}) collective-permute-start(bf16[288,896]{1,0:T(8,128)(2,1)S(1)} %pad_maximum_fusion.1.refs_0_), channel_id=1, source_target_pairs={{0,192},{32,224},{64,0},{96,32},{128,64},{160,96},{192,128},{224,1... | collective-permute-start | bytes 1548296 | tf_op jit(solution)/shard_map/ppermute | solution.py:18
  62.0 118.9 %collective-permute-start.11 = (bf16[288,896]{1,0:T(8,128)(2,1)S(1)}, bf16[288,896]{1,0:T(8,128)(2,1)}, u32[]{:S(2)}, u32[]{:S(2)}) collective-permute-start(bf16[288,896]{1,0:T(8,128)(2,1)S(1)} %pad_maximum_fusion.1.refs_0_), channel_id=1, source_target_pairs={{0,64},{32,96},{64,128},{96,160},{128,192},{160,224},{192,0},{224,... | collective-permute-start | bytes 1548296 | tf_op jit(solution)/shard_map/ppermute | solution.py:18
  129.0 49.0 %collective-permute-start.10 = (bf16[288,896]{1,0:T(8,128)(2,1)S(1)}, bf16[288,896]{1,0:T(8,128)(2,1)S(1)}, u32[]{:S(2)}, u32[]{:S(2)}) collective-permute-start(bf16[288,896]{1,0:T(8,128)(2,1)S(1)} %pad_maximum_fusion.1.refs_0_), channel_id=1, source_target_pairs={{0,32},{32,0},{64,96},{96,64},{128,160},{160,128},{192,224},{224,1... | collective-permute-start | bytes 1548296 | tf_op jit(solution)/shard_map/ppermute | solution.py:22
  130.3 58.3 %collective-permute-start = (bf16[288,896]{1,0:T(8,128)(2,1)S(1)}, bf16[288,896]{1,0:T(8,128)(2,1)S(1)}, u32[]{:S(2)}, u32[]{:S(2)}) collective-permute-start(bf16[288,896]{1,0:T(8,128)(2,1)S(1)} %pad_maximum_fusion.refs_0_.refs_8_), channel_id=1, source_target_pairs={{0,32},{32,0},{64,96},{96,64},{128,160},{160,128},{192,224},{224,1... | collective-permute-start | bytes 1548296 | tf_op jit(solution)/shard_map/ppermute | solution.py:22
  168.3 24.1 %collective-permute-start.1 = (bf16[288,896]{1,0:T(8,128)(2,1)S(1)}, bf16[288,896]{1,0:T(8,128)(2,1)S(1)}, u32[]{:S(2)}, u32[]{:S(2)}) collective-permute-start(bf16[288,896]{1,0:T(8,128)(2,1)S(1)} %pad_maximum_fusion.refs_0_.refs_8_), channel_id=1, source_target_pairs={{0,64},{32,96},{64,128},{96,160},{128,192},{160,224},{192,0},{224,... | collective-permute-start | bytes 1548296 | tf_op jit(solution)/shard_map/ppermute | solution.py:18
  178.0 26.5 %collective-permute-start.14 = (bf16[288,896]{1,0:T(8,128)(2,1)S(1)}, bf16[288,896]{1,0:T(8,128)(2,1)S(1)}, u32[]{:S(2)}, u32[]{:S(2)}) collective-permute-start(bf16[288,896]{1,0:T(8,128)(2,1)S(1)} %collective-permute-done.10.refs_1_), channel_id=1, source_target_pairs={{0,192},{32,224},{64,0},{96,32},{128,64},{160,96},{192,128},{224,1... | collective-permute-start | bytes 1548296 | tf_op jit(solution)/shard_map/ppermute | solution.py:18
  179.7 25.1 %collective-permute-start.13 = (bf16[288,896]{1,0:T(8,128)(2,1)S(1)}, bf16[288,896]{1,0:T(8,128)(2,1)S(1)}, u32[]{:S(2)}, u32[]{:S(2)}) collective-permute-start(bf16[288,896]{1,0:T(8,128)(2,1)S(1)} %collective-permute-done.10.refs_1_), channel_id=1, source_target_pairs={{0,64},{32,96},{64,128},{96,160},{128,192},{160,224},{192,0},{224,... | collective-permute-start | bytes 1548296 | tf_op jit(solution)/shard_map/ppermute | solution.py:18
  180.9 23.6 %collective-permute-start.15 = (bf16[288,896]{1,0:T(8,128)(2,1)}, bf16[288,896]{1,0:T(8,128)(2,1)S(1)}, u32[]{:S(2)}, u32[]{:S(2)}) collective-permute-start(bf16[288,896]{1,0:T(8,128)(2,1)} %collective-permute-done.11.refs_2_), channel_id=1, source_target_pairs={{0,64},{32,96},{64,128},{96,160},{128,192},{160,224},{192,0},{224,... | collective-permute-start | bytes 1548296 | tf_op jit(solution)/shard_map/ppermute | solution.py:18
  188.6 19.3 %collective-permute-start.4 = (bf16[288,896]{1,0:T(8,128)(2,1)S(1)}, bf16[288,896]{1,0:T(8,128)(2,1)S(1)}, u32[]{:S(2)}, u32[]{:S(2)}) collective-permute-start(bf16[288,896]{1,0:T(8,128)(2,1)S(1)} %collective-permute-done.refs_1_.refs_9_), channel_id=1, source_target_pairs={{0,192},{32,224},{64,0},{96,32},{128,64},{160,96},{192,128},{224,1... | collective-permute-start | bytes 1548296 | tf_op jit(solution)/shard_map/ppermute | solution.py:18
  192.4 33.0 %copy-start.6 = (bf16[288,896]{1,0:T(8,128)(2,1)S(1)}, bf16[288,896]{1,0:T(8,128)(2,1)}, u32[]{:S(2)}) copy-start(bf16[288,896]{1,0:T(8,128)(2,1)} %copy-done.5) | copy-start | bytes 1548292
  192.4 38.6 %collective-permute-start.2 = (bf16[288,896]{1,0:T(8,128)(2,1)S(1)}, bf16[288,896]{1,0:T(8,128)(2,1)S(1)}, u32[]{:S(2)}, u32[]{:S(2)}) collective-permute-start(bf16[288,896]{1,0:T(8,128)(2,1)S(1)} %pad_maximum_fusion.refs_0_.refs_8_), channel_id=1, source_target_pairs={{0,192},{32,224},{64,0},{96,32},{128,64},{160,96},{192,128},{224,1... | collective-permute-start | bytes 1548296 | tf_op jit(solution)/shard_map/ppermute | solution.py:18
  204.5 26.5 %collective-permute-start.3 = (bf16[288,896]{1,0:T(8,128)(2,1)S(1)}, bf16[288,896]{1,0:T(8,128)(2,1)S(1)}, u32[]{:S(2)}, u32[]{:S(2)}) collective-permute-start(bf16[288,896]{1,0:T(8,128)(2,1)S(1)} %collective-permute-done.refs_1_.refs_9_), channel_id=1, source_target_pairs={{0,64},{32,96},{64,128},{96,160},{128,192},{160,224},{192,0},{224,... | collective-permute-start | bytes 1548296 | tf_op jit(solution)/shard_map/ppermute | solution.py:18
  204.5 26.5 %collective-permute-start.5 = (bf16[288,896]{1,0:T(8,128)(2,1)S(1)}, bf16[288,896]{1,0:T(8,128)(2,1)S(1)}, u32[]{:S(2)}, u32[]{:S(2)}) collective-permute-start(bf16[288,896]{1,0:T(8,128)(2,1)S(1)} %collective-permute-done.1.refs_2_.refs_10_), channel_id=1, source_target_pairs={{0,64},{32,96},{64,128},{96,160},{128,192},{160,224},{192,0},{224,... | collective-permute-start | bytes 1548296 | tf_op jit(solution)/shard_map/ppermute | solution.py:18
  204.8 20.6 %collective-permute-start.16 = (bf16[288,896]{1,0:T(8,128)(2,1)S(1)}, bf16[288,896]{1,0:T(8,128)(2,1)S(1)}, u32[]{:S(2)}, u32[]{:S(2)}) collective-permute-start(bf16[288,896]{1,0:T(8,128)(2,1)S(1)} %collective-permute-done.14.refs_5_), channel_id=1, source_target_pairs={{0,192},{32,224},{64,0},{96,32},{128,64},{160,96},{192,128},{224,1... | collective-permute-start | bytes 1548296 | tf_op jit(solution)/shard_map/ppermute | solution.py:18
  207.9 27.2 %copy-start = (bf16[288,896]{1,0:T(8,128)(2,1)}, bf16[288,896]{1,0:T(8,128)(2,1)S(1)}, u32[]{:S(2)}) copy-start(bf16[288,896]{1,0:T(8,128)(2,1)S(1)} %collective-permute-done.4.refs_5_.refs_13_) | copy-start | bytes 1548292
  207.9 27.2 %collective-permute-start.6 = (bf16[288,896]{1,0:T(8,128)(2,1)S(1)}, bf16[288,896]{1,0:T(8,128)(2,1)S(1)}, u32[]{:S(2)}, u32[]{:S(2)}) collective-permute-start(bf16[288,896]{1,0:T(8,128)(2,1)S(1)} %collective-permute-done.4.refs_5_.refs_13_), channel_id=1, source_target_pairs={{0,192},{32,224},{64,0},{96,32},{128,64},{160,96},{192,128},{224,1... | collective-permute-start | bytes 1548296 | tf_op jit(solution)/shard_map/ppermute | solution.py:18
  299.6 27.6 %all-to-all-start.4 = ((bf16[32,64,128]{2,1,0:T(8,128)(2,1)}), bf16[32,64,128]{2,1,0:T(8,128)(2,1)}, u32[]{:S(2)}, u32[]{:S(2)}) async-start(bf16[32,64,128]{2,1,0:T(8,128)(2,1)} %maximum_maximum_fusion.2), calls=%async_computation.4 | async-start | bytes 1048576 | tf_op jit(solution)/shard_map/all_to_all | solution.py:182
  330.1 16.8 %all-to-all-start.5 = ((bf16[8,16,896]{2,1,0:T(8,128)(2,1)}), bf16[8,16,896]{2,1,0:T(8,128)(2,1)S(1)}, u32[]{:S(2)}, u32[]{:S(2)}) async-start(bf16[8,16,896]{2,1,0:T(8,128)(2,1)} %bitcast.105), calls=%async_computation.5 | async-start | bytes 458752 | tf_op jit(solution)/shard_map/all_to_all | solution.py:208
  (17 other events, 183.4 us)

commit v2 on v1

v2 whole, which is shorter than its diff:
```python
import jax
import jax.numpy as jnp
from jax import lax
from jax.experimental import pallas as pl
from jax.experimental.pallas import tpu as pltpu
from jax.sharding import PartitionSpec as P

LANES = 128
BF = jnp.bfloat16
F32 = jnp.float32


def dot(a, b, dims):
    return lax.dot_general(a, b, (dims, ((), ())), preferred_element_type=F32)


def hop(x, axis, step, size):
    return lax.ppermute(x, axis, [(i, (i + step) % size) for i in range(size)])


def flip(x, axis, bit, size):
    return lax.ppermute(x, axis, [(i, i ^ bit) for i in range(size)])


def to_chunks(x, experts, low):
    parts = x.shape[1] // LANES
    head = x[: experts * low].reshape(experts, low, parts, LANES)
    head = head.transpose(0, 2, 1, 3).reshape(experts, low * parts, LANES)
    last = x[experts * low :].reshape(experts, parts, LANES)
    pad = -(low + 1) * parts % 16
    return jnp.concatenate([head, last, jnp.zeros((experts, pad, LANES), x.dtype)], axis=1)


def from_chunks(y, experts, low, parts):
    head = y[:, : low * parts].reshape(experts, parts, low, LANES)
    head = head.transpose(0, 2, 1, 3).reshape(experts * low, parts * LANES)
    last = y[:, low * parts : (low + 1) * parts].reshape(experts, parts * LANES)
    return jnp.concatenate([head, last], axis=0)


def gather_slices(x, me, size):
    mate = flip(x, "dp", 1, size)
    own_up, own_down = hop(x, "dp", 2, size), hop(x, "dp", -2, size)
    mate_up, mate_down = hop(mate, "dp", 2, size), hop(mate, "dp", -2, size)
    own_far, mate_far = hop(own_up, "dp", 2, size), hop(mate_down, "dp", -2, size)
    return (x, mate, own_up, own_down, mate_up, mate_down, own_far, mate_far)


def slice_ids(me, size):
    mate = me ^ 1
    wrap = lambda v: v % size
    return jnp.stack(
        [me, mate, wrap(me + size - 2), wrap(me + 2), wrap(mate + size - 2), wrap(mate + 2),
         wrap(me + size - 4), wrap(mate + 4)]
    ).astype(jnp.int32)


def partial_kernel(ids, *refs):
    rows_ref, blocks, out_ref = refs[0], refs[1:-1], refs[-1]
    part = rows_ref.shape[1] // 2
    ins, cots = rows_ref[:, :part], rows_ref[:, part:]
    for k, w in enumerate(blocks):
        gate = dot(ins, w[:part, :], ((1,), (0,)))
        up = dot(ins, w[part : 2 * part, :], ((1,), (0,)))
        down = 0.0
        for q in range(part // LANES):
            tile = w[2 * part + q * LANES : 2 * part + (q + 1) * LANES, :]
            down += dot(cots[:, q * LANES : (q + 1) * LANES], tile, ((1,), (1,)))
        out_ref[ids[k]] = jnp.concatenate([gate, up, down], axis=1).astype(BF)


def point_kernel(part_ref, trio_ref, spread_ref):
    total = part_ref[0].astype(F32)
    for k in range(1, part_ref.shape[0]):
        total += part_ref[k].astype(F32)
    unit = total.shape[1] // 3
    gate, up, d_hidden = total[:, :unit], total[:, unit : 2 * unit], total[:, 2 * unit :]
    s = jax.nn.sigmoid(gate)
    hid = (gate * s * up).astype(BF)
    dg = (d_hidden * up * s * (1.0 + gate * (1.0 - s))).astype(BF)
    du = (d_hidden * gate * s).astype(BF)
    trio_ref[...] = jnp.concatenate([hid, dg, du], axis=1)
    pair = jnp.concatenate([dg, du], axis=1)
    for k in range(part_ref.shape[0]):
        spread_ref[k] = pair


def share_kernel(ids, *refs):
    pairs, blocks, out_ref, acc = refs[0], refs[1:-2], refs[-2], refs[-1]
    part = out_ref.shape[1]
    unit = pairs.shape[2] // 2
    for k, w in enumerate(blocks):
        pair = pairs[ids[k]]
        total = dot(pair[:, :unit], w[:part, :], ((1,), (1,)))
        total += dot(pair[:, unit:], w[part : 2 * part, :], ((1,), (1,)))
        if k == 0:
            acc[...] = total
        else:
            acc[...] += total
    out_ref[...] = acc[...].astype(BF)


def grad_kernel(ids, *refs):
    rows = refs[:8]
    here, there, gg_ref, gu_ref, gd_ref = refs[8:]
    part = rows[0].shape[1] // 2
    trio = jnp.where(ids[8] != 0, there[...].astype(F32), here[...].astype(F32)).astype(BF)
    unit = trio.shape[1] // 3
    hid, dg, du = trio[:, :unit], trio[:, unit : 2 * unit], trio[:, 2 * unit :]
    for k in range(8):
        at = pl.ds(pl.multiple_of(ids[k] * part, part), part)
        gg_ref[at, :] = dot(rows[k][:, :part], dg, ((0,), (0,))).astype(BF)
        gu_ref[at, :] = dot(rows[k][:, :part], du, ((0,), (0,))).astype(BF)
        gd_ref[:, at] = dot(hid, rows[k][:, part:], ((0,), (0,))).astype(BF)


def call(kernel, scalars, args, outs, flops, scratch=()):
    vm = pl.BlockSpec(memory_space=pltpu.VMEM)
    size = lambda a: a.size * a.dtype.itemsize
    return pl.pallas_call(
        kernel,
        out_shape=outs,
        in_specs=[pl.BlockSpec(memory_space=pltpu.SMEM)] * len(scalars) + [vm] * len(args),
        out_specs=jax.tree.map(lambda _: vm, outs),
        scratch_shapes=list(scratch),
        compiler_params=pltpu.CompilerParams(vmem_limit_bytes=48 << 20),
        cost_estimate=pl.CostEstimate(
            flops=flops,
            bytes_accessed=sum(map(size, args)) + sum(map(size, jax.tree.leaves(outs))),
            transcendentals=0,
        ),
    )(*scalars, *args)


def shards(tokens, cotangent, w_gate, w_up, w_down, routes, gates, matching):
    n_tok, width = tokens.shape[2], tokens.shape[3]
    topk = routes.shape[3]
    experts, groups = lax.axis_size("expert"), lax.axis_size("dp")
    cap = 3 * groups * n_tok * topk // (2 * experts)
    low = cap - 1
    part = width // groups
    parts = part // LANES
    hidden = w_gate.shape[2]
    me_e, me_d = lax.axis_index("expert"), lax.axis_index("dp")
    expert_iota = jnp.arange(experts, dtype=jnp.int32)
    flipped = jnp.sum(jnp.where(expert_iota == me_e, matching, 0)) != me_e
    ids = jnp.concatenate([slice_ids(me_d, groups), flipped.astype(jnp.int32)[None]])
    across = lambda x: flip(x, "expert", experts // 2, experts)

    def block(t):
        cut = lambda w, axis: lax.dynamic_slice_in_dim(w, t * part, part, axis)
        down = cut(w_down[0], 1).reshape(hidden, parts, LANES).transpose(1, 0, 2)
        return jnp.concatenate([cut(w_gate[0], 0), cut(w_up[0], 0), down.reshape(part, LANES)], axis=0)

    blocks = [block(me_d)] + [flip(block(me_d ^ k), "dp", k, groups) for k in range(1, groups)]
    sources = jnp.stack([me_d ^ k for k in range(groups)]).astype(jnp.int32)

    split = lambda x: x.reshape(n_tok, groups, part).transpose(1, 0, 2)
    flat_gates = gates.reshape(-1)
    meta = jnp.concatenate([routes.reshape(-1), flat_gates // 256, flat_gates % 256]).astype(F32)
    meta = jnp.pad(meta, (0, part - meta.shape[0])).astype(BF)
    meta = jnp.broadcast_to(meta[None, None], (groups, 1, part))
    stride = 32
    pad = jnp.zeros((groups, stride - 2 * n_tok - 1, part), BF)
    packed = jnp.concatenate([split(tokens[0, 0]), split(cotangent[0, 0]), meta, pad], axis=1)
    column = lax.all_to_all(packed, "dp", split_axis=0, concat_axis=0, tiled=True)
    picks = n_tok * topk
    told = column[:, 2 * n_tok, : 3 * picks].astype(F32).reshape(groups, 3, picks)
    route = told[:, 0].reshape(-1).astype(jnp.int32)
    gate_of = (told[:, 1] * 256.0 + told[:, 2]).reshape(-1) / 65536.0
    count = groups * picks

    onehot = (route[:, None] == expert_iota[None, :]).astype(BF)
    order = jnp.arange(count, dtype=jnp.int32)
    before = (order[:, None] > order[None, :]).astype(BF)
    earlier = dot(before, onehot, ((1,), (0,)))
    rank = jnp.sum(earlier * onehot.astype(F32), axis=1).astype(jnp.int32)
    slot = jnp.where(rank < low, route * low + rank, experts * low + route)
    slot_count = experts * cap
    slots = jnp.arange(slot_count, dtype=jnp.int32)
    gate_slot = jnp.sum(jnp.where(slots[:, None] == slot[None, :], gate_of[None, :], 0.0), axis=1)

    def places(step, first):
        by_tok = slot.reshape(groups, n_tok, topk)
        spread = jnp.pad(by_tok, ((0, 0), (first, step - first - n_tok), (0, 0)), constant_values=-1)
        spread = spread.reshape(groups * step, topk)
        hit = slots[:, None] == spread[None, :, 0]
        for k in range(1, topk):
            hit = hit | (slots[:, None] == spread[None, :, k])
        return hit.astype(BF)

    rows = column.reshape(groups * stride, part)
    send_in = dot(places(stride, 0), rows, ((1,), (0,))).astype(BF)
    send_cot = (dot(places(stride, n_tok), rows, ((1,), (0,))) * gate_slot[:, None]).astype(BF)

    def exchange(x):
        x = to_chunks(x, experts, low)
        return lax.all_to_all(x, "expert", split_axis=0, concat_axis=0, tiled=True)

    both = from_chunks(
        exchange(jnp.concatenate([send_in, send_cot], axis=1)), experts, low, 2 * parts
    )
    unit = 2 * slot_count * width * hidden
    sums = call(
        partial_kernel, (sources,), (both, *blocks),
        jax.ShapeDtypeStruct((groups, slot_count, 3 * hidden), BF), 3 * unit,
    )
    sums = lax.all_to_all(sums, "dp", split_axis=0, concat_axis=0, tiled=True)
    trio, pairs = call(
        point_kernel, (), (sums,),
        (
            jax.ShapeDtypeStruct((slot_count, 3 * hidden), BF),
            jax.ShapeDtypeStruct((groups, slot_count, 2 * hidden), BF),
        ), unit // 100,
    )
    pairs = lax.all_to_all(pairs, "dp", split_axis=0, concat_axis=0, tiled=True)
    share = call(
        share_kernel, (sources,), (pairs, *blocks),
        jax.ShapeDtypeStruct((slot_count, part), BF), 2 * unit,
        [pltpu.VMEM((slot_count, part), F32)],
    )

    slot_rows = gather_slices(jnp.where(flipped, across(both), both), me_d, groups)
    shapes = tuple(jax.ShapeDtypeStruct(w.shape[1:], BF) for w in (w_gate, w_up, w_down))
    grads = call(grad_kernel, (ids,), (*slot_rows, trio, across(trio)), shapes, 3 * unit)

    back = from_chunks(exchange(share), experts, low, parts)
    tok_rows = 16
    total = dot(places(tok_rows, 0), back, ((0,), (0,))).astype(BF)
    mine = lax.all_to_all(total.reshape(groups, tok_rows, part), "dp", split_axis=0, concat_axis=0, tiled=True)
    grad_input = mine[:, :n_tok].transpose(1, 0, 2).reshape(1, 1, n_tok, width)
    return grad_input, grads[0][None], grads[1][None], grads[2][None]


def solution(mesh):
    placed = (
        P("expert", "dp", None, None),
        P("expert", "dp", None, None),
        P("expert", None, "dp"),
        P("expert", None, "dp"),
        P("expert", "dp", None),
        P("expert", "dp", None, None),
        P("expert", "dp", None, None),
        P(),
    )
    return jax.shard_map(
        shards,
        mesh=mesh,
        in_specs=placed,
        out_specs=(
            P("expert", "dp", None, None),
            P("expert", None, "dp"),
            P("expert", None, "dp"),
            P("expert", "dp", None),
        ),
        check_vma=False,
    )
```

time: 351 us -> 300 us (0.85)
  blocking collectives: 52.1 us -> 0 us
  waiting for transfers between devices: 184 us -> 158 us
  local copies, waits for them, and re-layouts: 15 us -> 32.1 us
  starting transfers between devices: 56.6 us -> 67.8 us
    all_to_all x3 -> x4, waiting for transfers between devices: 96.6 us -> 31.6 us  [the longest x2 21.7 us: exchange(): return lax.all_to_all(x, 'expert', split_axis=0, concat_axis=0, tiled=True)]
    ppermute x5 -> x10, waiting for transfers between devices: 51 us -> 103 us  [flip(): return lax.ppermute(x, axis, [(i, i ^ bit) for i in range(size)])]
    all_to_all x1 -> x0, blocking collectives: 52.1 us -> none  [shards(): lax.all_to_all(share, 'dp', split_axis=0, concat_axis=0, tiled=True)]
    ppermute x12 -> x6, waiting for transfers between devices: 28.3 us -> 0.02 us  [hop(): return lax.ppermute(x, axis, [(i, (i + step) % size) for i in range(size)])]
    all_to_all x1, waiting for transfers between devices: 0.01 us -> 23.1 us  [shards(): lax.all_to_all(total.reshape(groups, tok_rows, part), 'dp', split_axis=0,...]
    concatenate x0 -> x9, other arithmetic: none -> 10.6 us  [the longest x8 10.6 us: block(): jnp.concatenate([cut(w_gate[0], 0), cut(w_up[0], 0), down.reshape(part, L...]
    ppermute x5 -> x10, starting transfers between devices: 6.06 us -> 15 us  [flip(): return lax.ppermute(x, axis, [(i, i ^ bit) for i in range(size)])]
    all_to_all x1, waiting for transfers between devices: 8.14 us -> 0.01 us  [shards(): lax.all_to_all(packed, 'dp', split_axis=0, concat_axis=0, tiled=True)]
  transfers between devices with their start and end apart: 22 -> 22, of which waited for: 10 -> 8; matrix products, arithmetic and copies ran while one was open for 3% -> 13% of each run, Pallas kernels for 4% -> 1%
where the time goes in v2:
time: 300 us; the launch traced here: 298 us
  waiting for transfers between devices  158 us (53%)
  starting transfers between devices  67.8 us (23%)
  local copies, waits for them, and re-layouts  32.1 us (11%)
  Pallas kernels  19.3 us (6%)
  other arithmetic  16.8 us (6%)
    ppermute x10, waiting for transfers between devices, flip(): return lax.ppermute(x, axis, [(i, i ^ bit) for i in range(size)])  103 us
    all_to_all x1, waiting for transfers between devices, shards(): lax.all_to_all(total.reshape(groups, tok_rows, part), 'dp', split_axis=0,...  23.1 us
    all_to_all x2, starting transfers between devices, exchange(): return lax.all_to_all(x, 'expert', split_axis=0, concat_axis=0, tiled=True)  21.8 us
    all_to_all x2, waiting for transfers between devices, exchange(): return lax.all_to_all(x, 'expert', split_axis=0, concat_axis=0, tiled=True)  21.7 us
    pallas_call x4, Pallas kernels, call(): pl.pallas_call(kernel, out_shape=outs, in_specs=[pl.BlockSpec(memory_spac...  19.3 us
    ppermute x10, starting transfers between devices, flip(): return lax.ppermute(x, axis, [(i, i ^ bit) for i in range(size)])  15 us
    unnamed x74, local copies, waits for them, and re-layouts  12.2 us
    concatenate x8, other arithmetic, block(): jnp.concatenate([cut(w_gate[0], 0), cut(w_up[0], 0), down.reshape(part, L...  10.6 us
  transfers between devices with their start and end apart: 22, of which 8 were waited for; matrix products, arithmetic and copies ran while one was open for 13% of the time, Pallas kernels for 1%

profile of v2, /device:TPU:6, one launch (start us, length us, event | category | flops | bytes accessed | tf_op | source)
XLA Modules:
  0.0 297.7 jit_solution(17375366702088604933)
XLA Ops:
  5.4 5.9 %all-to-all-start = ((bf16[8,32,896]{2,1,0:T(8,128)(2,1)}), bf16[8,32,896]{2,1,0:T(8,128)(2,1)S(1)}, u32[]{:S(2)}, u32[]{:S(2)}) async-start(bf16[8,32,896]{2,1,0:T(8,128)(2,1)} %copy.132), calls=%async_computation | async-start | bytes 917504 | tf_op jit(solution)/shard_map/all_to_all | solution.py:166
  11.4 2.6 constant_dynamic-slice_fusion
  14.3 3.6 %dynamic-slice_bitcast_fusion = (bf16[896,128]{1,0:T(8,128)(2,1)}, bf16[896,128]{1,0:T(8,128)(2,1)}, bf16[896,128]{1,0:T(8,128)(2,1)}, bf16[896,128]{1,0:T(8,128...) fusion(bf16[1,7168,128]{2,1,0:T(8,128)(2,1)} %param.11, ...), kind=kLoop, calls=%fused_computation.38 | loop fusion | bytes 7340064 | tf_op jit(solution)/shard_map/dynamic_slice | solution.py:151
  26.7 11.8 %all-to-all-start.1 = ((bf16[32,128,128]{2,1,0:T(8,128)(2,1)}), bf16[32,128,128]{2,1,0:T(8,128)(2,1)}, u32[]{:S(2)}, u32[]{:S(2)}) async-start(bf16[32,128,128]{2,1,0:T(8,128)(2,1)} %maximum_maximum_fusion), calls=%async_computation.1 | async-start | bytes 2097152 | tf_op jit(solution)/shard_map/all_to_all | solution.py:198
  43.0 3.0 collective-permute-start.3
  55.7 10.1 %all-to-all-done.1 = bf16[32,128,128]{2,1,0:T(8,128)(2,1)} async-done(((bf16[32,128,128]{2,1,0:T(8,128)(2,1)}), bf16[32,128,128]{2,1,0:T(8,128)(2,1)}, u32[]{:S(2)}, u32[]{:S(2)}) %all-to-all-start.1) | async-done | bytes 1048608 | tf_op jit(solution)/shard_map/all_to_all | solution.py:198
  66.8 2.2 collective-permute-start.5
  68.9 2.1 collective-permute-start.6
  73.4 22.6 %collective-permute-done.3.refs_5_ = bf16[2688,128]{1,0:T(8,128)(2,1)} collective-permute-done((bf16[2688,128]{1,0:T(8,128)(2,1)}, bf16[2688,128]{1,0:T(8,128)(2,1)}, u32[]{:S(2)}, u32[]{:S(2)}) %collective-permute-start.3) | collective-permute-done | bytes 688160 | tf_op jit(solution)/shard_map/ppermute | solution.py:22
  96.0 23.2 %collective-permute-done.5.refs_7_ = bf16[2688,128]{1,0:T(8,128)(2,1)S(1)} collective-permute-done((bf16[2688,128]{1,0:T(8,128)(2,1)}, bf16[2688,128]{1,0:T(8,128)(2,1)S(1)}, u32[]{:S(2)}, u32[]{:S(2)}) %collective-permute-start.5) | collective-permute-done | bytes 688160 | tf_op jit(solution)/shard_map/ppermute | solution.py:22
  119.2 6.2 %shard_map.111 = bf16[8,288,384]{2,1,0:T(8,128)(2,1)} custom-call(s32[8]{0:T(128)S(1)} %stack.55.ids, bf16[288,1792]{1,0:T(8,128)(2,1)} %pad_maximum_fusion.refs_0_, bf16[2688,128]{1,0:T(8,128)(2,1)S(1)} %pad_maximum_fusion.1.refs_1_, bf16[2688,128]{1,0:T(8,128)(2,1)S(1)} %collective-permute-done.refs_2_, ...), custom_call_target="tpu_custom_call" | custom-call | flops 1585446912 | bytes 8306688 | tf_op jit(solution)/shard_map/pallas_call | solution.py:120
  127.2 5.3 %all-to-all-start.2 = ((bf16[8,288,384]{2,1,0:T(8,128)(2,1)}), bf16[8,288,384]{2,1,0:T(8,128)(2,1)S(1)}, u32[]{:S(2)}, u32[]{:S(2)}) async-start(bf16[8,288,384]{2,1,0:T(8,128)(2,1)} %shard_map.111), calls=%async_computation.2 | async-start | bytes 3538944 | tf_op jit(solution)/shard_map/all_to_all | solution.py:208
  134.4 41.5 %collective-permute-done.7 = bf16[288,1792]{1,0:T(8,128)(2,1)} collective-permute-done((bf16[288,1792]{1,0:T(8,128)(2,1)}, bf16[288,1792]{1,0:T(8,128)(2,1)}, u32[]{:S(2)}, u32[]{:S(2)}) %collective-permute-start.7) | collective-permute-done | bytes 1032224 | tf_op jit(solution)/shard_map/ppermute | solution.py:22
  179.5 6.3 %all-to-all-start.3 = ((bf16[8,288,256]{2,1,0:T(8,128)(2,1)}), bf16[8,288,256]{2,1,0:T(8,128)(2,1)}, u32[]{:S(2)}, u32[]{:S(2)}) async-start(bf16[8,288,256]{2,1,0:T(8,128)(2,1)} %copy-done.10), calls=%async_computation.3 | async-start | bytes 2359296 | tf_op jit(solution)/shard_map/all_to_all | solution.py:216
  187.4 16.0 %collective-permute-done.8.refs_1_ = bf16[288,1792]{1,0:T(8,128)(2,1)} collective-permute-done((bf16[288,1792]{1,0:T(8,128)(2,1)S(1)}, bf16[288,1792]{1,0:T(8,128)(2,1)}, u32[]{:S(2)}, u32[]{:S(2)}) %collective-permute-start.8) | collective-permute-done | bytes 1032224 | tf_op jit(solution)/shard_map/ppermute | solution.py:22
  205.1 9.9 %all-to-all-done.3.refs_0_ = bf16[8,288,256]{2,1,0:T(8,128)(2,1)} async-done(((bf16[8,288,256]{2,1,0:T(8,128)(2,1)}), bf16[8,288,256]{2,1,0:T(8,128)(2,1)}, u32[]{:S(2)}, u32[]{:S(2)}) %all-to-all-start.3) | async-done | bytes 1179680 | tf_op jit(solution)/shard_map/all_to_all | solution.py:216
  218.3 4.0 %shard_map.113 = bf16[288,896]{1,0:T(8,128)(2,1)S(1)} custom-call(s32[8]{0:T(128)S(1)} %stack.55.ids, bf16[8,288,256]{2,1,0:T(8,128)(2,1)} %all-to-all-done.3.refs_0_, bf16[2688,128]{1,0:T(8,128)(2,1)S(1)} %pad_maximum_fusion.1.refs_1_, bf16[2688,128]{1,0:T(8,128)(2,1)S(1)} %copy-done.1, bf16[2688,128]{1,0:T(8,128)(2,1)S(1)} %copy-done.3, ...), custom_call_target="tpu_custom_call" | custom-call | flops 1056964608 | bytes 7200768 | tf_op jit(solution)/shard_map/pallas_call | solution.py:120
  223.4 10.1 %all-to-all-start.4 = ((bf16[32,64,128]{2,1,0:T(8,128)(2,1)}), bf16[32,64,128]{2,1,0:T(8,128)(2,1)}, u32[]{:S(2)}, u32[]{:S(2)}) async-start(bf16[32,64,128]{2,1,0:T(8,128)(2,1)} %maximum_maximum_fusion.1), calls=%async_computation.4 | async-start | bytes 1048576 | tf_op jit(solution)/shard_map/all_to_all | solution.py:198
  235.7 3.2 %collective-permute-start.14 = (bf16[288,1792]{1,0:T(8,128)(2,1)}, bf16[288,1792]{1,0:T(8,128)(2,1)}, u32[]{:S(2)}, u32[]{:S(2)}) collective-permute-start(bf16[288,1792]{1,0:T(8,128)(2,1)} %collective-permute-done.12.refs_5_), channel_id=1, source_target_pairs={{0,192},{32,224},{64,0},{96,32},{128,64},{160,96},{192,128},{224,1... | collective-permute-start | bytes 3096584 | tf_op jit(solution)/shard_map/ppermute | solution.py:18
  239.1 11.6 %all-to-all-done.4 = bf16[32,64,128]{2,1,0:T(8,128)(2,1)} async-done(((bf16[32,64,128]{2,1,0:T(8,128)(2,1)}), bf16[32,64,128]{2,1,0:T(8,128)(2,1)}, u32[]{:S(2)}, u32[]{:S(2)}) %all-to-all-start.4) | async-done | bytes 524320 | tf_op jit(solution)/shard_map/all_to_all | solution.py:198
  253.7 4.9 %all-to-all-start.5 = ((bf16[8,16,896]{2,1,0:T(8,128)(2,1)}), bf16[8,16,896]{2,1,0:T(8,128)(2,1)}, u32[]{:S(2)}, u32[]{:S(2)}) async-start(bf16[8,16,896]{2,1,0:T(8,128)(2,1)} %bitcast.176), calls=%async_computation.5 | async-start | bytes 458752 | tf_op jit(solution)/shard_map/all_to_all | solution.py:230
  258.7 3.7 %collective-permute-start.15 = (bf16[288,384]{1,0:T(8,128)(2,1)S(1)}, bf16[288,384]{1,0:T(8,128)(2,1)}, u32[]{:S(2)}, u32[]{:S(2)}) collective-permute-start(bf16[288,384]{1,0:T(8,128)(2,1)S(1)} %copy-done.12), channel_id=1, source_target_pairs={{0,16},{1,17},{2,18},{3,19},{4,20},{5,21},{6,22},{7,23},{8,24},{9,... | collective-permute-start | bytes 663560 | tf_op jit(solution)/shard_map/ppermute | solution.py:22
  262.4 23.1 %all-to-all-done.5 = bf16[8,16,896]{2,1,0:T(8,128)(2,1)} async-done(((bf16[8,16,896]{2,1,0:T(8,128)(2,1)}), bf16[8,16,896]{2,1,0:T(8,128)(2,1)}, u32[]{:S(2)}, u32[]{:S(2)}) %all-to-all-start.5) | async-done | bytes 229408 | tf_op jit(solution)/shard_map/all_to_all | solution.py:230
  288.9 8.9 %shard_map.114 = (bf16[7168,128]{1,0:T(8,128)(2,1)}, bf16[7168,128]{1,0:T(8,128)(2,1)}, bf16[128,7168]{1,0:T(8,128)(2,1)}) custom-call(s32[9]{0:T(128)S(1)} %concatenate.63.ids, bf16[288,1792]{1,0:T(8,128)(2,1)S(1)} %broadcast_select_fusion.refs_0_, bf16[288,1792]{1,0:T(8,128)(2,1)} %collective-permute-done.8.refs_1_, ...), custom_call_target="tpu_custom_call" | custom-call | flops 1585446912 | bytes 14204928 | tf_op jit(solution)/shard_map/pallas_call | solution.py:120
  (175 shorter events, 54.4 us)
Async XLA Ops:
  5.4 17.1 %all-to-all-start = ((bf16[8,32,896]{2,1,0:T(8,128)(2,1)}), bf16[8,32,896]{2,1,0:T(8,128)(2,1)S(1)}, u32[]{:S(2)}, u32[]{:S(2)}) async-start(bf16[8,32,896]{2,1,0:T(8,128)(2,1)} %copy.132), calls=%async_computation | async-start | bytes 917504 | tf_op jit(solution)/shard_map/all_to_all | solution.py:166
  18.8 47.9 %collective-permute-start = (bf16[2688,128]{1,0:T(8,128)(2,1)}, bf16[2688,128]{1,0:T(8,128)(2,1)S(1)}, u32[]{:S(2)}, u32[]{:S(2)}) collective-permute-start(bf16[2688,128]{1,0:T(8,128)(2,1)} %pad_maximum_fusion.2), channel_id=1, source_target_pairs={{0,32},{32,0},{64,96},{96,64},{128,160},{160,128},{192,224},{224,1... | collective-permute-start | bytes 2064392 | tf_op jit(solution)/shard_map/ppermute | solution.py:22
  20.1 48.9 %collective-permute-start.1 = (bf16[2688,128]{1,0:T(8,128)(2,1)}, bf16[2688,128]{1,0:T(8,128)(2,1)S(1)}, u32[]{:S(2)}, u32[]{:S(2)}) collective-permute-start(bf16[2688,128]{1,0:T(8,128)(2,1)} %pad_maximum_fusion.3), channel_id=1, source_target_pairs={{0,64},{32,96},{64,0},{96,32},{128,192},{160,224},{192,128},{224,1... | collective-permute-start | bytes 2064392 | tf_op jit(solution)/shard_map/ppermute | solution.py:22
  26.7 39.1 %all-to-all-start.1 = ((bf16[32,128,128]{2,1,0:T(8,128)(2,1)}), bf16[32,128,128]{2,1,0:T(8,128)(2,1)}, u32[]{:S(2)}, u32[]{:S(2)}) async-start(bf16[32,128,128]{2,1,0:T(8,128)(2,1)} %maximum_maximum_fusion), calls=%async_computation.1 | async-start | bytes 2097152 | tf_op jit(solution)/shard_map/all_to_all | solution.py:198
  39.4 34.0 %collective-permute-start.2 = (bf16[2688,128]{1,0:T(8,128)(2,1)}, bf16[2688,128]{1,0:T(8,128)(2,1)S(1)}, u32[]{:S(2)}, u32[]{:S(2)}) collective-permute-start(bf16[2688,128]{1,0:T(8,128)(2,1)} %pad_maximum_fusion.4), channel_id=1, source_target_pairs={{0,96},{32,64},{64,32},{96,0},{128,224},{160,192},{192,160},{224,1... | collective-permute-start | bytes 2064392 | tf_op jit(solution)/shard_map/ppermute | solution.py:22
  43.0 53.0 %collective-permute-start.3 = (bf16[2688,128]{1,0:T(8,128)(2,1)}, bf16[2688,128]{1,0:T(8,128)(2,1)}, u32[]{:S(2)}, u32[]{:S(2)}) collective-permute-start(bf16[2688,128]{1,0:T(8,128)(2,1)} %pad_maximum_fusion.5), channel_id=1, source_target_pairs={{0,128},{32,160},{64,192},{96,224},{128,0},{160,32},{192,64},{224,... | collective-permute-start | bytes 2064392 | tf_op jit(solution)/shard_map/ppermute | solution.py:22
  48.3 47.7 %collective-permute-start.4 = (bf16[2688,128]{1,0:T(8,128)(2,1)}, bf16[2688,128]{1,0:T(8,128)(2,1)}, u32[]{:S(2)}, u32[]{:S(2)}) collective-permute-start(bf16[2688,128]{1,0:T(8,128)(2,1)} %pad_maximum_fusion.6), channel_id=1, source_target_pairs={{0,160},{32,128},{64,224},{96,192},{128,32},{160,0},{192,96},{224,... | collective-permute-start | bytes 2064392 | tf_op jit(solution)/shard_map/ppermute | solution.py:22
  66.8 52.4 %copy-start = (bf16[2688,128]{1,0:T(8,128)(2,1)}, bf16[2688,128]{1,0:T(8,128)(2,1)S(1)}, u32[]{:S(2)}) copy-start(bf16[2688,128]{1,0:T(8,128)(2,1)S(1)} %collective-permute-done.refs_2_) | copy-start | bytes 2064388
  66.8 52.4 %collective-permute-start.5 = (bf16[2688,128]{1,0:T(8,128)(2,1)}, bf16[2688,128]{1,0:T(8,128)(2,1)S(1)}, u32[]{:S(2)}, u32[]{:S(2)}) collective-permute-start(bf16[2688,128]{1,0:T(8,128)(2,1)} %pad_maximum_fusion.7), channel_id=1, source_target_pairs={{0,192},{32,224},{64,128},{96,160},{128,64},{160,96},{192,0},{224,... | collective-permute-start | bytes 2064392 | tf_op jit(solution)/shard_map/ppermute | solution.py:22
  68.9 50.3 %collective-permute-start.6 = (bf16[2688,128]{1,0:T(8,128)(2,1)}, bf16[2688,128]{1,0:T(8,128)(2,1)S(1)}, u32[]{:S(2)}, u32[]{:S(2)}) collective-permute-start(bf16[2688,128]{1,0:T(8,128)(2,1)} %pad_maximum_fusion.8), channel_id=1, source_target_pairs={{0,224},{32,192},{64,160},{96,128},{128,96},{160,64},{192,32},{224... | collective-permute-start | bytes 2064392 | tf_op jit(solution)/shard_map/ppermute | solution.py:22
  73.4 52.1 %copy-start.4 = (bf16[2688,128]{1,0:T(8,128)(2,1)}, bf16[2688,128]{1,0:T(8,128)(2,1)S(1)}, u32[]{:S(2)}) copy-start(bf16[2688,128]{1,0:T(8,128)(2,1)S(1)} %collective-permute-done.2.refs_4_) | copy-start | bytes 2064388
  127.2 50.3 %all-to-all-start.2 = ((bf16[8,288,384]{2,1,0:T(8,128)(2,1)}), bf16[8,288,384]{2,1,0:T(8,128)(2,1)S(1)}, u32[]{:S(2)}, u32[]{:S(2)}) async-start(bf16[8,288,384]{2,1,0:T(8,128)(2,1)} %shard_map.111), calls=%async_computation.2 | async-start | bytes 3538944 | tf_op jit(solution)/shard_map/all_to_all | solution.py:208
  132.5 43.4 %collective-permute-start.7 = (bf16[288,1792]{1,0:T(8,128)(2,1)}, bf16[288,1792]{1,0:T(8,128)(2,1)}, u32[]{:S(2)}, u32[]{:S(2)}) collective-permute-start(bf16[288,1792]{1,0:T(8,128)(2,1)} %pad_maximum_fusion.refs_0_), channel_id=1, source_target_pairs={{0,16},{1,17},{2,18},{3,19},{4,20},{5,21},{6,22},{7,23},{8,24},{9,... | collective-permute-start | bytes 3096584 | tf_op jit(solution)/shard_map/ppermute | solution.py:22
  177.4 25.9 %collective-permute-start.8 = (bf16[288,1792]{1,0:T(8,128)(2,1)S(1)}, bf16[288,1792]{1,0:T(8,128)(2,1)}, u32[]{:S(2)}, u32[]{:S(2)}) collective-permute-start(bf16[288,1792]{1,0:T(8,128)(2,1)S(1)} %broadcast_select_fusion.refs_0_), channel_id=1, source_target_pairs={{0,32},{32,0},{64,96},{96,64},{128,160},{160,128},{192,224},{224,1... | collective-permute-start | bytes 3096584 | tf_op jit(solution)/shard_map/ppermute | solution.py:22
  179.5 35.5 %all-to-all-start.3 = ((bf16[8,288,256]{2,1,0:T(8,128)(2,1)}), bf16[8,288,256]{2,1,0:T(8,128)(2,1)}, u32[]{:S(2)}, u32[]{:S(2)}) async-start(bf16[8,288,256]{2,1,0:T(8,128)(2,1)} %copy-done.10), calls=%async_computation.3 | async-start | bytes 2359296 | tf_op jit(solution)/shard_map/all_to_all | solution.py:216
  185.9 49.8 %collective-permute-start.9 = (bf16[288,1792]{1,0:T(8,128)(2,1)S(1)}, bf16[288,1792]{1,0:T(8,128)(2,1)}, u32[]{:S(2)}, u32[]{:S(2)}) collective-permute-start(bf16[288,1792]{1,0:T(8,128)(2,1)S(1)} %broadcast_select_fusion.refs_0_), channel_id=1, source_target_pairs={{0,64},{32,96},{64,128},{96,160},{128,192},{160,224},{192,0},{224,... | collective-permute-start | bytes 3096584 | tf_op jit(solution)/shard_map/ppermute | solution.py:18
  203.3 32.4 %collective-permute-start.12 = (bf16[288,1792]{1,0:T(8,128)(2,1)}, bf16[288,1792]{1,0:T(8,128)(2,1)}, u32[]{:S(2)}, u32[]{:S(2)}) collective-permute-start(bf16[288,1792]{1,0:T(8,128)(2,1)} %collective-permute-done.8.refs_1_), channel_id=1, source_target_pairs={{0,192},{32,224},{64,0},{96,32},{128,64},{160,96},{192,128},{224,1... | collective-permute-start | bytes 3096584 | tf_op jit(solution)/shard_map/ppermute | solution.py:18
  223.4 27.3 %all-to-all-start.4 = ((bf16[32,64,128]{2,1,0:T(8,128)(2,1)}), bf16[32,64,128]{2,1,0:T(8,128)(2,1)}, u32[]{:S(2)}, u32[]{:S(2)}) async-start(bf16[32,64,128]{2,1,0:T(8,128)(2,1)} %maximum_maximum_fusion.1), calls=%async_computation.4 | async-start | bytes 1048576 | tf_op jit(solution)/shard_map/all_to_all | solution.py:198
  233.5 55.3 %collective-permute-start.10 = (bf16[288,1792]{1,0:T(8,128)(2,1)S(1)}, bf16[288,1792]{1,0:T(8,128)(2,1)S(1)}, u32[]{:S(2)}, u32[]{:S(2)}) collective-permute-start(bf16[288,1792]{1,0:T(8,128)(2,1)S(1)} %broadcast_select_fusion.refs_0_), channel_id=1, source_target_pairs={{0,192},{32,224},{64,0},{96,32},{128,64},{160,96},{192,128},{224,1... | collective-permute-start | bytes 3096584 | tf_op jit(solution)/shard_map/ppermute | solution.py:18
  234.8 54.1 %collective-permute-start.11 = (bf16[288,1792]{1,0:T(8,128)(2,1)}, bf16[288,1792]{1,0:T(8,128)(2,1)S(1)}, u32[]{:S(2)}, u32[]{:S(2)}) collective-permute-start(bf16[288,1792]{1,0:T(8,128)(2,1)} %collective-permute-done.8.refs_1_), channel_id=1, source_target_pairs={{0,64},{32,96},{64,128},{96,160},{128,192},{160,224},{192,0},{224,... | collective-permute-start | bytes 3096584 | tf_op jit(solution)/shard_map/ppermute | solution.py:18
  235.6 53.2 %collective-permute-start.13 = (bf16[288,1792]{1,0:T(8,128)(2,1)}, bf16[288,1792]{1,0:T(8,128)(2,1)}, u32[]{:S(2)}, u32[]{:S(2)}) collective-permute-start(bf16[288,1792]{1,0:T(8,128)(2,1)} %collective-permute-done.9.refs_2_), channel_id=1, source_target_pairs={{0,64},{32,96},{64,128},{96,160},{128,192},{160,224},{192,0},{224,... | collective-permute-start | bytes 3096584 | tf_op jit(solution)/shard_map/ppermute | solution.py:18
  235.7 53.2 %collective-permute-start.14 = (bf16[288,1792]{1,0:T(8,128)(2,1)}, bf16[288,1792]{1,0:T(8,128)(2,1)}, u32[]{:S(2)}, u32[]{:S(2)}) collective-permute-start(bf16[288,1792]{1,0:T(8,128)(2,1)} %collective-permute-done.12.refs_5_), channel_id=1, source_target_pairs={{0,192},{32,224},{64,0},{96,32},{128,64},{160,96},{192,128},{224,1... | collective-permute-start | bytes 3096584 | tf_op jit(solution)/shard_map/ppermute | solution.py:18
  253.7 31.7 %all-to-all-start.5 = ((bf16[8,16,896]{2,1,0:T(8,128)(2,1)}), bf16[8,16,896]{2,1,0:T(8,128)(2,1)}, u32[]{:S(2)}, u32[]{:S(2)}) async-start(bf16[8,16,896]{2,1,0:T(8,128)(2,1)} %bitcast.176), calls=%async_computation.5 | async-start | bytes 458752 | tf_op jit(solution)/shard_map/all_to_all | solution.py:230
  258.7 30.2 %collective-permute-start.15 = (bf16[288,384]{1,0:T(8,128)(2,1)S(1)}, bf16[288,384]{1,0:T(8,128)(2,1)}, u32[]{:S(2)}, u32[]{:S(2)}) collective-permute-start(bf16[288,384]{1,0:T(8,128)(2,1)S(1)} %copy-done.12), channel_id=1, source_target_pairs={{0,16},{1,17},{2,18},{3,19},{4,20},{5,21},{6,22},{7,23},{8,24},{9,... | collective-permute-start | bytes 663560 | tf_op jit(solution)/shard_map/ppermute | solution.py:22
  (25 other events, 250.7 us)

commit v3 on v2

--- a/solution.py
+++ b/solution.py
@@ -1,3 +1,5 @@
+import functools
+
 import jax
 import jax.numpy as jnp
 from jax import lax
@@ -20,6 +22,91 @@
 
 def flip(x, axis, bit, size):
     return lax.ppermute(x, axis, [(i, i ^ bit) for i in range(size)])
+
+
+def after(x, *others):
+    return lax.optimization_barrier((x, *others))[0]
+
+
+def pack_kernel(tok, cot, routes, gates, out):
+    groups, rows, lanes = out.shape
+    n_tok, topk = routes.shape
+    part = (lanes - LANES) // 2
+    lane = lax.broadcasted_iota(jnp.int32, (n_tok, LANES), 1)
+    meta = jnp.zeros((n_tok, LANES), jnp.int32)
+    for k in range(topk):
+        g = gates[:, k : k + 1]
+        for at, v in ((3 * k, routes[:, k : k + 1]), (3 * k + 1, g // 256), (3 * k + 2, g % 256)):
+            meta = jnp.where(lane == at, v, meta)
+    meta = meta.astype(F32).astype(BF)
+    fill = jnp.zeros((rows - n_tok, lanes), BF)
+    for d in range(groups):
+        at = slice(d * part, (d + 1) * part)
+        rows_here = jnp.concatenate([tok[:, at], cot[:, at], meta], axis=1)
+        out[d] = jnp.concatenate([rows_here, fill], axis=0)
+
+
+def block_kernel(ids, wg, wu, wd, *outs):
+    part = outs[0].shape[0] // 3
+    for k, out in enumerate(outs):
+        start = pl.multiple_of(ids[k] * part, part)
+        out[:part, :] = wg[pl.ds(start, part), :]
+        out[part : 2 * part, :] = wu[pl.ds(start, part), :]
+        for q in range(part // LANES):
+            at = pl.ds(pl.multiple_of(start + q * LANES, LANES), LANES)
+            out[2 * part + q * LANES : 2 * part + (q + 1) * LANES, :] = wd[:, at]
+
+
+def route_kernel(n_tok, topk, rows_ref, out_ref, place_ref):
+    groups, stride, lanes = rows_ref.shape
+    experts, chunk, _ = out_ref.shape
+    count = groups * stride
+    cap = place_ref.shape[1] // experts
+    low = cap - 1
+    head = experts * low
+    x = rows_ref[...].reshape(count, lanes)
+    meta = x[:, lanes - LANES :].astype(F32)
+    row = lax.broadcasted_iota(jnp.int32, (count, 1), 0)
+    valid = row % stride < n_tok
+    expert = lax.broadcasted_iota(jnp.int32, (count, experts), 1).astype(F32)
+    named = [jnp.where(valid & (meta[:, 3 * k : 3 * k + 1] == expert), 1.0, 0.0) for k in range(topk)]
+    every = sum(named)
+    above = lax.broadcasted_iota(jnp.int32, (count, count), 0) > lax.broadcasted_iota(
+        jnp.int32, (count, count), 1
+    )
+    earlier = dot(above.astype(F32).astype(BF), every.astype(BF), ((1,), (0,)))
+    tail = chunk - low * (lanes - LANES) // LANES
+    wide = lax.broadcasted_iota(jnp.int32, (count, head + experts * tail), 1)
+    narrow = lax.broadcasted_iota(jnp.int32, (count, experts * cap), 1)
+    pick = place = gate = None
+    for k in range(topk):
+        rank = jnp.sum(earlier * named[k], axis=1, keepdims=True).astype(jnp.int32)
+        name = meta[:, 3 * k : 3 * k + 1].astype(jnp.int32)
+        first = jnp.where(valid & (rank < low), name * low + rank, -1)
+        last = jnp.where(valid & (rank >= low), name, -1)
+        hit = (wide == first) | ((wide >= head) & ((wide - head) // tail == last))
+        hit = jnp.where(hit, 1.0, 0.0).astype(BF)
+        small = jnp.where((narrow == first) | ((narrow >= head) & (narrow - head == last)), 1.0, 0.0)
+        g = dot(hit, x[:, lanes - LANES :], ((0,), (0,)))
+        g = (g[:, 3 * k + 1 : 3 * k + 2] * 256.0 + g[:, 3 * k + 2 : 3 * k + 3]) * (1.0 / 65536.0)
+        pick, place, gate = (hit, small, g) if k == 0 else (pick + hit, place + small, gate + g)
+    place_ref[...] = place.astype(BF)
+    parts = (lanes - LANES) // LANES
+    slots = head + experts * tail
+    spot = lax.broadcasted_iota(jnp.int32, (experts * tail, LANES), 0) % tail
+    ends = jnp.zeros((experts * tail, LANES), F32)
+    heads = []
+    for q in range(parts):
+        rows = dot(pick, x[:, q * LANES : (q + 1) * LANES], ((0,), (0,)))
+        if q >= parts // 2:
+            rows = rows * gate
+        heads.append(rows[:head].reshape(experts, low, LANES))
+        ends = jnp.where(spot == q, rows[head:], ends)
+        if q % 2 == 1:
+            pair = jnp.concatenate(heads, axis=1)
+            out_ref[:, (q - 1) * low : (q + 1) * low, :] = pair.astype(BF)
+            heads = []
+    out_ref[:, parts * low :, :] = ends.reshape(experts, tail, LANES).astype(BF)
 
 
 def to_chunks(x, experts, low):
@@ -147,64 +234,43 @@
     ids = jnp.concatenate([slice_ids(me_d, groups), flipped.astype(jnp.int32)[None]])
     across = lambda x: flip(x, "expert", experts // 2, experts)
 
-    def block(t):
-        cut = lambda w, axis: lax.dynamic_slice_in_dim(w, t * part, part, axis)
-        down = cut(w_down[0], 1).reshape(hidden, parts, LANES).transpose(1, 0, 2)
-        return jnp.concatenate([cut(w_gate[0], 0), cut(w_up[0], 0), down.reshape(part, LANES)], axis=0)
-
-    blocks = [block(me_d)] + [flip(block(me_d ^ k), "dp", k, groups) for k in range(1, groups)]
-    sources = jnp.stack([me_d ^ k for k in range(groups)]).astype(jnp.int32)
-
-    split = lambda x: x.reshape(n_tok, groups, part).transpose(1, 0, 2)
-    flat_gates = gates.reshape(-1)
-    meta = jnp.concatenate([routes.reshape(-1), flat_gates // 256, flat_gates % 256]).astype(F32)
-    meta = jnp.pad(meta, (0, part - meta.shape[0])).astype(BF)
-    meta = jnp.broadcast_to(meta[None, None], (groups, 1, part))
-    stride = 32
-    pad = jnp.zeros((groups, stride - 2 * n_tok - 1, part), BF)
-    packed = jnp.concatenate([split(tokens[0, 0]), split(cotangent[0, 0]), meta, pad], axis=1)
+    slot_count = experts * cap
+    stride = -(-n_tok // 16) * 16
+    lanes = 2 * part + LANES
+
+    packed = call(
+        pack_kernel, (), (tokens[0, 0], cotangent[0, 0], routes[0, 0], gates[0, 0]),
+        jax.ShapeDtypeStruct((groups, stride, lanes), BF), 0,
+    )
     column = lax.all_to_all(packed, "dp", split_axis=0, concat_axis=0, tiled=True)
-    picks = n_tok * topk
-    told = column[:, 2 * n_tok, : 3 * picks].astype(F32).reshape(groups, 3, picks)
-    route = told[:, 0].reshape(-1).astype(jnp.int32)
-    gate_of = (told[:, 1] * 256.0 + told[:, 2]).reshape(-1) / 65536.0
-    count = groups * picks
-
-    onehot = (route[:, None] == expert_iota[None, :]).astype(BF)
-    order = jnp.arange(count, dtype=jnp.int32)
-    before = (order[:, None] > order[None, :]).astype(BF)
-    earlier = dot(before, onehot, ((1,), (0,)))
-    rank = jnp.sum(earlier * onehot.astype(F32), axis=1).astype(jnp.int32)
-    slot = jnp.where(rank < low, route * low + rank, experts * low + route)
-    slot_count = experts * cap
-    slots = jnp.arange(slot_count, dtype=jnp.int32)
-    gate_slot = jnp.sum(jnp.where(slots[:, None] == slot[None, :], gate_of[None, :], 0.0), axis=1)
-
-    def places(step, first):
-        by_tok = slot.reshape(groups, n_tok, topk)
-        spread = jnp.pad(by_tok, ((0, 0), (first, step - first - n_tok), (0, 0)), constant_values=-1)
-        spread = spread.reshape(groups * step, topk)
-        hit = slots[:, None] == spread[None, :, 0]
-        for k in range(1, topk):
-            hit = hit | (slots[:, None] == spread[None, :, k])
-        return hit.astype(BF)
-
-    rows = column.reshape(groups * stride, part)
-    send_in = dot(places(stride, 0), rows, ((1,), (0,))).astype(BF)
-    send_cot = (dot(places(stride, n_tok), rows, ((1,), (0,))) * gate_slot[:, None]).astype(BF)
+
+    turns = (2, 6, 1, 3, 7, 4, 5)
+    sources = jnp.stack([me_d] + [me_d ^ k for k in turns]).astype(jnp.int32)
+    cut = jax.ShapeDtypeStruct((3 * part, hidden), BF)
+    sends = call(block_kernel, (sources,), (w_gate[0], w_up[0], w_down[0]), (cut,) * groups, 0)
+    blocks = [sends[0]] + [flip(b, "dp", k, groups) for k, b in zip(turns, sends[1:])]
+
+    chunk = 2 * parts * low + 16 * (-(-2 * parts // 16))
+    to_home, places = call(
+        functools.partial(route_kernel, n_tok, topk), (), (column,),
+        (
+            jax.ShapeDtypeStruct((experts, chunk, LANES), BF),
+            jax.ShapeDtypeStruct((groups * stride, slot_count), BF),
+        ), 0,
+    )
 
     def exchange(x):
-        x = to_chunks(x, experts, low)
         return lax.all_to_all(x, "expert", split_axis=0, concat_axis=0, tiled=True)
 
-    both = from_chunks(
-        exchange(jnp.concatenate([send_in, send_cot], axis=1)), experts, low, 2 * parts
-    )
+    arrived = exchange(after(to_home, *blocks[1:4]))
+    both = from_chunks(after(arrived, *blocks[4:6]), experts, low, 2 * parts)
     unit = 2 * slot_count * width * hidden
     sums = call(
         partial_kernel, (sources,), (both, *blocks),
         jax.ShapeDtypeStruct((groups, slot_count, 3 * hidden), BF), 3 * unit,
     )
+    slot_rows = jnp.where(flipped, across(both), both)
+    sums = after(sums, slot_rows)
     sums = lax.all_to_all(sums, "dp", split_axis=0, concat_axis=0, tiled=True)
     trio, pairs = call(
         point_kernel, (), (sums,),
@@ -214,20 +280,20 @@
         ), unit // 100,
     )
     pairs = lax.all_to_all(pairs, "dp", split_axis=0, concat_axis=0, tiled=True)
+    ring = gather_slices(slot_rows, me_d, groups)
+    pairs = after(pairs, ring[2], ring[3])
     share = call(
         share_kernel, (sources,), (pairs, *blocks),
         jax.ShapeDtypeStruct((slot_count, part), BF), 2 * unit,
         [pltpu.VMEM((slot_count, part), F32)],
     )
-
-    slot_rows = gather_slices(jnp.where(flipped, across(both), both), me_d, groups)
     shapes = tuple(jax.ShapeDtypeStruct(w.shape[1:], BF) for w in (w_gate, w_up, w_down))
-    grads = call(grad_kernel, (ids,), (*slot_rows, trio, across(trio)), shapes, 3 * unit)
-
-    back = from_chunks(exchange(share), experts, low, parts)
-    tok_rows = 16
-    total = dot(places(tok_rows, 0), back, ((0,), (0,))).astype(BF)
-    mine = lax.all_to_all(total.reshape(groups, tok_rows, part), "dp", split_axis=0, concat_axis=0, tiled=True)
+    grads = call(grad_kernel, (ids,), (*ring, trio, across(trio)), shapes, 3 * unit)
+
+    back = exchange(to_chunks(share, experts, low))
+    back = from_chunks(after(back, ring[4], ring[5]), experts, low, parts)
+    total = dot(places, back, ((1,), (0,))).astype(BF)
+    mine = lax.all_to_all(total.reshape(groups, stride, part), "dp", split_axis=0, concat_axis=0, tiled=True)
     grad_input = mine[:, :n_tok].transpose(1, 0, 2).reshape(1, 1, n_tok, width)
     return grad_input, grads[0][None], grads[1][None], grads[2][None]
 

time: 300 us -> 271 us (0.903)
  waiting for transfers between devices: 158 us -> 137 us
  blocking collectives: 0 us -> 20.2 us
  local copies, waits for them, and re-layouts: 32.1 us -> 16.8 us
  other arithmetic: 16.8 us -> 4.18 us
  Pallas kernels: 19.3 us -> 27.2 us
  starting transfers between devices: 67.8 us -> 61.4 us
    all_to_all x2 -> x1, waiting for transfers between devices: 23.1 us -> 0.01 us  [shards(): lax.all_to_all(total.reshape(groups, stride, part), 'dp', split_axis=0, c...]
    all_to_all x0 -> x1, blocking collectives: none -> 20.2 us  [shards(): lax.all_to_all(packed, 'dp', split_axis=0, concat_axis=0, tiled=True)]
    all_to_all x1, waiting for transfers between devices: 0.01 us -> 19.5 us  [shards(): sums = lax.all_to_all(sums, 'dp', split_axis=0, concat_axis=0, tiled=True)]
    ppermute x10, waiting for transfers between devices: 103 us -> 86 us  [flip(): return lax.ppermute(x, axis, [(i, i ^ bit) for i in range(size)])]
    concatenate x10 -> x0, other arithmetic: 10.7 us -> none  [the longest x8 10.6 us: block(): jnp.concatenate([cut(w_gate[0], 0), cut(w_up[0], 0), down.reshape(part, L...]
    ppermute x6, waiting for transfers between devices: 0.02 us -> 10.5 us  [hop(): return lax.ppermute(x, axis, [(i, (i + step) % size) for i in range(size)])]
    all_to_all x2, waiting for transfers between devices: 21.7 us -> 13.6 us  [exchange(): return lax.all_to_all(x, 'expert', split_axis=0, concat_axis=0, tiled=True)]
    pallas_call x4 -> x7, Pallas kernels: 19.3 us -> 27.2 us  [call(): pl.pallas_call(kernel, out_shape=outs, in_specs=[pl.BlockSpec(memory_spac...]
  transfers between devices with their start and end apart: 22 -> 21, of which waited for: 8 -> 10; matrix products, arithmetic and copies ran while one was open for 13% -> 2% of each run, Pallas kernels for 1% -> 8%
where the time goes in v3:
time: 271 us; the launch traced here: 270 us
  waiting for transfers between devices  137 us (51%)
  starting transfers between devices  61.4 us (23%)
  Pallas kernels  27.2 us (10%)
  blocking collectives  20.2 us (7%)
  local copies, waits for them, and re-layouts  16.8 us (6%)
  other arithmetic  4.18 us (2%)
    ppermute x10, waiting for transfers between devices, flip(): return lax.ppermute(x, axis, [(i, i ^ bit) for i in range(size)])  86 us
    pallas_call x7, Pallas kernels, call(): pl.pallas_call(kernel, out_shape=outs, in_specs=[pl.BlockSpec(memory_spac...  27.2 us
    all_to_all x2, starting transfers between devices, exchange(): return lax.all_to_all(x, 'expert', split_axis=0, concat_axis=0, tiled=True)  23.4 us
    all_to_all x1, blocking collectives, shards(): lax.all_to_all(packed, 'dp', split_axis=0, concat_axis=0, tiled=True)  20.2 us
    all_to_all x1, waiting for transfers between devices, shards(): sums = lax.all_to_all(sums, 'dp', split_axis=0, concat_axis=0, tiled=True)  19.5 us
    all_to_all x2, waiting for transfers between devices, exchange(): return lax.all_to_all(x, 'expert', split_axis=0, concat_axis=0, tiled=True)  13.6 us
    ppermute x10, starting transfers between devices, flip(): return lax.ppermute(x, axis, [(i, i ^ bit) for i in range(size)])  13.1 us
    unnamed x58, local copies, waits for them, and re-layouts  11.3 us
  transfers between devices with their start and end apart: 21, of which 10 were waited for; matrix products, arithmetic and copies ran while one was open for 2% of the time, Pallas kernels for 8%

profile of v3, /device:TPU:6, one launch (start us, length us, event | category | flops | bytes accessed | tf_op | source)
XLA Modules:
  0.0 269.7 jit_solution(13428666480263861531)
XLA Ops:
  0.7 4.9 %shard_map.113 = (bf16[2688,128]{1,0:T(8,128)(2,1)S(1)}, bf16[2688,128]{1,0:T(8,128)(2,1)}, bf16[2688,128]{1,0:T(8,128)(2,1)}, bf16[2688,128]{1,0:T(8,128)(2,1)}...) custom-call(s32[8]{0:T(128)S(1)} %stack.55.ids, ...), custom_call_target="tpu_custom_call" | custom-call | bytes 11010048 | tf_op jit(solution)/shard_map/pallas_call | solution.py:207
  8.0 2.2 collective-permute-start.1
  12.3 20.2 %all_to_all.30.rows_ref = bf16[8,16,1920]{2,1,0:T(8,128)(2,1)S(1)} all-to-all(bf16[8,16,1920]{2,1,0:T(8,128)(2,1)S(1)} %shard_map.111), channel_id=1, replica_groups=mesh['dp'=8,'expert'=32] {'dp'}, dimensions={0} | all-to-all | bytes 983040 | tf_op jit(solution)/shard_map/all_to_all | solution.py:245
  35.6 11.6 %all-to-all-start.1 = ((bf16[32,128,128]{2,1,0:T(8,128)(2,1)}), bf16[32,128,128]{2,1,0:T(8,128)(2,1)}, u32[]{:S(2)}, u32[]{:S(2)}) async-start(bf16[32,128,128]{2,1,0:T(8,128)(2,1)} %copy-done.12), calls=%async_computation.1 | async-start | bytes 2097152 | tf_op jit(solution)/shard_map/all_to_all | solution.py:263
  48.8 2.4 collective-permute-start.4
  51.2 25.3 %collective-permute-done.3.refs_5_ = bf16[2688,128]{1,0:T(8,128)(2,1)S(1)} collective-permute-done((bf16[2688,128]{1,0:T(8,128)(2,1)}, bf16[2688,128]{1,0:T(8,128)(2,1)S(1)}, u32[]{:S(2)}, u32[]{:S(2)}) %collective-permute-start.3) | collective-permute-done | bytes 688160 | tf_op jit(solution)/shard_map/ppermute | solution.py:24
  76.5 15.0 %collective-permute-done.4.refs_6_ = bf16[2688,128]{1,0:T(8,128)(2,1)S(1)} collective-permute-done((bf16[2688,128]{1,0:T(8,128)(2,1)}, bf16[2688,128]{1,0:T(8,128)(2,1)S(1)}, u32[]{:S(2)}, u32[]{:S(2)}) %collective-permute-start.4) | collective-permute-done | bytes 688160 | tf_op jit(solution)/shard_map/ppermute | solution.py:24
  98.6 2.2 collective-permute-start.6
  102.0 14.2 %collective-permute-done.5.refs_7_ = bf16[2688,128]{1,0:T(8,128)(2,1)} collective-permute-done((bf16[2688,128]{1,0:T(8,128)(2,1)}, bf16[2688,128]{1,0:T(8,128)(2,1)}, u32[]{:S(2)}, u32[]{:S(2)}) %collective-permute-start.5) | collective-permute-done | bytes 688160 | tf_op jit(solution)/shard_map/ppermute | solution.py:24
  116.2 19.8 %collective-permute-done.6.refs_8_ = bf16[2688,128]{1,0:T(8,128)(2,1)} collective-permute-done((bf16[2688,128]{1,0:T(8,128)(2,1)}, bf16[2688,128]{1,0:T(8,128)(2,1)}, u32[]{:S(2)}, u32[]{:S(2)}) %collective-permute-start.6) | collective-permute-done | bytes 688160 | tf_op jit(solution)/shard_map/ppermute | solution.py:24
  137.1 6.3 %shard_map.114 = bf16[8,288,384]{2,1,0:T(8,128)(2,1)} custom-call(s32[8]{0:T(128)S(1)} %stack.55.ids, bf16[288,1792]{1,0:T(8,128)(2,1)} %pad_maximum_fusion.refs_0_, bf16[2688,128]{1,0:T(8,128)(2,1)S(1)} %get-tuple-element.33.refs_1_, bf16[2688,128]{1,0:T(8,128)(2,1)S(1)} %collective-permute-done.refs_2_, ...), custom_call_target="tpu_custom_call" | custom-call | flops 1585446912 | bytes 8306688 | tf_op jit(solution)/shard_map/pallas_call | solution.py:207
  144.9 5.4 %all-to-all-start.2 = ((bf16[8,288,384]{2,1,0:T(8,128)(2,1)}), bf16[8,288,384]{2,1,0:T(8,128)(2,1)S(1)}, u32[]{:S(2)}, u32[]{:S(2)}) async-start(bf16[8,288,384]{2,1,0:T(8,128)(2,1)} %shard_map.114), calls=%async_computation.2 | async-start | bytes 3538944 | tf_op jit(solution)/shard_map/all_to_all | solution.py:274
  153.5 19.5 %all-to-all-done.2.part_ref = bf16[8,288,384]{2,1,0:T(8,128)(2,1)S(1)} async-done(((bf16[8,288,384]{2,1,0:T(8,128)(2,1)}), bf16[8,288,384]{2,1,0:T(8,128)(2,1)S(1)}, u32[]{:S(2)}, u32[]{:S(2)}) %all-to-all-start.2) | async-done | bytes 1769504 | tf_op jit(solution)/shard_map/all_to_all | solution.py:274
  175.0 6.4 %all-to-all-start.3 = ((bf16[8,288,256]{2,1,0:T(8,128)(2,1)}), bf16[8,288,256]{2,1,0:T(8,128)(2,1)}, u32[]{:S(2)}, u32[]{:S(2)}) async-start(bf16[8,288,256]{2,1,0:T(8,128)(2,1)} %copy-done.11), calls=%async_computation.3 | async-start | bytes 2359296 | tf_op jit(solution)/shard_map/all_to_all | solution.py:282
  181.5 11.7 %collective-permute-done.10.refs_1_ = bf16[288,1792]{1,0:T(8,128)(2,1)} collective-permute-done((bf16[288,1792]{1,0:T(8,128)(2,1)S(1)}, bf16[288,1792]{1,0:T(8,128)(2,1)}, u32[]{:S(2)}, u32[]{:S(2)}) %collective-permute-start.10) | collective-permute-done | bytes 1032224 | tf_op jit(solution)/shard_map/ppermute | solution.py:24
  196.6 3.6 %collective-permute-done.8.refs_2_ = bf16[288,1792]{1,0:T(8,128)(2,1)} collective-permute-done((bf16[288,1792]{1,0:T(8,128)(2,1)S(1)}, bf16[288,1792]{1,0:T(8,128)(2,1)}, u32[]{:S(2)}, u32[]{:S(2)}) %collective-permute-start.8) | collective-permute-done | bytes 1032224 | tf_op jit(solution)/shard_map/ppermute | solution.py:20
  200.2 7.7 %all-to-all-done.3.refs_0_ = bf16[8,288,256]{2,1,0:T(8,128)(2,1)} async-done(((bf16[8,288,256]{2,1,0:T(8,128)(2,1)}), bf16[8,288,256]{2,1,0:T(8,128)(2,1)}, u32[]{:S(2)}, u32[]{:S(2)}) %all-to-all-start.3) | async-done | bytes 1179680 | tf_op jit(solution)/shard_map/all_to_all | solution.py:282
  211.2 4.7 %shard_map.116 = bf16[288,896]{1,0:T(8,128)(2,1)} custom-call(s32[8]{0:T(128)S(1)} %stack.55.ids, bf16[8,288,256]{2,1,0:T(8,128)(2,1)} %all-to-all-done.3.refs_0_, bf16[2688,128]{1,0:T(8,128)(2,1)S(1)} %get-tuple-element.33.refs_1_, bf16[2688,128]{1,0:T(8,128)(2,1)S(1)} %copy-done.1, bf16[2688,128]{1,0:T(8,128)(2,1)S(1)} %copy-done.3, ...), custom_call_target="tpu_custom_call" | custom-call | flops 1056964608 | bytes 7200768 | tf_op jit(solution)/shard_map/pallas_call | solution.py:207
  219.0 11.7 %all-to-all-start.4 = ((bf16[32,64,128]{2,1,0:T(8,128)(2,1)}), bf16[32,64,128]{2,1,0:T(8,128)(2,1)S(1)}, u32[]{:S(2)}, u32[]{:S(2)}) async-start(bf16[32,64,128]{2,1,0:T(8,128)(2,1)} %maximum_maximum_fusion), calls=%async_computation.4 | async-start | bytes 1048576 | tf_op jit(solution)/shard_map/all_to_all | solution.py:263
  230.8 3.2 %collective-permute-start.14 = (bf16[288,1792]{1,0:T(8,128)(2,1)}, bf16[288,1792]{1,0:T(8,128)(2,1)}, u32[]{:S(2)}, u32[]{:S(2)}) collective-permute-start(bf16[288,1792]{1,0:T(8,128)(2,1)} %collective-permute-done.12.refs_5_), channel_id=1, source_target_pairs={{0,192},{32,224},{64,0},{96,32},{128,64},{160,96},{192,128},{224,1... | collective-permute-start | bytes 3096584 | tf_op jit(solution)/shard_map/ppermute | solution.py:20
  234.3 13.6 %all-to-all-done.4 = bf16[32,64,128]{2,1,0:T(8,128)(2,1)S(1)} async-done(((bf16[32,64,128]{2,1,0:T(8,128)(2,1)}), bf16[32,64,128]{2,1,0:T(8,128)(2,1)S(1)}, u32[]{:S(2)}, u32[]{:S(2)}) %all-to-all-start.4) | async-done | bytes 524320 | tf_op jit(solution)/shard_map/all_to_all | solution.py:263
  249.0 3.4 %all-to-all-start.5 = ((bf16[8,16,896]{2,1,0:T(8,128)(2,1)}), bf16[8,16,896]{2,1,0:T(8,128)(2,1)S(1)}, u32[]{:S(2)}, u32[]{:S(2)}) async-start(bf16[8,16,896]{2,1,0:T(8,128)(2,1)} %bitcast.24), calls=%async_computation.5 | async-start | bytes 458752 | tf_op jit(solution)/shard_map/all_to_all | solution.py:296
  252.5 6.8 %collective-permute-done.13.refs_6_ = bf16[288,1792]{1,0:T(8,128)(2,1)} collective-permute-done((bf16[288,1792]{1,0:T(8,128)(2,1)}, bf16[288,1792]{1,0:T(8,128)(2,1)}, u32[]{:S(2)}, u32[]{:S(2)}) %collective-permute-start.13) | collective-permute-done | bytes 1032224 | tf_op jit(solution)/shard_map/ppermute | solution.py:20
  259.3 9.5 %shard_map.117 = (bf16[7168,128]{1,0:T(8,128)(2,1)}, bf16[7168,128]{1,0:T(8,128)(2,1)}, bf16[128,7168]{1,0:T(8,128)(2,1)}) custom-call(s32[9]{0:T(128)S(1)} %concatenate.15.ids, bf16[288,1792]{1,0:T(8,128)(2,1)S(1)} %broadcast_select_fusion.refs_0_, bf16[288,1792]{1,0:T(8,128)(2,1)} %collective-permute-done.10.refs_1_, ...), custom_call_target="tpu_custom_call" | custom-call | flops 1585446912 | bytes 14204928 | tf_op jit(solution)/shard_map/pallas_call | solution.py:207
  (104 shorter events, 36.8 us)
Async XLA Ops:
  6.5 28.1 %collective-permute-start = (bf16[2688,128]{1,0:T(8,128)(2,1)}, bf16[2688,128]{1,0:T(8,128)(2,1)S(1)}, u32[]{:S(2)}, u32[]{:S(2)}) collective-permute-start(bf16[2688,128]{1,0:T(8,128)(2,1)} %get-tuple-element.26), channel_id=1, source_target_pairs={{0,64},{32,96},{64,0},{96,32},{128,192},{160,224},{192,128},{224,1... | collective-permute-start | bytes 2064392 | tf_op jit(solution)/shard_map/ppermute | solution.py:24
  8.0 26.6 %collective-permute-start.1 = (bf16[2688,128]{1,0:T(8,128)(2,1)}, bf16[2688,128]{1,0:T(8,128)(2,1)S(1)}, u32[]{:S(2)}, u32[]{:S(2)}) collective-permute-start(bf16[2688,128]{1,0:T(8,128)(2,1)} %get-tuple-element.27), channel_id=1, source_target_pairs={{0,192},{32,224},{64,128},{96,160},{128,64},{160,96},{192,0},{224,... | collective-permute-start | bytes 2064392 | tf_op jit(solution)/shard_map/ppermute | solution.py:24
  10.2 24.4 %collective-permute-start.2 = (bf16[2688,128]{1,0:T(8,128)(2,1)}, bf16[2688,128]{1,0:T(8,128)(2,1)S(1)}, u32[]{:S(2)}, u32[]{:S(2)}) collective-permute-start(bf16[2688,128]{1,0:T(8,128)(2,1)} %get-tuple-element.28), channel_id=1, source_target_pairs={{0,32},{32,0},{64,96},{96,64},{128,160},{160,128},{192,224},{224,1... | collective-permute-start | bytes 2064392 | tf_op jit(solution)/shard_map/ppermute | solution.py:24
  34.6 101.3 %copy-start = (bf16[2688,128]{1,0:T(8,128)(2,1)}, bf16[2688,128]{1,0:T(8,128)(2,1)S(1)}, u32[]{:S(2)}) copy-start(bf16[2688,128]{1,0:T(8,128)(2,1)S(1)} %collective-permute-done.refs_2_) | copy-start | bytes 2064388
  34.6 101.3 %copy-start.2 = (bf16[2688,128]{1,0:T(8,128)(2,1)}, bf16[2688,128]{1,0:T(8,128)(2,1)S(1)}, u32[]{:S(2)}) copy-start(bf16[2688,128]{1,0:T(8,128)(2,1)S(1)} %collective-permute-done.1.refs_3_) | copy-start | bytes 2064388
  35.6 100.4 %copy-start.4 = (bf16[2688,128]{1,0:T(8,128)(2,1)}, bf16[2688,128]{1,0:T(8,128)(2,1)S(1)}, u32[]{:S(2)}) copy-start(bf16[2688,128]{1,0:T(8,128)(2,1)S(1)} %collective-permute-done.2.refs_4_) | copy-start | bytes 2064388
  35.6 56.8 %all-to-all-start.1 = ((bf16[32,128,128]{2,1,0:T(8,128)(2,1)}), bf16[32,128,128]{2,1,0:T(8,128)(2,1)}, u32[]{:S(2)}, u32[]{:S(2)}) async-start(bf16[32,128,128]{2,1,0:T(8,128)(2,1)} %copy-done.12), calls=%async_computation.1 | async-start | bytes 2097152 | tf_op jit(solution)/shard_map/all_to_all | solution.py:263
  47.2 29.3 %collective-permute-start.3 = (bf16[2688,128]{1,0:T(8,128)(2,1)}, bf16[2688,128]{1,0:T(8,128)(2,1)S(1)}, u32[]{:S(2)}, u32[]{:S(2)}) collective-permute-start(bf16[2688,128]{1,0:T(8,128)(2,1)} %copy-done.18), channel_id=1, source_target_pairs={{0,96},{32,64},{64,32},{96,0},{128,224},{160,192},{192,160},{224,1... | collective-permute-start | bytes 2064392 | tf_op jit(solution)/shard_map/ppermute | solution.py:24
  48.8 42.7 %collective-permute-start.4 = (bf16[2688,128]{1,0:T(8,128)(2,1)}, bf16[2688,128]{1,0:T(8,128)(2,1)S(1)}, u32[]{:S(2)}, u32[]{:S(2)}) collective-permute-start(bf16[2688,128]{1,0:T(8,128)(2,1)} %copy-done.17), channel_id=1, source_target_pairs={{0,224},{32,192},{64,160},{96,128},{128,96},{160,64},{192,32},{224... | collective-permute-start | bytes 2064392 | tf_op jit(solution)/shard_map/ppermute | solution.py:24
  96.5 46.8 %collective-permute-start.7 = (bf16[288,1792]{1,0:T(8,128)(2,1)}, bf16[288,1792]{1,0:T(8,128)(2,1)}, u32[]{:S(2)}, u32[]{:S(2)}) collective-permute-start(bf16[288,1792]{1,0:T(8,128)(2,1)} %pad_maximum_fusion.refs_0_), channel_id=1, source_target_pairs={{0,16},{1,17},{2,18},{3,19},{4,20},{5,21},{6,22},{7,23},{8,24},{9,... | collective-permute-start | bytes 3096584 | tf_op jit(solution)/shard_map/ppermute | solution.py:24
  97.5 18.7 %collective-permute-start.5 = (bf16[2688,128]{1,0:T(8,128)(2,1)}, bf16[2688,128]{1,0:T(8,128)(2,1)}, u32[]{:S(2)}, u32[]{:S(2)}) collective-permute-start(bf16[2688,128]{1,0:T(8,128)(2,1)} %get-tuple-element.34), channel_id=1, source_target_pairs={{0,128},{32,160},{64,192},{96,224},{128,0},{160,32},{192,64},{224,... | collective-permute-start | bytes 2064392 | tf_op jit(solution)/shard_map/ppermute | solution.py:24
  98.6 37.4 %collective-permute-start.6 = (bf16[2688,128]{1,0:T(8,128)(2,1)}, bf16[2688,128]{1,0:T(8,128)(2,1)}, u32[]{:S(2)}, u32[]{:S(2)}) collective-permute-start(bf16[2688,128]{1,0:T(8,128)(2,1)} %get-tuple-element.35), channel_id=1, source_target_pairs={{0,160},{32,128},{64,224},{96,192},{128,32},{160,0},{192,96},{224,... | collective-permute-start | bytes 2064392 | tf_op jit(solution)/shard_map/ppermute | solution.py:24
  144.9 28.1 %all-to-all-start.2 = ((bf16[8,288,384]{2,1,0:T(8,128)(2,1)}), bf16[8,288,384]{2,1,0:T(8,128)(2,1)S(1)}, u32[]{:S(2)}, u32[]{:S(2)}) async-start(bf16[8,288,384]{2,1,0:T(8,128)(2,1)} %shard_map.114), calls=%async_computation.2 | async-start | bytes 3538944 | tf_op jit(solution)/shard_map/all_to_all | solution.py:274
  150.3 49.9 %collective-permute-start.8 = (bf16[288,1792]{1,0:T(8,128)(2,1)S(1)}, bf16[288,1792]{1,0:T(8,128)(2,1)}, u32[]{:S(2)}, u32[]{:S(2)}) collective-permute-start(bf16[288,1792]{1,0:T(8,128)(2,1)S(1)} %broadcast_select_fusion.refs_0_), channel_id=1, source_target_pairs={{0,64},{32,96},{64,128},{96,160},{128,192},{160,224},{192,0},{224,... | collective-permute-start | bytes 3096584 | tf_op jit(solution)/shard_map/ppermute | solution.py:20
  151.7 48.5 %collective-permute-start.9 = (bf16[288,1792]{1,0:T(8,128)(2,1)S(1)}, bf16[288,1792]{1,0:T(8,128)(2,1)}, u32[]{:S(2)}, u32[]{:S(2)}) collective-permute-start(bf16[288,1792]{1,0:T(8,128)(2,1)S(1)} %broadcast_select_fusion.refs_0_), channel_id=1, source_target_pairs={{0,192},{32,224},{64,0},{96,32},{128,64},{160,96},{192,128},{224,1... | collective-permute-start | bytes 3096584 | tf_op jit(solution)/shard_map/ppermute | solution.py:20
  153.5 39.8 %collective-permute-start.10 = (bf16[288,1792]{1,0:T(8,128)(2,1)S(1)}, bf16[288,1792]{1,0:T(8,128)(2,1)}, u32[]{:S(2)}, u32[]{:S(2)}) collective-permute-start(bf16[288,1792]{1,0:T(8,128)(2,1)S(1)} %broadcast_select_fusion.refs_0_), channel_id=1, source_target_pairs={{0,32},{32,0},{64,96},{96,64},{128,160},{160,128},{192,224},{224,1... | collective-permute-start | bytes 3096584 | tf_op jit(solution)/shard_map/ppermute | solution.py:24
  175.0 32.8 %all-to-all-start.3 = ((bf16[8,288,256]{2,1,0:T(8,128)(2,1)}), bf16[8,288,256]{2,1,0:T(8,128)(2,1)}, u32[]{:S(2)}, u32[]{:S(2)}) async-start(bf16[8,288,256]{2,1,0:T(8,128)(2,1)} %copy-done.11), calls=%async_computation.3 | async-start | bytes 2359296 | tf_op jit(solution)/shard_map/all_to_all | solution.py:282
  193.3 41.0 %collective-permute-start.11 = (bf16[288,1792]{1,0:T(8,128)(2,1)}, bf16[288,1792]{1,0:T(8,128)(2,1)}, u32[]{:S(2)}, u32[]{:S(2)}) collective-permute-start(bf16[288,1792]{1,0:T(8,128)(2,1)} %collective-permute-done.10.refs_1_), channel_id=1, source_target_pairs={{0,64},{32,96},{64,128},{96,160},{128,192},{160,224},{192,0},{224,... | collective-permute-start | bytes 3096584 | tf_op jit(solution)/shard_map/ppermute | solution.py:20
  195.3 35.5 %collective-permute-start.12 = (bf16[288,1792]{1,0:T(8,128)(2,1)}, bf16[288,1792]{1,0:T(8,128)(2,1)}, u32[]{:S(2)}, u32[]{:S(2)}) collective-permute-start(bf16[288,1792]{1,0:T(8,128)(2,1)} %collective-permute-done.10.refs_1_), channel_id=1, source_target_pairs={{0,192},{32,224},{64,0},{96,32},{128,64},{160,96},{192,128},{224,1... | collective-permute-start | bytes 3096584 | tf_op jit(solution)/shard_map/ppermute | solution.py:20
  219.0 28.9 %all-to-all-start.4 = ((bf16[32,64,128]{2,1,0:T(8,128)(2,1)}), bf16[32,64,128]{2,1,0:T(8,128)(2,1)S(1)}, u32[]{:S(2)}, u32[]{:S(2)}) async-start(bf16[32,64,128]{2,1,0:T(8,128)(2,1)} %maximum_maximum_fusion), calls=%async_computation.4 | async-start | bytes 1048576 | tf_op jit(solution)/shard_map/all_to_all | solution.py:263
  230.7 28.6 %collective-permute-start.13 = (bf16[288,1792]{1,0:T(8,128)(2,1)}, bf16[288,1792]{1,0:T(8,128)(2,1)}, u32[]{:S(2)}, u32[]{:S(2)}) collective-permute-start(bf16[288,1792]{1,0:T(8,128)(2,1)} %collective-permute-done.8.refs_2_), channel_id=1, source_target_pairs={{0,64},{32,96},{64,128},{96,160},{128,192},{160,224},{192,0},{224,... | collective-permute-start | bytes 3096584 | tf_op jit(solution)/shard_map/ppermute | solution.py:20
  230.8 28.5 %collective-permute-start.14 = (bf16[288,1792]{1,0:T(8,128)(2,1)}, bf16[288,1792]{1,0:T(8,128)(2,1)}, u32[]{:S(2)}, u32[]{:S(2)}) collective-permute-start(bf16[288,1792]{1,0:T(8,128)(2,1)} %collective-permute-done.12.refs_5_), channel_id=1, source_target_pairs={{0,192},{32,224},{64,0},{96,32},{128,64},{160,96},{192,128},{224,1... | collective-permute-start | bytes 3096584 | tf_op jit(solution)/shard_map/ppermute | solution.py:20
  234.1 18.5 %collective-permute-start.15 = (bf16[288,384]{1,0:T(8,128)(2,1)S(1)}, bf16[288,384]{1,0:T(8,128)(2,1)S(1)}, u32[]{:S(2)}, u32[]{:S(2)}) collective-permute-start(bf16[288,384]{1,0:T(8,128)(2,1)S(1)} %copy-done.16), channel_id=1, source_target_pairs={{0,16},{1,17},{2,18},{3,19},{4,20},{5,21},{6,22},{7,23},{8,24},{9,... | collective-permute-start | bytes 663560 | tf_op jit(solution)/shard_map/ppermute | solution.py:24
  249.0 19.8 %all-to-all-start.5 = ((bf16[8,16,896]{2,1,0:T(8,128)(2,1)}), bf16[8,16,896]{2,1,0:T(8,128)(2,1)S(1)}, u32[]{:S(2)}, u32[]{:S(2)}) async-start(bf16[8,16,896]{2,1,0:T(8,128)(2,1)} %bitcast.24), calls=%async_computation.5 | async-start | bytes 458752 | tf_op jit(solution)/shard_map/all_to_all | solution.py:296
  (25 other events, 242.3 us)

commit v4 on v3

--- a/solution.py
+++ b/solution.py
@@ -47,14 +47,15 @@
 
 
 def block_kernel(ids, wg, wu, wd, *outs):
-    part = outs[0].shape[0] // 3
-    for k, out in enumerate(outs):
-        start = pl.multiple_of(ids[k] * part, part)
-        out[:part, :] = wg[pl.ds(start, part), :]
-        out[part : 2 * part, :] = wu[pl.ds(start, part), :]
-        for q in range(part // LANES):
+    count = len(outs) // 2
+    span = outs[0].shape[0] // 2
+    for k in range(count):
+        start = pl.multiple_of(ids[k] * span, span)
+        outs[k][:span, :] = wg[pl.ds(start, span), :]
+        outs[k][span:, :] = wu[pl.ds(start, span), :]
+        for q in range(span // LANES):
             at = pl.ds(pl.multiple_of(start + q * LANES, LANES), LANES)
-            out[2 * part + q * LANES : 2 * part + (q + 1) * LANES, :] = wd[:, at]
+            outs[count + k][q * LANES : (q + 1) * LANES, :] = wd[:, at]
 
 
 def route_kernel(n_tok, topk, rows_ref, out_ref, place_ref):
@@ -125,8 +126,7 @@
     return jnp.concatenate([head, last], axis=0)
 
 
-def gather_slices(x, me, size):
-    mate = flip(x, "dp", 1, size)
+def gather_slices(x, mate, size):
     own_up, own_down = hop(x, "dp", 2, size), hop(x, "dp", -2, size)
     mate_up, mate_down = hop(mate, "dp", 2, size), hop(mate, "dp", -2, size)
     own_far, mate_far = hop(own_up, "dp", 2, size), hop(mate_down, "dp", -2, size)
@@ -142,24 +142,29 @@
     ).astype(jnp.int32)
 
 
-def partial_kernel(ids, *refs):
-    rows_ref, blocks, out_ref = refs[0], refs[1:-1], refs[-1]
-    part = rows_ref.shape[1] // 2
-    ins, cots = rows_ref[:, :part], rows_ref[:, part:]
-    for k, w in enumerate(blocks):
-        gate = dot(ins, w[:part, :], ((1,), (0,)))
-        up = dot(ins, w[part : 2 * part, :], ((1,), (0,)))
-        down = 0.0
-        for q in range(part // LANES):
-            tile = w[2 * part + q * LANES : 2 * part + (q + 1) * LANES, :]
-            down += dot(cots[:, q * LANES : (q + 1) * LANES], tile, ((1,), (1,)))
-        out_ref[ids[k]] = jnp.concatenate([gate, up, down], axis=1).astype(BF)
-
-
-def point_kernel(part_ref, trio_ref, spread_ref):
-    total = part_ref[0].astype(F32)
-    for k in range(1, part_ref.shape[0]):
-        total += part_ref[k].astype(F32)
+def partial_kernel(ids, own_ref, mate_ref, *refs):
+    count = len(refs) // 3
+    part = own_ref.shape[1] // 2
+    for k in range(count):
+        w, wd, out_ref = refs[k], refs[count + k], refs[2 * count + k]
+        span = w.shape[0] // 2
+        gate = up = down = 0.0
+        for half, rows in ((ids[ids.shape[0] - 1], own_ref), (1 - ids[ids.shape[0] - 1], mate_ref)):
+            base = half * part
+            at = lambda which, n=part, off=0: pl.ds(pl.multiple_of(which * span + base + off, LANES), n)
+            gate += dot(rows[:, :part], w[at(0), :], ((1,), (0,)))
+            up += dot(rows[:, :part], w[at(1), :], ((1,), (0,)))
+            for q in range(part // LANES):
+                cots = rows[:, part + q * LANES : part + (q + 1) * LANES]
+                down += dot(cots, wd[at(0, LANES, q * LANES), :], ((1,), (1,)))
+        out_ref[...] = jnp.concatenate([gate, up, down], axis=1).astype(BF)
+
+
+def point_kernel(*refs):
+    trio_ref, pair_ref = refs[-2:]
+    total = refs[0][...].astype(F32)
+    for part_ref in refs[1:-2]:
+        total += part_ref[...].astype(F32)
     unit = total.shape[1] // 3
     gate, up, d_hidden = total[:, :unit], total[:, unit : 2 * unit], total[:, 2 * unit :]
     s = jax.nn.sigmoid(gate)
@@ -167,24 +172,26 @@
     dg = (d_hidden * up * s * (1.0 + gate * (1.0 - s))).astype(BF)
     du = (d_hidden * gate * s).astype(BF)
     trio_ref[...] = jnp.concatenate([hid, dg, du], axis=1)
-    pair = jnp.concatenate([dg, du], axis=1)
-    for k in range(part_ref.shape[0]):
-        spread_ref[k] = pair
-
-
-def share_kernel(ids, *refs):
-    pairs, blocks, out_ref, acc = refs[0], refs[1:-2], refs[-2], refs[-1]
+    pair_ref[...] = jnp.concatenate([dg, du], axis=1)
+
+
+def share_kernel(which, ids, *refs):
+    out_ref, acc = refs[-2:]
+    count = len(refs) // 2 - 1
     part = out_ref.shape[1]
-    unit = pairs.shape[2] // 2
-    for k, w in enumerate(blocks):
-        pair = pairs[ids[k]]
-        total = dot(pair[:, :unit], w[:part, :], ((1,), (1,)))
-        total += dot(pair[:, unit:], w[part : 2 * part, :], ((1,), (1,)))
+    unit = refs[0].shape[1] // 2
+    half = ids[ids.shape[0] - 1] if which == 0 else 1 - ids[ids.shape[0] - 1]
+    for k in range(count):
+        pair, w = refs[k], refs[count + k]
+        span = w.shape[0] // 2
+        at = lambda n: pl.ds(pl.multiple_of(n * span + half * part, LANES), part)
+        total = dot(pair[:, :unit], w[at(0), :], ((1,), (1,)))
+        total += dot(pair[:, unit:], w[at(1), :], ((1,), (1,)))
         if k == 0:
             acc[...] = total
         else:
             acc[...] += total
-    out_ref[...] = acc[...].astype(BF)
+    out_ref[...] = acc[...].astype(out_ref.dtype)
 
 
 def grad_kernel(ids, *refs):
@@ -244,11 +251,13 @@
     )
     column = lax.all_to_all(packed, "dp", split_axis=0, concat_axis=0, tiled=True)
 
-    turns = (2, 6, 1, 3, 7, 4, 5)
-    sources = jnp.stack([me_d] + [me_d ^ k for k in turns]).astype(jnp.int32)
-    cut = jax.ShapeDtypeStruct((3 * part, hidden), BF)
-    sends = call(block_kernel, (sources,), (w_gate[0], w_up[0], w_down[0]), (cut,) * groups, 0)
-    blocks = [sends[0]] + [flip(b, "dp", k, groups) for k, b in zip(turns, sends[1:])]
+    turns = (2, 6, 4)
+    ring_len = groups // 2
+    sources = jnp.stack([me_d // 2] + [(me_d ^ k) // 2 for k in turns] + [me_d % 2]).astype(jnp.int32)
+    cut = lambda n: (jax.ShapeDtypeStruct((n * part, hidden), BF),) * ring_len
+    sends = call(block_kernel, (sources,), (w_gate[0], w_up[0], w_down[0]), cut(4) + cut(2), 0)
+    arrive = lambda sent: [sent[0]] + [flip(b, "dp", k, groups) for k, b in zip(turns, sent[1:])]
+    w_in, w_out = arrive(sends[:ring_len]), arrive(sends[ring_len:])
 
     chunk = 2 * parts * low + 16 * (-(-2 * parts // 16))
     to_home, places = call(
@@ -262,36 +271,42 @@
     def exchange(x):
         return lax.all_to_all(x, "expert", split_axis=0, concat_axis=0, tiled=True)
 
-    arrived = exchange(after(to_home, *blocks[1:4]))
-    both = from_chunks(after(arrived, *blocks[4:6]), experts, low, 2 * parts)
+    arrived = exchange(after(to_home, *w_in[1:3]))
+    both = from_chunks(after(arrived, w_in[3]), experts, low, 2 * parts)
+    mate_both = flip(both, "dp", 1, groups)
     unit = 2 * slot_count * width * hidden
     sums = call(
-        partial_kernel, (sources,), (both, *blocks),
-        jax.ShapeDtypeStruct((groups, slot_count, 3 * hidden), BF), 3 * unit,
-    )
-    slot_rows = jnp.where(flipped, across(both), both)
-    sums = after(sums, slot_rows)
-    sums = lax.all_to_all(sums, "dp", split_axis=0, concat_axis=0, tiled=True)
-    trio, pairs = call(
-        point_kernel, (), (sums,),
+        partial_kernel, (sources,), (both, mate_both, *w_in, *w_out),
+        (jax.ShapeDtypeStruct((slot_count, 3 * hidden), BF),) * ring_len, 3 * unit,
+    )
+    sums = arrive(sums)
+    trio, pair = call(
+        point_kernel, (), sums,
         (
             jax.ShapeDtypeStruct((slot_count, 3 * hidden), BF),
-            jax.ShapeDtypeStruct((groups, slot_count, 2 * hidden), BF),
+            jax.ShapeDtypeStruct((slot_count, 2 * hidden), BF),
         ), unit // 100,
     )
-    pairs = lax.all_to_all(pairs, "dp", split_axis=0, concat_axis=0, tiled=True)
-    ring = gather_slices(slot_rows, me_d, groups)
-    pairs = after(pairs, ring[2], ring[3])
-    share = call(
-        share_kernel, (sources,), (pairs, *blocks),
-        jax.ShapeDtypeStruct((slot_count, part), BF), 2 * unit,
-        [pltpu.VMEM((slot_count, part), F32)],
-    )
+    flips = across(after(both, mate_both))
+    pairs = arrive((after(pair, flips),) * ring_len)
+    slot_rows = jnp.where(flipped, flips, both)
+    slot_mate = flip(slot_rows, "dp", 1, groups)
+    ring = gather_slices(after(slot_rows, *pairs), after(slot_mate, *pairs), groups)
+
+    halves = [
+        call(
+            functools.partial(share_kernel, which), (sources,), (*pairs, *w_in),
+            jax.ShapeDtypeStruct((slot_count, part), kind), unit,
+            [pltpu.VMEM((slot_count, part), F32)],
+        )
+        for which, kind in ((1, BF), (0, F32))
+    ]
+    share = (flip(halves[0], "dp", 1, groups).astype(F32) + halves[1]).astype(BF)
     shapes = tuple(jax.ShapeDtypeStruct(w.shape[1:], BF) for w in (w_gate, w_up, w_down))
     grads = call(grad_kernel, (ids,), (*ring, trio, across(trio)), shapes, 3 * unit)
 
     back = exchange(to_chunks(share, experts, low))
-    back = from_chunks(after(back, ring[4], ring[5]), experts, low, parts)
+    back = from_chunks(back, experts, low, parts)
     total = dot(places, back, ((1,), (0,))).astype(BF)
     mine = lax.all_to_all(total.reshape(groups, stride, part), "dp", split_axis=0, concat_axis=0, tiled=True)
     grad_input = mine[:, :n_tok].transpose(1, 0, 2).reshape(1, 1, n_tok, width)

time: 271 us -> 268 us (0.989)
  local copies, waits for them, and re-layouts: 16.8 us -> 9.72 us
  blocking collectives: 20.2 us -> 25.1 us
  starting transfers between devices: 61.4 us -> 65.2 us
  waiting for transfers between devices: 137 us -> 134 us
    all_to_all x2 -> x0, waiting for transfers between devices: 27.2 us -> none  [the longest x1 19.5 us: shards(): sums = lax.all_to_all(sums, 'dp', split_axis=0, concat_axis=0, tiled=True)]
    all_to_all x1, waiting for transfers between devices: 0.01 us -> 24.7 us  [shards(): lax.all_to_all(total.reshape(groups, stride, part), 'dp', split_axis=0, c...]
    ppermute x10 -> x17, starting transfers between devices: 13.1 us -> 27 us  [flip(): return lax.ppermute(x, axis, [(i, i ^ bit) for i in range(size)])]
    all_to_all x2 -> x0, starting transfers between devices: 11.8 us -> none  [the longest x1 6.43 us: shards(): pairs = lax.all_to_all(pairs, 'dp', split_axis=0, concat_axis=0, tiled=True)]
    ppermute x6, waiting for transfers between devices: 10.5 us -> 0.02 us  [hop(): return lax.ppermute(x, axis, [(i, (i + step) % size) for i in range(size)])]
    ppermute x10 -> x17, waiting for transfers between devices: 86 us -> 94.3 us  [flip(): return lax.ppermute(x, axis, [(i, i ^ bit) for i in range(size)])]
    unnamed x58 -> x48, local copies, waits for them, and re-layouts: 11.3 us -> 5.96 us
    all_to_all x1, blocking collectives: 20.2 us -> 25.1 us  [shards(): lax.all_to_all(packed, 'dp', split_axis=0, concat_axis=0, tiled=True)]
  transfers between devices with their start and end apart: 21 -> 26, of which waited for: 10 -> 15; matrix products, arithmetic and copies ran while one was open for 2% -> 2% of each run, Pallas kernels for 8% -> 4%
where the time goes in v4:
time: 268 us; the launch traced here: 265 us
  waiting for transfers between devices  134 us (50%)
  starting transfers between devices  65.2 us (24%)
  Pallas kernels  25.6 us (10%)
  blocking collectives  25.1 us (9%)
  local copies, waits for them, and re-layouts  9.72 us (4%)
  other arithmetic  3.01 us (1%)
    ppermute x17, waiting for transfers between devices, flip(): return lax.ppermute(x, axis, [(i, i ^ bit) for i in range(size)])  94.3 us
    ppermute x17, starting transfers between devices, flip(): return lax.ppermute(x, axis, [(i, i ^ bit) for i in range(size)])  27 us
    all_to_all x2, starting transfers between devices, exchange(): return lax.all_to_all(x, 'expert', split_axis=0, concat_axis=0, tiled=True)  26.6 us
    pallas_call x8, Pallas kernels, call(): pl.pallas_call(kernel, out_shape=outs, in_specs=[pl.BlockSpec(memory_spac...  25.6 us
    all_to_all x1, blocking collectives, shards(): lax.all_to_all(packed, 'dp', split_axis=0, concat_axis=0, tiled=True)  25.1 us
    all_to_all x1, waiting for transfers between devices, shards(): lax.all_to_all(total.reshape(groups, stride, part), 'dp', split_axis=0, c...  24.7 us
    all_to_all x2, waiting for transfers between devices, exchange(): return lax.all_to_all(x, 'expert', split_axis=0, concat_axis=0, tiled=True)  14.8 us
    ppermute x6, starting transfers between devices, hop(): return lax.ppermute(x, axis, [(i, (i + step) % size) for i in range(size)])  7.42 us
  transfers between devices with their start and end apart: 26, of which 15 were waited for; matrix products, arithmetic and copies ran while one was open for 2% of the time, Pallas kernels for 4%

profile of v4, /device:TPU:6, one launch (start us, length us, event | category | flops | bytes accessed | tf_op | source)
XLA Modules:
  0.0 264.9 jit_solution(5583432746321355798)
XLA Ops:
  0.8 4.6 %shard_map.113 = (bf16[3584,128]{1,0:T(8,128)(2,1)S(1)}, bf16[3584,128]{1,0:T(8,128)(2,1)}, bf16[3584,128]{1,0:T(8,128)(2,1)}, bf16[3584,128]{1,0:T(8,128)(2,1)S...) custom-call(s32[5]{0:T(128)S(1)} %stack.47.ids, ...), custom_call_target="tpu_custom_call" | custom-call | bytes 11010048 | tf_op jit(solution)/shard_map/pallas_call | solution.py:214
  13.7 25.1 %all_to_all.20.rows_ref = bf16[8,16,1920]{2,1,0:T(8,128)(2,1)S(1)} all-to-all(bf16[8,16,1920]{2,1,0:T(8,128)(2,1)S(1)} %shard_map.111), channel_id=1, replica_groups=mesh['dp'=8,'expert'=32] {'dp'}, dimensions={0} | all-to-all | bytes 983040 | tf_op jit(solution)/shard_map/all_to_all | solution.py:252
  41.2 11.6 %all-to-all-start.1 = ((bf16[32,128,128]{2,1,0:T(8,128)(2,1)}), bf16[32,128,128]{2,1,0:T(8,128)(2,1)}, u32[]{:S(2)}, u32[]{:S(2)}) async-start(bf16[32,128,128]{2,1,0:T(8,128)(2,1)} %copy-done), calls=%async_computation.1 | async-start | bytes 2097152 | tf_op jit(solution)/shard_map/all_to_all | solution.py:272
  54.6 22.5 %collective-permute-done.2.refs_3_.refs_7_ = bf16[3584,128]{1,0:T(8,128)(2,1)} collective-permute-done((bf16[3584,128]{1,0:T(8,128)(2,1)}, bf16[3584,128]{1,0:T(8,128)(2,1)}, u32[]{:S(2)}, u32[]{:S(2)}) %collective-permute-start.2) | collective-permute-done | bytes 917536 | tf_op jit(solution)/shard_map/ppermute | solution.py:24
  77.1 3.0 %all-to-all-done.1 = bf16[32,128,128]{2,1,0:T(8,128)(2,1)} async-done(((bf16[32,128,128]{2,1,0:T(8,128)(2,1)}), bf16[32,128,128]{2,1,0:T(8,128)(2,1)}, u32[]{:S(2)}, u32[]{:S(2)}) %all-to-all-start.1) | async-done | bytes 1048608 | tf_op jit(solution)/shard_map/all_to_all | solution.py:272
  83.5 23.3 %collective-permute-done.3.mate_ref = bf16[288,1792]{1,0:T(8,128)(2,1)S(1)} collective-permute-done((bf16[288,1792]{1,0:T(8,128)(2,1)S(1)}, bf16[288,1792]{1,0:T(8,128)(2,1)S(1)}, u32[]{:S(2)}, u32[]{:S(2)}) %collective-permute-start.3) | collective-permute-done | bytes 1032224 | tf_op jit(solution)/shard_map/ppermute | solution.py:24
  112.5 9.4 %collective-permute-done.4.refs_5_ = bf16[1792,128]{1,0:T(8,128)(2,1)S(1)} collective-permute-done((bf16[1792,128]{1,0:T(8,128)(2,1)S(1)}, bf16[1792,128]{1,0:T(8,128)(2,1)S(1)}, u32[]{:S(2)}, u32[]{:S(2)}) %collective-permute-start.4) | collective-permute-done | bytes 458784 | tf_op jit(solution)/shard_map/ppermute | solution.py:24
  121.8 5.6 %collective-permute-done.5.refs_6_ = bf16[1792,128]{1,0:T(8,128)(2,1)S(1)} collective-permute-done((bf16[1792,128]{1,0:T(8,128)(2,1)S(1)}, bf16[1792,128]{1,0:T(8,128)(2,1)S(1)}, u32[]{:S(2)}, u32[]{:S(2)}) %collective-permute-start.5) | collective-permute-done | bytes 458784 | tf_op jit(solution)/shard_map/ppermute | solution.py:24
  129.2 5.3 %shard_map.114 = (bf16[288,384]{1,0:T(8,128)(2,1)S(1)}, bf16[288,384]{1,0:T(8,128)(2,1)S(1)}, bf16[288,384]{1,0:T(8,128)(2,1)S(1)}, bf16[288,384]{1,0:T(8,128)(2,1)S(1)}) custom-call(s32[5]{0:T(128)S(1)} %stack.47.ids, bf16[288,1792]{1,0:T(8,128)(2,1)} %copy-done.14, bf16[288,1792]{1,0:T(8,128)(2,1)} %copy-done.19, ...), custom_call_target="tpu_custom_call" | custom-call | flops 1585446912 | bytes 8454144 | tf_op jit(solution)/shard_map/pallas_call | solution.py:214
  134.7 2.2 collective-permute-start.8
  140.5 4.5 %collective-permute-done.8.refs_2_ = bf16[288,384]{1,0:T(8,128)(2,1)S(1)} collective-permute-done((bf16[288,384]{1,0:T(8,128)(2,1)S(1)}, bf16[288,384]{1,0:T(8,128)(2,1)S(1)}, u32[]{:S(2)}, u32[]{:S(2)}) %collective-permute-start.8) | collective-permute-done | bytes 221216 | tf_op jit(solution)/shard_map/ppermute | solution.py:24
  145.9 2.8 %collective-permute-start.13 = (bf16[288,256]{1,0:T(8,128)(2,1)S(1)}, bf16[288,256]{1,0:T(8,128)(2,1)S(1)}, u32[]{:S(2)}, u32[]{:S(2)}) collective-permute-start(bf16[288,256]{1,0:T(8,128)(2,1)S(1)} %get-tuple-element.47.refs_0_), channel_id=1, source_target_pairs={{0,128},{32,160},{64,192},{96,224},{128,0},{160,32},{192,64},{224,... | collective-permute-start | bytes 442376 | tf_op jit(solution)/shard_map/ppermute | solution.py:24
  152.5 2.5 collective-permute-done.12.refs_2_
  155.7 2.4 shard_map.116
  161.5 2.4 shard_map.117
  164.0 8.9 %collective-permute-done.14 = bf16[288,896]{1,0:T(8,128)(2,1)S(1)} collective-permute-done((bf16[288,896]{1,0:T(8,128)(2,1)S(1)}, bf16[288,896]{1,0:T(8,128)(2,1)S(1)}, u32[]{:S(2)}, u32[]{:S(2)}) %collective-permute-start.14) | collective-permute-done | bytes 516128 | tf_op jit(solution)/shard_map/ppermute | solution.py:24
  173.1 12.6 %collective-permute-done.15.refs_1_ = bf16[288,1792]{1,0:T(8,128)(2,1)} collective-permute-done((bf16[288,1792]{1,0:T(8,128)(2,1)}, bf16[288,1792]{1,0:T(8,128)(2,1)}, u32[]{:S(2)}, u32[]{:S(2)}) %collective-permute-start.15) | collective-permute-done | bytes 1032224 | tf_op jit(solution)/shard_map/ppermute | solution.py:24
  188.8 15.0 %all-to-all-start.2 = ((bf16[32,64,128]{2,1,0:T(8,128)(2,1)}), bf16[32,64,128]{2,1,0:T(8,128)(2,1)S(1)}, u32[]{:S(2)}, u32[]{:S(2)}) async-start(bf16[32,64,128]{2,1,0:T(8,128)(2,1)} %maximum_maximum_fusion), calls=%async_computation.2 | async-start | bytes 1048576 | tf_op jit(solution)/shard_map/all_to_all | solution.py:272
  205.9 3.2 %collective-permute-start.21 = (bf16[288,1792]{1,0:T(8,128)(2,1)}, bf16[288,1792]{1,0:T(8,128)(2,1)}, u32[]{:S(2)}, u32[]{:S(2)}) collective-permute-start(bf16[288,1792]{1,0:T(8,128)(2,1)} %collective-permute-done.19.refs_5_), channel_id=1, source_target_pairs={{0,192},{32,224},{64,0},{96,32},{128,64},{160,96},{192,128},{224,1... | collective-permute-start | bytes 3096584 | tf_op jit(solution)/shard_map/ppermute | solution.py:20
  209.1 11.8 %all-to-all-done.2 = bf16[32,64,128]{2,1,0:T(8,128)(2,1)S(1)} async-done(((bf16[32,64,128]{2,1,0:T(8,128)(2,1)}), bf16[32,64,128]{2,1,0:T(8,128)(2,1)S(1)}, u32[]{:S(2)}, u32[]{:S(2)}) %all-to-all-start.2) | async-done | bytes 524320 | tf_op jit(solution)/shard_map/all_to_all | solution.py:272
  222.0 4.1 %all-to-all-start.3 = ((bf16[8,16,896]{2,1,0:T(8,128)(2,1)}), bf16[8,16,896]{2,1,0:T(8,128)(2,1)S(1)}, u32[]{:S(2)}, u32[]{:S(2)}) async-start(bf16[8,16,896]{2,1,0:T(8,128)(2,1)} %bitcast.64), calls=%async_computation.3 | async-start | bytes 458752 | tf_op jit(solution)/shard_map/all_to_all | solution.py:311
  226.2 3.9 %collective-permute-start.22 = (bf16[288,384]{1,0:T(8,128)(2,1)S(1)}, bf16[288,384]{1,0:T(8,128)(2,1)S(1)}, u32[]{:S(2)}, u32[]{:S(2)}) collective-permute-start(bf16[288,384]{1,0:T(8,128)(2,1)S(1)} %copy-done.4), channel_id=1, source_target_pairs={{0,16},{1,17},{2,18},{3,19},{4,20},{5,21},{6,22},{7,23},{8,24},{9,... | collective-permute-start | bytes 663560 | tf_op jit(solution)/shard_map/ppermute | solution.py:24
  230.1 24.7 %all-to-all-done.3 = bf16[8,16,896]{2,1,0:T(8,128)(2,1)S(1)} async-done(((bf16[8,16,896]{2,1,0:T(8,128)(2,1)}), bf16[8,16,896]{2,1,0:T(8,128)(2,1)S(1)}, u32[]{:S(2)}, u32[]{:S(2)}) %all-to-all-start.3) | async-done | bytes 229408 | tf_op jit(solution)/shard_map/all_to_all | solution.py:311
  255.7 9.2 %shard_map.118 = (bf16[7168,128]{1,0:T(8,128)(2,1)}, bf16[7168,128]{1,0:T(8,128)(2,1)}, bf16[128,7168]{1,0:T(8,128)(2,1)}) custom-call(s32[9]{0:T(128)S(1)} %concatenate.15.ids, bf16[288,1792]{1,0:T(8,128)(2,1)} %broadcast_select_fusion.refs_0_, bf16[288,1792]{1,0:T(8,128)(2,1)} %collective-permute-done.15.refs_1_, ...), custom_call_target="tpu_custom_call" | custom-call | flops 1585446912 | bytes 14204928 | tf_op jit(solution)/shard_map/pallas_call | solution.py:214
  (106 shorter events, 42.8 us)
Async XLA Ops:
  8.7 32.5 %collective-permute-start = (bf16[3584,128]{1,0:T(8,128)(2,1)}, bf16[3584,128]{1,0:T(8,128)(2,1)S(1)}, u32[]{:S(2)}, u32[]{:S(2)}) collective-permute-start(bf16[3584,128]{1,0:T(8,128)(2,1)} %get-tuple-element.31), channel_id=1, source_target_pairs={{0,64},{32,96},{64,0},{96,32},{128,192},{160,224},{192,128},{224,1... | collective-permute-start | bytes 2752520 | tf_op jit(solution)/shard_map/ppermute | solution.py:24
  10.2 30.9 %collective-permute-start.1 = (bf16[3584,128]{1,0:T(8,128)(2,1)}, bf16[3584,128]{1,0:T(8,128)(2,1)S(1)}, u32[]{:S(2)}, u32[]{:S(2)}) collective-permute-start(bf16[3584,128]{1,0:T(8,128)(2,1)} %get-tuple-element.32), channel_id=1, source_target_pairs={{0,192},{32,224},{64,128},{96,160},{128,64},{160,96},{192,0},{224,... | collective-permute-start | bytes 2752520 | tf_op jit(solution)/shard_map/ppermute | solution.py:24
  41.2 39.0 %all-to-all-start.1 = ((bf16[32,128,128]{2,1,0:T(8,128)(2,1)}), bf16[32,128,128]{2,1,0:T(8,128)(2,1)}, u32[]{:S(2)}, u32[]{:S(2)}) async-start(bf16[32,128,128]{2,1,0:T(8,128)(2,1)} %copy-done), calls=%async_computation.1 | async-start | bytes 2097152 | tf_op jit(solution)/shard_map/all_to_all | solution.py:272
  52.8 24.3 %collective-permute-start.2 = (bf16[3584,128]{1,0:T(8,128)(2,1)}, bf16[3584,128]{1,0:T(8,128)(2,1)}, u32[]{:S(2)}, u32[]{:S(2)}) collective-permute-start(bf16[3584,128]{1,0:T(8,128)(2,1)} %copy-done.5), channel_id=1, source_target_pairs={{0,128},{32,160},{64,192},{96,224},{128,0},{160,32},{192,64},{224,... | collective-permute-start | bytes 2752520 | tf_op jit(solution)/shard_map/ppermute | solution.py:24
  82.6 24.2 %collective-permute-start.3 = (bf16[288,1792]{1,0:T(8,128)(2,1)S(1)}, bf16[288,1792]{1,0:T(8,128)(2,1)S(1)}, u32[]{:S(2)}, u32[]{:S(2)}) collective-permute-start(bf16[288,1792]{1,0:T(8,128)(2,1)S(1)} %pad_maximum_fusion.own_ref), channel_id=1, source_target_pairs={{0,32},{32,0},{64,96},{96,64},{128,160},{160,128},{192,224},{224,1... | collective-permute-start | bytes 3096584 | tf_op jit(solution)/shard_map/ppermute | solution.py:24
  106.8 39.1 %collective-permute-start.10 = (bf16[288,1792]{1,0:T(8,128)(2,1)S(1)}, bf16[288,1792]{1,0:T(8,128)(2,1)S(1)}, u32[]{:S(2)}, u32[]{:S(2)}) collective-permute-start(bf16[288,1792]{1,0:T(8,128)(2,1)S(1)} %pad_maximum_fusion.own_ref), channel_id=1, source_target_pairs={{0,16},{1,17},{2,18},{3,19},{4,20},{5,21},{6,22},{7,23},{8,24},{9,... | collective-permute-start | bytes 3096584 | tf_op jit(solution)/shard_map/ppermute | solution.py:24
  108.4 13.5 %collective-permute-start.4 = (bf16[1792,128]{1,0:T(8,128)(2,1)S(1)}, bf16[1792,128]{1,0:T(8,128)(2,1)S(1)}, u32[]{:S(2)}, u32[]{:S(2)}) collective-permute-start(bf16[1792,128]{1,0:T(8,128)(2,1)S(1)} %copy-done.11), channel_id=1, source_target_pairs={{0,64},{32,96},{64,0},{96,32},{128,192},{160,224},{192,128},{224,1... | collective-permute-start | bytes 1376264 | tf_op jit(solution)/shard_map/ppermute | solution.py:24
  108.5 19.0 %collective-permute-start.5 = (bf16[1792,128]{1,0:T(8,128)(2,1)S(1)}, bf16[1792,128]{1,0:T(8,128)(2,1)S(1)}, u32[]{:S(2)}, u32[]{:S(2)}) collective-permute-start(bf16[1792,128]{1,0:T(8,128)(2,1)S(1)} %copy-done.9), channel_id=1, source_target_pairs={{0,192},{32,224},{64,128},{96,160},{128,64},{160,96},{192,0},{224,... | collective-permute-start | bytes 1376264 | tf_op jit(solution)/shard_map/ppermute | solution.py:24
  110.7 18.5 %collective-permute-start.6 = (bf16[1792,128]{1,0:T(8,128)(2,1)S(1)}, bf16[1792,128]{1,0:T(8,128)(2,1)S(1)}, u32[]{:S(2)}, u32[]{:S(2)}) collective-permute-start(bf16[1792,128]{1,0:T(8,128)(2,1)S(1)} %copy-done.7), channel_id=1, source_target_pairs={{0,128},{32,160},{64,192},{96,224},{128,0},{160,32},{192,64},{224,... | collective-permute-start | bytes 1376264 | tf_op jit(solution)/shard_map/ppermute | solution.py:24
  134.7 10.3 %collective-permute-start.8 = (bf16[288,384]{1,0:T(8,128)(2,1)S(1)}, bf16[288,384]{1,0:T(8,128)(2,1)S(1)}, u32[]{:S(2)}, u32[]{:S(2)}) collective-permute-start(bf16[288,384]{1,0:T(8,128)(2,1)S(1)} %get-tuple-element.43), channel_id=1, source_target_pairs={{0,192},{32,224},{64,128},{96,160},{128,64},{160,96},{192,0},{224,... | collective-permute-start | bytes 663560 | tf_op jit(solution)/shard_map/ppermute | solution.py:24
  136.9 8.1 %collective-permute-start.9 = (bf16[288,384]{1,0:T(8,128)(2,1)S(1)}, bf16[288,384]{1,0:T(8,128)(2,1)S(1)}, u32[]{:S(2)}, u32[]{:S(2)}) collective-permute-start(bf16[288,384]{1,0:T(8,128)(2,1)S(1)} %get-tuple-element.44), channel_id=1, source_target_pairs={{0,128},{32,160},{64,192},{96,224},{128,0},{160,32},{192,64},{224,... | collective-permute-start | bytes 663560 | tf_op jit(solution)/shard_map/ppermute | solution.py:24
  145.9 6.6 %collective-permute-start.13 = (bf16[288,256]{1,0:T(8,128)(2,1)S(1)}, bf16[288,256]{1,0:T(8,128)(2,1)S(1)}, u32[]{:S(2)}, u32[]{:S(2)}) collective-permute-start(bf16[288,256]{1,0:T(8,128)(2,1)S(1)} %get-tuple-element.47.refs_0_), channel_id=1, source_target_pairs={{0,128},{32,160},{64,192},{96,224},{128,0},{160,32},{192,64},{224,... | collective-permute-start | bytes 442376 | tf_op jit(solution)/shard_map/ppermute | solution.py:24
  148.7 6.4 %collective-permute-start.12 = (bf16[288,256]{1,0:T(8,128)(2,1)S(1)}, bf16[288,256]{1,0:T(8,128)(2,1)S(1)}, u32[]{:S(2)}, u32[]{:S(2)}) collective-permute-start(bf16[288,256]{1,0:T(8,128)(2,1)S(1)} %get-tuple-element.47.refs_0_), channel_id=1, source_target_pairs={{0,192},{32,224},{64,128},{96,160},{128,64},{160,96},{192,0},{224,... | collective-permute-start | bytes 442376 | tf_op jit(solution)/shard_map/ppermute | solution.py:24
  158.1 14.8 %collective-permute-start.14 = (bf16[288,896]{1,0:T(8,128)(2,1)S(1)}, bf16[288,896]{1,0:T(8,128)(2,1)S(1)}, u32[]{:S(2)}, u32[]{:S(2)}) collective-permute-start(bf16[288,896]{1,0:T(8,128)(2,1)S(1)} %shard_map.116), channel_id=1, source_target_pairs={{0,32},{32,0},{64,96},{96,64},{128,160},{160,128},{192,224},{224,1... | collective-permute-start | bytes 1548296 | tf_op jit(solution)/shard_map/ppermute | solution.py:24
  160.3 25.5 %collective-permute-start.15 = (bf16[288,1792]{1,0:T(8,128)(2,1)}, bf16[288,1792]{1,0:T(8,128)(2,1)}, u32[]{:S(2)}, u32[]{:S(2)}) collective-permute-start(bf16[288,1792]{1,0:T(8,128)(2,1)} %broadcast_select_fusion.refs_0_), channel_id=1, source_target_pairs={{0,32},{32,0},{64,96},{96,64},{128,160},{160,128},{192,224},{224,1... | collective-permute-start | bytes 3096584 | tf_op jit(solution)/shard_map/ppermute | solution.py:24
  161.5 44.3 %collective-permute-start.16 = (bf16[288,1792]{1,0:T(8,128)(2,1)}, bf16[288,1792]{1,0:T(8,128)(2,1)}, u32[]{:S(2)}, u32[]{:S(2)}) collective-permute-start(bf16[288,1792]{1,0:T(8,128)(2,1)} %broadcast_select_fusion.refs_0_), channel_id=1, source_target_pairs={{0,64},{32,96},{64,128},{96,160},{128,192},{160,224},{192,0},{224,... | collective-permute-start | bytes 3096584 | tf_op jit(solution)/shard_map/ppermute | solution.py:20
  185.7 20.2 %collective-permute-start.19 = (bf16[288,1792]{1,0:T(8,128)(2,1)}, bf16[288,1792]{1,0:T(8,128)(2,1)}, u32[]{:S(2)}, u32[]{:S(2)}) collective-permute-start(bf16[288,1792]{1,0:T(8,128)(2,1)} %collective-permute-done.15.refs_1_), channel_id=1, source_target_pairs={{0,192},{32,224},{64,0},{96,32},{128,64},{160,96},{192,128},{224,1... | collective-permute-start | bytes 3096584 | tf_op jit(solution)/shard_map/ppermute | solution.py:20
  188.8 32.1 %all-to-all-start.2 = ((bf16[32,64,128]{2,1,0:T(8,128)(2,1)}), bf16[32,64,128]{2,1,0:T(8,128)(2,1)S(1)}, u32[]{:S(2)}, u32[]{:S(2)}) async-start(bf16[32,64,128]{2,1,0:T(8,128)(2,1)} %maximum_maximum_fusion), calls=%async_computation.2 | async-start | bytes 1048576 | tf_op jit(solution)/shard_map/all_to_all | solution.py:272
  203.8 51.9 %collective-permute-start.17 = (bf16[288,1792]{1,0:T(8,128)(2,1)}, bf16[288,1792]{1,0:T(8,128)(2,1)S(1)}, u32[]{:S(2)}, u32[]{:S(2)}) collective-permute-start(bf16[288,1792]{1,0:T(8,128)(2,1)} %broadcast_select_fusion.refs_0_), channel_id=1, source_target_pairs={{0,192},{32,224},{64,0},{96,32},{128,64},{160,96},{192,128},{224,1... | collective-permute-start | bytes 3096584 | tf_op jit(solution)/shard_map/ppermute | solution.py:20
  203.9 51.8 %collective-permute-start.18 = (bf16[288,1792]{1,0:T(8,128)(2,1)}, bf16[288,1792]{1,0:T(8,128)(2,1)S(1)}, u32[]{:S(2)}, u32[]{:S(2)}) collective-permute-start(bf16[288,1792]{1,0:T(8,128)(2,1)} %collective-permute-done.15.refs_1_), channel_id=1, source_target_pairs={{0,64},{32,96},{64,128},{96,160},{128,192},{160,224},{192,0},{224,... | collective-permute-start | bytes 3096584 | tf_op jit(solution)/shard_map/ppermute | solution.py:20
  205.9 49.8 %collective-permute-start.20 = (bf16[288,1792]{1,0:T(8,128)(2,1)}, bf16[288,1792]{1,0:T(8,128)(2,1)}, u32[]{:S(2)}, u32[]{:S(2)}) collective-permute-start(bf16[288,1792]{1,0:T(8,128)(2,1)} %collective-permute-done.16.refs_2_), channel_id=1, source_target_pairs={{0,64},{32,96},{64,128},{96,160},{128,192},{160,224},{192,0},{224,... | collective-permute-start | bytes 3096584 | tf_op jit(solution)/shard_map/ppermute | solution.py:20
  205.9 49.8 %collective-permute-start.21 = (bf16[288,1792]{1,0:T(8,128)(2,1)}, bf16[288,1792]{1,0:T(8,128)(2,1)}, u32[]{:S(2)}, u32[]{:S(2)}) collective-permute-start(bf16[288,1792]{1,0:T(8,128)(2,1)} %collective-permute-done.19.refs_5_), channel_id=1, source_target_pairs={{0,192},{32,224},{64,0},{96,32},{128,64},{160,96},{192,128},{224,1... | collective-permute-start | bytes 3096584 | tf_op jit(solution)/shard_map/ppermute | solution.py:20
  222.0 32.8 %all-to-all-start.3 = ((bf16[8,16,896]{2,1,0:T(8,128)(2,1)}), bf16[8,16,896]{2,1,0:T(8,128)(2,1)S(1)}, u32[]{:S(2)}, u32[]{:S(2)}) async-start(bf16[8,16,896]{2,1,0:T(8,128)(2,1)} %bitcast.64), calls=%async_computation.3 | async-start | bytes 458752 | tf_op jit(solution)/shard_map/all_to_all | solution.py:311
  226.2 29.5 %collective-permute-start.22 = (bf16[288,384]{1,0:T(8,128)(2,1)S(1)}, bf16[288,384]{1,0:T(8,128)(2,1)S(1)}, u32[]{:S(2)}, u32[]{:S(2)}) collective-permute-start(bf16[288,384]{1,0:T(8,128)(2,1)S(1)} %copy-done.4), channel_id=1, source_target_pairs={{0,16},{1,17},{2,18},{3,19},{4,20},{5,21},{6,22},{7,23},{8,24},{9,... | collective-permute-start | bytes 663560 | tf_op jit(solution)/shard_map/ppermute | solution.py:24
  (25 other events, 393.2 us)

commit v5 on v4

--- a/solution.py
+++ b/solution.py
@@ -46,16 +46,20 @@
         out[d] = jnp.concatenate([rows_here, fill], axis=0)
 
 
-def block_kernel(ids, wg, wu, wd, *outs):
-    count = len(outs) // 2
+def in_kernel(ids, wg, wu, *outs):
     span = outs[0].shape[0] // 2
-    for k in range(count):
-        start = pl.multiple_of(ids[k] * span, span)
-        outs[k][:span, :] = wg[pl.ds(start, span), :]
-        outs[k][span:, :] = wu[pl.ds(start, span), :]
+    for k, out in enumerate(outs):
+        at = pl.ds(pl.multiple_of(ids[k] * span, span), span)
+        out[:span, :] = wg[at, :]
+        out[span:, :] = wu[at, :]
+
+
+def out_kernel(ids, wd, *outs):
+    span = outs[0].shape[0]
+    for k, out in enumerate(outs):
         for q in range(span // LANES):
-            at = pl.ds(pl.multiple_of(start + q * LANES, LANES), LANES)
-            outs[count + k][q * LANES : (q + 1) * LANES, :] = wd[:, at]
+            at = pl.ds(pl.multiple_of(ids[k] * span + q * LANES, LANES), LANES)
+            out[q * LANES : (q + 1) * LANES, :] = wd[:, at]
 
 
 def route_kernel(n_tok, topk, rows_ref, out_ref, place_ref):
@@ -145,18 +149,19 @@
 def partial_kernel(ids, own_ref, mate_ref, *refs):
     count = len(refs) // 3
     part = own_ref.shape[1] // 2
+    mine = ids[ids.shape[0] - 1]
     for k in range(count):
-        w, wd, out_ref = refs[k], refs[count + k], refs[2 * count + k]
-        span = w.shape[0] // 2
+        w, wd, out_ref = refs[k::count]
+        span = 2 * part
+        at = lambda which, base, n: pl.ds(pl.multiple_of(which * span + base, LANES), n)
         gate = up = down = 0.0
-        for half, rows in ((ids[ids.shape[0] - 1], own_ref), (1 - ids[ids.shape[0] - 1], mate_ref)):
+        for half, rows in ((mine, own_ref), (1 - mine, mate_ref)):
             base = half * part
-            at = lambda which, n=part, off=0: pl.ds(pl.multiple_of(which * span + base + off, LANES), n)
-            gate += dot(rows[:, :part], w[at(0), :], ((1,), (0,)))
-            up += dot(rows[:, :part], w[at(1), :], ((1,), (0,)))
+            gate += dot(rows[:, :part], w[at(0, base, part), :], ((1,), (0,)))
+            up += dot(rows[:, :part], w[at(1, base, part), :], ((1,), (0,)))
             for q in range(part // LANES):
                 cots = rows[:, part + q * LANES : part + (q + 1) * LANES]
-                down += dot(cots, wd[at(0, LANES, q * LANES), :], ((1,), (1,)))
+                down += dot(cots, wd[at(0, base + q * LANES, LANES), :], ((1,), (1,)))
         out_ref[...] = jnp.concatenate([gate, up, down], axis=1).astype(BF)
 
 
@@ -180,11 +185,11 @@
     count = len(refs) // 2 - 1
     part = out_ref.shape[1]
     unit = refs[0].shape[1] // 2
-    half = ids[ids.shape[0] - 1] if which == 0 else 1 - ids[ids.shape[0] - 1]
+    mine = ids[ids.shape[0] - 1]
+    base = (mine if which == 0 else 1 - mine) * part
     for k in range(count):
-        pair, w = refs[k], refs[count + k]
-        span = w.shape[0] // 2
-        at = lambda n: pl.ds(pl.multiple_of(n * span + half * part, LANES), part)
+        pair, w = refs[:-2][k::count]
+        at = lambda which: pl.ds(pl.multiple_of(which * 2 * part + base, LANES), part)
         total = dot(pair[:, :unit], w[at(0), :], ((1,), (1,)))
         total += dot(pair[:, unit:], w[at(1), :], ((1,), (1,)))
         if k == 0:
@@ -254,25 +259,27 @@
     turns = (2, 6, 4)
     ring_len = groups // 2
     sources = jnp.stack([me_d // 2] + [(me_d ^ k) // 2 for k in turns] + [me_d % 2]).astype(jnp.int32)
+    chunk = 2 * parts * low + 16 * (-(-2 * parts // 16))
+    def route(rows):
+        return call(
+            functools.partial(route_kernel, n_tok, topk), (), (rows,),
+            (
+                jax.ShapeDtypeStruct((experts, chunk, LANES), BF),
+                jax.ShapeDtypeStruct((groups * stride, slot_count), BF),
+            ), 0,
+        )
+
+    arrive = lambda sent: [sent[0]] + [flip(b, "dp", k, groups) for k, b in zip(turns, sent[1:])]
     cut = lambda n: (jax.ShapeDtypeStruct((n * part, hidden), BF),) * ring_len
-    sends = call(block_kernel, (sources,), (w_gate[0], w_up[0], w_down[0]), cut(4) + cut(2), 0)
-    arrive = lambda sent: [sent[0]] + [flip(b, "dp", k, groups) for k, b in zip(turns, sent[1:])]
-    w_in, w_out = arrive(sends[:ring_len]), arrive(sends[ring_len:])
-
-    chunk = 2 * parts * low + 16 * (-(-2 * parts // 16))
-    to_home, places = call(
-        functools.partial(route_kernel, n_tok, topk), (), (column,),
-        (
-            jax.ShapeDtypeStruct((experts, chunk, LANES), BF),
-            jax.ShapeDtypeStruct((groups * stride, slot_count), BF),
-        ), 0,
-    )
+    w_out = arrive(call(out_kernel, (after(sources, packed),), (w_down[0],), cut(2), 0))
+    to_home, places = route(column)
+    w_in = arrive(call(in_kernel, (after(sources, to_home),), (w_gate[0], w_up[0]), cut(4), 0))
 
     def exchange(x):
         return lax.all_to_all(x, "expert", split_axis=0, concat_axis=0, tiled=True)
 
-    arrived = exchange(after(to_home, *w_in[1:3]))
-    both = from_chunks(after(arrived, w_in[3]), experts, low, 2 * parts)
+    arrived = exchange(after(to_home, *w_out[1:3]))
+    both = from_chunks(after(arrived, w_out[3], *w_in[1:3]), experts, low, 2 * parts)
     mate_both = flip(both, "dp", 1, groups)
     unit = 2 * slot_count * width * hidden
     sums = call(
@@ -287,11 +294,11 @@
             jax.ShapeDtypeStruct((slot_count, 2 * hidden), BF),
         ), unit // 100,
     )
-    flips = across(after(both, mate_both))
-    pairs = arrive((after(pair, flips),) * ring_len)
-    slot_rows = jnp.where(flipped, flips, both)
-    slot_mate = flip(slot_rows, "dp", 1, groups)
-    ring = gather_slices(after(slot_rows, *pairs), after(slot_mate, *pairs), groups)
+    here, there = (both, mate_both), [across(after(v, mate_both)) for v in (both, mate_both)]
+    pairs = arrive((pair,) * ring_len)
+    pairs = lax.optimization_barrier((*pairs, there[0]))[:ring_len]
+    slots = [jnp.where(flipped, a, b) for a, b in zip(there, here)]
+    ring = gather_slices(after(slots[0], *pairs), slots[1], groups)
 
     halves = [
         call(
@@ -302,6 +309,7 @@
         for which, kind in ((1, BF), (0, F32))
     ]
     share = (flip(halves[0], "dp", 1, groups).astype(F32) + halves[1]).astype(BF)
+    share = after(share, there[1])
     shapes = tuple(jax.ShapeDtypeStruct(w.shape[1:], BF) for w in (w_gate, w_up, w_down))
     grads = call(grad_kernel, (ids,), (*ring, trio, across(trio)), shapes, 3 * unit)
 

time: 268 us -> 239 us (0.89)
  waiting for transfers between devices: 134 us -> 116 us
  blocking collectives: 25.1 us -> 16.3 us
  starting transfers between devices: 65.2 us -> 57.5 us
  local copies, waits for them, and re-layouts: 9.72 us -> 15.3 us
  other arithmetic: 3.01 us -> 7.75 us
  Pallas kernels: 25.6 us -> 22.5 us
    ppermute x17, waiting for transfers between devices: 94.3 us -> 77.7 us  [flip(): return lax.ppermute(x, axis, [(i, i ^ bit) for i in range(size)])]
    all_to_all x1, blocking collectives: 25.1 us -> 16.3 us  [shards(): lax.all_to_all(packed, 'dp', split_axis=0, concat_axis=0, tiled=True)]
    all_to_all x2, waiting for transfers between devices: 14.8 us -> 9.93 us  [exchange(): return lax.all_to_all(x, 'expert', split_axis=0, concat_axis=0, tiled=True)]
    all_to_all x2, starting transfers between devices: 26.6 us -> 22.3 us  [exchange(): return lax.all_to_all(x, 'expert', split_axis=0, concat_axis=0, tiled=True)]
    unnamed x48 -> x46, local copies, waits for them, and re-layouts: 5.96 us -> 10.1 us
    select_n x1 -> x2, other arithmetic: 1.23 us -> 4.79 us  [shards(): slots = [jnp.where(flipped, a, b) for a, b in zip(there, here)]]
    pallas_call x8 -> x9, Pallas kernels: 25.6 us -> 22.5 us  [call(): pl.pallas_call(kernel, out_shape=outs, in_specs=[pl.BlockSpec(memory_spac...]
    ppermute x6, waiting for transfers between devices: 0.02 us -> 2.88 us  [hop(): return lax.ppermute(x, axis, [(i, (i + step) % size) for i in range(size)])]
  transfers between devices with their start and end apart: 26 -> 26, of which waited for: 15 -> 11; matrix products, arithmetic and copies ran while one was open for 2% -> 4% of each run, Pallas kernels for 4% -> 5%
where the time goes in v5:
time: 239 us; the launch traced here: 238 us
  waiting for transfers between devices  116 us (49%)
  starting transfers between devices  57.5 us (24%)
  Pallas kernels  22.5 us (9%)
  blocking collectives  16.3 us (7%)
  local copies, waits for them, and re-layouts  15.3 us (6%)
  other arithmetic  7.75 us (3%)
    ppermute x17, waiting for transfers between devices, flip(): return lax.ppermute(x, axis, [(i, i ^ bit) for i in range(size)])  77.7 us
    ppermute x17, starting transfers between devices, flip(): return lax.ppermute(x, axis, [(i, i ^ bit) for i in range(size)])  25.6 us
    all_to_all x1, waiting for transfers between devices, shards(): lax.all_to_all(total.reshape(groups, stride, part), 'dp', split_axis=0, c...  25.6 us
    pallas_call x9, Pallas kernels, call(): pl.pallas_call(kernel, out_shape=outs, in_specs=[pl.BlockSpec(memory_spac...  22.5 us
    all_to_all x2, starting transfers between devices, exchange(): return lax.all_to_all(x, 'expert', split_axis=0, concat_axis=0, tiled=True)  22.3 us
    all_to_all x1, blocking collectives, shards(): lax.all_to_all(packed, 'dp', split_axis=0, concat_axis=0, tiled=True)  16.3 us
    unnamed x46, local copies, waits for them, and re-layouts  10.1 us
    all_to_all x2, waiting for transfers between devices, exchange(): return lax.all_to_all(x, 'expert', split_axis=0, concat_axis=0, tiled=True)  9.93 us
  transfers between devices with their start and end apart: 26, of which 11 were waited for; matrix products, arithmetic and copies ran while one was open for 4% of the time, Pallas kernels for 5%

profile of v5, /device:TPU:6, one launch (start us, length us, event | category | flops | bytes accessed | tf_op | source)
XLA Modules:
  0.0 238.1 jit_solution(5670749442150911096)
XLA Ops:
  9.2 2.2 collective-permute-start.1
  11.4 16.3 %all_to_all.20.rows_ref = bf16[8,16,1920]{2,1,0:T(8,128)(2,1)S(1)} all-to-all(bf16[8,16,1920]{2,1,0:T(8,128)(2,1)S(1)} %shard_map.111), channel_id=1, replica_groups=mesh['dp'=8,'expert'=32] {'dp'}, dimensions={0} | all-to-all | bytes 983040 | tf_op jit(solution)/shard_map/all_to_all | solution.py:257
  31.7 11.7 %all-to-all-start.1 = ((bf16[32,128,128]{2,1,0:T(8,128)(2,1)}), bf16[32,128,128]{2,1,0:T(8,128)(2,1)}, u32[]{:S(2)}, u32[]{:S(2)}) async-start(bf16[32,128,128]{2,1,0:T(8,128)(2,1)} %copy-done.4), calls=%async_computation.1 | async-start | bytes 2097152 | tf_op jit(solution)/shard_map/all_to_all | solution.py:279
  46.2 2.2 collective-permute-start.4
  48.3 1.8 collective-permute-start.2
  50.2 29.7 %collective-permute-done.2.refs_7_ = bf16[1792,128]{1,0:T(8,128)(2,1)S(1)} collective-permute-done((bf16[1792,128]{1,0:T(8,128)(2,1)S(1)}, bf16[1792,128]{1,0:T(8,128)(2,1)S(1)}, u32[]{:S(2)}, u32[]{:S(2)}) %collective-permute-start.2) | collective-permute-done | bytes 458784 | tf_op jit(solution)/shard_map/ppermute | solution.py:24
  86.1 22.6 %collective-permute-done.5.mate_ref = bf16[288,1792]{1,0:T(8,128)(2,1)} collective-permute-done((bf16[288,1792]{1,0:T(8,128)(2,1)}, bf16[288,1792]{1,0:T(8,128)(2,1)}, u32[]{:S(2)}, u32[]{:S(2)}) %collective-permute-start.5) | collective-permute-done | bytes 1032224 | tf_op jit(solution)/shard_map/ppermute | solution.py:24
  109.1 3.1 %collective-permute-start.15 = (bf16[288,1792]{1,0:T(8,128)(2,1)}, bf16[288,1792]{1,0:T(8,128)(2,1)}, u32[]{:S(2)}, u32[]{:S(2)}) collective-permute-start(bf16[288,1792]{1,0:T(8,128)(2,1)} %collective-permute-done.5.mate_ref), channel_id=1, source_target_pairs={{0,16},{1,17},{2,18},{3,19},{4,20},{5,21},{6,22},{7,23},{8,24},{9,... | collective-permute-start | bytes 3096584 | tf_op jit(solution)/shard_map/ppermute | solution.py:24
  113.1 5.2 %shard_map.115 = (bf16[288,384]{1,0:T(8,128)(2,1)S(1)}, bf16[288,384]{1,0:T(8,128)(2,1)S(1)}, bf16[288,384]{1,0:T(8,128)(2,1)S(1)}, bf16[288,384]{1,0:T(8,128)(2,1)S(1)}) custom-call(s32[5]{0:T(128)S(1)} %stack.47.ids, bf16[288,1792]{1,0:T(8,128)(2,1)} %pad_maximum_fusion.own_ref, bf16[288,1792]{1,0:T(8,128)(2,1)} %collective-permute-done.5.mate_ref, ...), custom_call_target="tpu_custom_call" | custom-call | flops 1585446912 | bytes 8454144 | tf_op jit(solution)/shard_map/pallas_call | solution.py:219
  119.8 2.7 %collective-permute-start.9 = (bf16[288,384]{1,0:T(8,128)(2,1)S(1)}, bf16[288,384]{1,0:T(8,128)(2,1)S(1)}, u32[]{:S(2)}, u32[]{:S(2)}) collective-permute-start(bf16[288,384]{1,0:T(8,128)(2,1)S(1)} %get-tuple-element.52), channel_id=1, source_target_pairs={{0,128},{32,160},{64,192},{96,224},{128,0},{160,32},{192,64},{224,... | collective-permute-start | bytes 663560 | tf_op jit(solution)/shard_map/ppermute | solution.py:24
  122.5 3.4 %collective-permute-done.7.refs_1_ = bf16[288,384]{1,0:T(8,128)(2,1)S(1)} collective-permute-done((bf16[288,384]{1,0:T(8,128)(2,1)S(1)}, bf16[288,384]{1,0:T(8,128)(2,1)S(1)}, u32[]{:S(2)}, u32[]{:S(2)}) %collective-permute-start.7) | collective-permute-done | bytes 221216 | tf_op jit(solution)/shard_map/ppermute | solution.py:24
  126.0 3.9 %collective-permute-done.8.refs_2_ = bf16[288,384]{1,0:T(8,128)(2,1)S(1)} collective-permute-done((bf16[288,384]{1,0:T(8,128)(2,1)S(1)}, bf16[288,384]{1,0:T(8,128)(2,1)S(1)}, u32[]{:S(2)}, u32[]{:S(2)}) %collective-permute-start.8) | collective-permute-done | bytes 221216 | tf_op jit(solution)/shard_map/ppermute | solution.py:24
  135.7 1.9 collective-permute-done.12.refs_3_
  139.1 2.5 %broadcast_select_fusion.1.refs_0_ = bf16[288,1792]{1,0:T(8,128)(2,1)} fusion(bf16[288,1792]{1,0:T(8,128)(2,1)} %collective-permute-done.13, pred[]{:T(512)S(6)} %ne.71, bf16[32,1792]{1,0:T(8,128)(2,1)} %bitcast.61, bf16[256,1792]{1,0:T(8,128)(2,1)} %copy-done.19), kind=kLoop, calls=%fused_computation.4 | loop fusion | flops 2580480 | bytes 3096577 | tf_op jit(solution)/shard_map/jit(_where)/select_n | solution.py:300
  144.6 13.8 %collective-permute-done.15 = bf16[288,1792]{1,0:T(8,128)(2,1)} collective-permute-done((bf16[288,1792]{1,0:T(8,128)(2,1)}, bf16[288,1792]{1,0:T(8,128)(2,1)}, u32[]{:S(2)}, u32[]{:S(2)}) %collective-permute-start.15) | collective-permute-done | bytes 1032224 | tf_op jit(solution)/shard_map/ppermute | solution.py:24
  158.3 2.3 broadcast_select_fusion.refs_1_
  165.7 10.6 %all-to-all-start.2 = ((bf16[32,64,128]{2,1,0:T(8,128)(2,1)}), bf16[32,64,128]{2,1,0:T(8,128)(2,1)S(1)}, u32[]{:S(2)}, u32[]{:S(2)}) async-start(bf16[32,64,128]{2,1,0:T(8,128)(2,1)} %maximum_maximum_fusion), calls=%async_computation.2 | async-start | bytes 1048576 | tf_op jit(solution)/shard_map/all_to_all | solution.py:279
  178.6 2.9 %collective-permute-done.19.refs_5_ = bf16[288,1792]{1,0:T(8,128)(2,1)} collective-permute-done((bf16[288,1792]{1,0:T(8,128)(2,1)}, bf16[288,1792]{1,0:T(8,128)(2,1)}, u32[]{:S(2)}, u32[]{:S(2)}) %collective-permute-start.19) | collective-permute-done | bytes 1032224 | tf_op jit(solution)/shard_map/ppermute | solution.py:20
  181.5 2.1 collective-permute-start.21
  183.6 9.9 %all-to-all-done.2 = bf16[32,64,128]{2,1,0:T(8,128)(2,1)S(1)} async-done(((bf16[32,64,128]{2,1,0:T(8,128)(2,1)}), bf16[32,64,128]{2,1,0:T(8,128)(2,1)S(1)}, u32[]{:S(2)}, u32[]{:S(2)}) %all-to-all-start.2) | async-done | bytes 524320 | tf_op jit(solution)/shard_map/all_to_all | solution.py:279
  194.6 3.9 %all-to-all-start.3 = ((bf16[8,16,896]{2,1,0:T(8,128)(2,1)}), bf16[8,16,896]{2,1,0:T(8,128)(2,1)S(1)}, u32[]{:S(2)}, u32[]{:S(2)}) async-start(bf16[8,16,896]{2,1,0:T(8,128)(2,1)} %bitcast.64), calls=%async_computation.3 | async-start | bytes 458752 | tf_op jit(solution)/shard_map/all_to_all | solution.py:319
  198.5 3.9 %collective-permute-start.22 = (bf16[288,384]{1,0:T(8,128)(2,1)S(1)}, bf16[288,384]{1,0:T(8,128)(2,1)S(1)}, u32[]{:S(2)}, u32[]{:S(2)}) collective-permute-start(bf16[288,384]{1,0:T(8,128)(2,1)S(1)} %copy-done.14), channel_id=1, source_target_pairs={{0,16},{1,17},{2,18},{3,19},{4,20},{5,21},{6,22},{7,23},{8,24},{9,... | collective-permute-start | bytes 663560 | tf_op jit(solution)/shard_map/ppermute | solution.py:24
  202.4 25.6 %all-to-all-done.3 = bf16[8,16,896]{2,1,0:T(8,128)(2,1)S(1)} async-done(((bf16[8,16,896]{2,1,0:T(8,128)(2,1)}), bf16[8,16,896]{2,1,0:T(8,128)(2,1)S(1)}, u32[]{:S(2)}, u32[]{:S(2)}) %all-to-all-start.3) | async-done | bytes 229408 | tf_op jit(solution)/shard_map/all_to_all | solution.py:319
  229.0 9.2 %shard_map.119 = (bf16[7168,128]{1,0:T(8,128)(2,1)}, bf16[7168,128]{1,0:T(8,128)(2,1)}, bf16[128,7168]{1,0:T(8,128)(2,1)}) custom-call(s32[9]{0:T(128)S(1)} %concatenate.15.ids, bf16[288,1792]{1,0:T(8,128)(2,1)} %broadcast_select_fusion.1.refs_0_, bf16[288,1792]{1,0:T(8,128)(2,1)} %broadcast_select_fusion.refs_1_, ...), custom_call_target="tpu_custom_call" | custom-call | flops 1585446912 | bytes 14204928 | tf_op jit(solution)/shard_map/pallas_call | solution.py:219
  (106 shorter events, 43.1 us)
Async XLA Ops:
  7.6 22.5 %collective-permute-start = (bf16[1792,128]{1,0:T(8,128)(2,1)S(1)}, bf16[1792,128]{1,0:T(8,128)(2,1)S(1)}, u32[]{:S(2)}, u32[]{:S(2)}) collective-permute-start(bf16[1792,128]{1,0:T(8,128)(2,1)S(1)} %get-tuple-element.38), channel_id=1, source_target_pairs={{0,64},{32,96},{64,0},{96,32},{128,192},{160,224},{192,128},{224,1... | collective-permute-start | bytes 1376264 | tf_op jit(solution)/shard_map/ppermute | solution.py:24
  9.2 21.7 %collective-permute-start.1 = (bf16[1792,128]{1,0:T(8,128)(2,1)S(1)}, bf16[1792,128]{1,0:T(8,128)(2,1)S(1)}, u32[]{:S(2)}, u32[]{:S(2)}) collective-permute-start(bf16[1792,128]{1,0:T(8,128)(2,1)S(1)} %get-tuple-element.39), channel_id=1, source_target_pairs={{0,192},{32,224},{64,128},{96,160},{128,64},{160,96},{192,0},{224,... | collective-permute-start | bytes 1376264 | tf_op jit(solution)/shard_map/ppermute | solution.py:24
  31.7 49.1 %all-to-all-start.1 = ((bf16[32,128,128]{2,1,0:T(8,128)(2,1)}), bf16[32,128,128]{2,1,0:T(8,128)(2,1)}, u32[]{:S(2)}, u32[]{:S(2)}) async-start(bf16[32,128,128]{2,1,0:T(8,128)(2,1)} %copy-done.4), calls=%async_computation.1 | async-start | bytes 2097152 | tf_op jit(solution)/shard_map/all_to_all | solution.py:279
  46.1 34.6 %collective-permute-start.3 = (bf16[3584,128]{1,0:T(8,128)(2,1)S(1)}, bf16[3584,128]{1,0:T(8,128)(2,1)S(1)}, u32[]{:S(2)}, u32[]{:S(2)}) collective-permute-start(bf16[3584,128]{1,0:T(8,128)(2,1)S(1)} %get-tuple-element.43), channel_id=1, source_target_pairs={{0,64},{32,96},{64,0},{96,32},{128,192},{160,224},{192,128},{224,1... | collective-permute-start | bytes 2752520 | tf_op jit(solution)/shard_map/ppermute | solution.py:24
  46.2 34.6 %collective-permute-start.4 = (bf16[3584,128]{1,0:T(8,128)(2,1)S(1)}, bf16[3584,128]{1,0:T(8,128)(2,1)S(1)}, u32[]{:S(2)}, u32[]{:S(2)}) collective-permute-start(bf16[3584,128]{1,0:T(8,128)(2,1)S(1)} %get-tuple-element.44), channel_id=1, source_target_pairs={{0,192},{32,224},{64,128},{96,160},{128,64},{160,96},{192,0},{224,... | collective-permute-start | bytes 2752520 | tf_op jit(solution)/shard_map/ppermute | solution.py:24
  48.3 31.6 %collective-permute-start.2 = (bf16[1792,128]{1,0:T(8,128)(2,1)S(1)}, bf16[1792,128]{1,0:T(8,128)(2,1)S(1)}, u32[]{:S(2)}, u32[]{:S(2)}) collective-permute-start(bf16[1792,128]{1,0:T(8,128)(2,1)S(1)} %copy-done.18), channel_id=1, source_target_pairs={{0,128},{32,160},{64,192},{96,224},{128,0},{160,32},{192,64},{224,... | collective-permute-start | bytes 1376264 | tf_op jit(solution)/shard_map/ppermute | solution.py:24
  84.3 24.3 %collective-permute-start.5 = (bf16[288,1792]{1,0:T(8,128)(2,1)}, bf16[288,1792]{1,0:T(8,128)(2,1)}, u32[]{:S(2)}, u32[]{:S(2)}) collective-permute-start(bf16[288,1792]{1,0:T(8,128)(2,1)} %pad_maximum_fusion.own_ref), channel_id=1, source_target_pairs={{0,32},{32,0},{64,96},{96,64},{128,160},{160,128},{192,224},{224,1... | collective-permute-start | bytes 3096584 | tf_op jit(solution)/shard_map/ppermute | solution.py:24
  85.1 27.1 %collective-permute-start.6 = (bf16[3584,128]{1,0:T(8,128)(2,1)S(1)}, bf16[3584,128]{1,0:T(8,128)(2,1)S(1)}, u32[]{:S(2)}, u32[]{:S(2)}) collective-permute-start(bf16[3584,128]{1,0:T(8,128)(2,1)S(1)} %copy-done.16), channel_id=1, source_target_pairs={{0,128},{32,160},{64,192},{96,224},{128,0},{160,32},{192,64},{224,... | collective-permute-start | bytes 2752520 | tf_op jit(solution)/shard_map/ppermute | solution.py:24
  108.6 30.5 %collective-permute-start.13 = (bf16[288,1792]{1,0:T(8,128)(2,1)}, bf16[288,1792]{1,0:T(8,128)(2,1)}, u32[]{:S(2)}, u32[]{:S(2)}) collective-permute-start(bf16[288,1792]{1,0:T(8,128)(2,1)} %pad_maximum_fusion.own_ref), channel_id=1, source_target_pairs={{0,16},{1,17},{2,18},{3,19},{4,20},{5,21},{6,22},{7,23},{8,24},{9,... | collective-permute-start | bytes 3096584 | tf_op jit(solution)/shard_map/ppermute | solution.py:24
  109.1 49.3 %collective-permute-start.15 = (bf16[288,1792]{1,0:T(8,128)(2,1)}, bf16[288,1792]{1,0:T(8,128)(2,1)}, u32[]{:S(2)}, u32[]{:S(2)}) collective-permute-start(bf16[288,1792]{1,0:T(8,128)(2,1)} %collective-permute-done.5.mate_ref), channel_id=1, source_target_pairs={{0,16},{1,17},{2,18},{3,19},{4,20},{5,21},{6,22},{7,23},{8,24},{9,... | collective-permute-start | bytes 3096584 | tf_op jit(solution)/shard_map/ppermute | solution.py:24
  118.3 7.6 %collective-permute-start.7 = (bf16[288,384]{1,0:T(8,128)(2,1)S(1)}, bf16[288,384]{1,0:T(8,128)(2,1)S(1)}, u32[]{:S(2)}, u32[]{:S(2)}) collective-permute-start(bf16[288,384]{1,0:T(8,128)(2,1)S(1)} %get-tuple-element.50), channel_id=1, source_target_pairs={{0,64},{32,96},{64,0},{96,32},{128,192},{160,224},{192,128},{224,1... | collective-permute-start | bytes 663560 | tf_op jit(solution)/shard_map/ppermute | solution.py:24
  118.4 11.4 %collective-permute-start.8 = (bf16[288,384]{1,0:T(8,128)(2,1)S(1)}, bf16[288,384]{1,0:T(8,128)(2,1)S(1)}, u32[]{:S(2)}, u32[]{:S(2)}) collective-permute-start(bf16[288,384]{1,0:T(8,128)(2,1)S(1)} %get-tuple-element.51), channel_id=1, source_target_pairs={{0,192},{32,224},{64,128},{96,160},{128,64},{160,96},{192,0},{224,... | collective-permute-start | bytes 663560 | tf_op jit(solution)/shard_map/ppermute | solution.py:24
  119.8 10.0 %collective-permute-start.9 = (bf16[288,384]{1,0:T(8,128)(2,1)S(1)}, bf16[288,384]{1,0:T(8,128)(2,1)S(1)}, u32[]{:S(2)}, u32[]{:S(2)}) collective-permute-start(bf16[288,384]{1,0:T(8,128)(2,1)S(1)} %get-tuple-element.52), channel_id=1, source_target_pairs={{0,128},{32,160},{64,192},{96,224},{128,0},{160,32},{192,64},{224,... | collective-permute-start | bytes 663560 | tf_op jit(solution)/shard_map/ppermute | solution.py:24
  132.2 6.9 %collective-permute-start.11 = (bf16[288,256]{1,0:T(8,128)(2,1)S(1)}, bf16[288,256]{1,0:T(8,128)(2,1)S(1)}, u32[]{:S(2)}, u32[]{:S(2)}) collective-permute-start(bf16[288,256]{1,0:T(8,128)(2,1)S(1)} %get-tuple-element.55.refs_0_), channel_id=1, source_target_pairs={{0,192},{32,224},{64,128},{96,160},{128,64},{160,96},{192,0},{224,... | collective-permute-start | bytes 442376 | tf_op jit(solution)/shard_map/ppermute | solution.py:24
  143.4 21.0 %collective-permute-start.14 = (bf16[288,896]{1,0:T(8,128)(2,1)S(1)}, bf16[288,896]{1,0:T(8,128)(2,1)S(1)}, u32[]{:S(2)}, u32[]{:S(2)}) collective-permute-start(bf16[288,896]{1,0:T(8,128)(2,1)S(1)} %shard_map.117), channel_id=1, source_target_pairs={{0,32},{32,0},{64,96},{96,64},{128,160},{160,128},{192,224},{224,1... | collective-permute-start | bytes 1548296 | tf_op jit(solution)/shard_map/ppermute | solution.py:24
  144.3 34.2 %collective-permute-start.16 = (bf16[288,1792]{1,0:T(8,128)(2,1)}, bf16[288,1792]{1,0:T(8,128)(2,1)}, u32[]{:S(2)}, u32[]{:S(2)}) collective-permute-start(bf16[288,1792]{1,0:T(8,128)(2,1)} %broadcast_select_fusion.1.refs_0_), channel_id=1, source_target_pairs={{0,64},{32,96},{64,128},{96,160},{128,192},{160,224},{192,0},{224,... | collective-permute-start | bytes 3096584 | tf_op jit(solution)/shard_map/ppermute | solution.py:20
  160.6 20.8 %collective-permute-start.19 = (bf16[288,1792]{1,0:T(8,128)(2,1)}, bf16[288,1792]{1,0:T(8,128)(2,1)}, u32[]{:S(2)}, u32[]{:S(2)}) collective-permute-start(bf16[288,1792]{1,0:T(8,128)(2,1)} %broadcast_select_fusion.refs_1_), channel_id=1, source_target_pairs={{0,192},{32,224},{64,0},{96,32},{128,64},{160,96},{192,128},{224,1... | collective-permute-start | bytes 3096584 | tf_op jit(solution)/shard_map/ppermute | solution.py:20
  165.7 27.8 %all-to-all-start.2 = ((bf16[32,64,128]{2,1,0:T(8,128)(2,1)}), bf16[32,64,128]{2,1,0:T(8,128)(2,1)S(1)}, u32[]{:S(2)}, u32[]{:S(2)}) async-start(bf16[32,64,128]{2,1,0:T(8,128)(2,1)} %maximum_maximum_fusion), calls=%async_computation.2 | async-start | bytes 1048576 | tf_op jit(solution)/shard_map/all_to_all | solution.py:279
  176.4 52.6 %collective-permute-start.17 = (bf16[288,1792]{1,0:T(8,128)(2,1)}, bf16[288,1792]{1,0:T(8,128)(2,1)S(1)}, u32[]{:S(2)}, u32[]{:S(2)}) collective-permute-start(bf16[288,1792]{1,0:T(8,128)(2,1)} %broadcast_select_fusion.1.refs_0_), channel_id=1, source_target_pairs={{0,192},{32,224},{64,0},{96,32},{128,64},{160,96},{192,128},{224,1... | collective-permute-start | bytes 3096584 | tf_op jit(solution)/shard_map/ppermute | solution.py:20
  177.5 51.5 %collective-permute-start.18 = (bf16[288,1792]{1,0:T(8,128)(2,1)}, bf16[288,1792]{1,0:T(8,128)(2,1)S(1)}, u32[]{:S(2)}, u32[]{:S(2)}) collective-permute-start(bf16[288,1792]{1,0:T(8,128)(2,1)} %broadcast_select_fusion.refs_1_), channel_id=1, source_target_pairs={{0,64},{32,96},{64,128},{96,160},{128,192},{160,224},{192,0},{224,... | collective-permute-start | bytes 3096584 | tf_op jit(solution)/shard_map/ppermute | solution.py:20
  178.5 50.5 %collective-permute-start.20 = (bf16[288,1792]{1,0:T(8,128)(2,1)}, bf16[288,1792]{1,0:T(8,128)(2,1)}, u32[]{:S(2)}, u32[]{:S(2)}) collective-permute-start(bf16[288,1792]{1,0:T(8,128)(2,1)} %collective-permute-done.16.refs_2_), channel_id=1, source_target_pairs={{0,64},{32,96},{64,128},{96,160},{128,192},{160,224},{192,0},{224,... | collective-permute-start | bytes 3096584 | tf_op jit(solution)/shard_map/ppermute | solution.py:20
  181.5 47.5 %collective-permute-start.21 = (bf16[288,1792]{1,0:T(8,128)(2,1)}, bf16[288,1792]{1,0:T(8,128)(2,1)}, u32[]{:S(2)}, u32[]{:S(2)}) collective-permute-start(bf16[288,1792]{1,0:T(8,128)(2,1)} %collective-permute-done.19.refs_5_), channel_id=1, source_target_pairs={{0,192},{32,224},{64,0},{96,32},{128,64},{160,96},{192,128},{224,1... | collective-permute-start | bytes 3096584 | tf_op jit(solution)/shard_map/ppermute | solution.py:20
  194.6 33.5 %all-to-all-start.3 = ((bf16[8,16,896]{2,1,0:T(8,128)(2,1)}), bf16[8,16,896]{2,1,0:T(8,128)(2,1)S(1)}, u32[]{:S(2)}, u32[]{:S(2)}) async-start(bf16[8,16,896]{2,1,0:T(8,128)(2,1)} %bitcast.64), calls=%async_computation.3 | async-start | bytes 458752 | tf_op jit(solution)/shard_map/all_to_all | solution.py:319
  198.5 30.4 %collective-permute-start.22 = (bf16[288,384]{1,0:T(8,128)(2,1)S(1)}, bf16[288,384]{1,0:T(8,128)(2,1)S(1)}, u32[]{:S(2)}, u32[]{:S(2)}) collective-permute-start(bf16[288,384]{1,0:T(8,128)(2,1)S(1)} %copy-done.14), channel_id=1, source_target_pairs={{0,16},{1,17},{2,18},{3,19},{4,20},{5,21},{6,22},{7,23},{8,24},{9,... | collective-permute-start | bytes 663560 | tf_op jit(solution)/shard_map/ppermute | solution.py:24
  (24 other events, 318.9 us)

commit v6 on v5

--- a/solution.py
+++ b/solution.py
@@ -46,20 +46,15 @@
         out[d] = jnp.concatenate([rows_here, fill], axis=0)
 
 
-def in_kernel(ids, wg, wu, *outs):
-    span = outs[0].shape[0] // 2
+def block_kernel(ids, wg, wu, wd, *outs):
+    span = outs[0].shape[0] // 3
     for k, out in enumerate(outs):
-        at = pl.ds(pl.multiple_of(ids[k] * span, span), span)
-        out[:span, :] = wg[at, :]
-        out[span:, :] = wu[at, :]
-
-
-def out_kernel(ids, wd, *outs):
-    span = outs[0].shape[0]
-    for k, out in enumerate(outs):
+        start = pl.multiple_of(ids[k] * span, span)
+        out[:span, :] = wg[pl.ds(start, span), :]
+        out[span : 2 * span, :] = wu[pl.ds(start, span), :]
         for q in range(span // LANES):
-            at = pl.ds(pl.multiple_of(ids[k] * span + q * LANES, LANES), LANES)
-            out[q * LANES : (q + 1) * LANES, :] = wd[:, at]
+            at = pl.ds(pl.multiple_of(start + q * LANES, LANES), LANES)
+            out[2 * span + q * LANES : 2 * span + (q + 1) * LANES, :] = wd[:, at]
 
 
 def route_kernel(n_tok, topk, rows_ref, out_ref, place_ref):
@@ -147,12 +142,12 @@
 
 
 def partial_kernel(ids, own_ref, mate_ref, *refs):
-    count = len(refs) // 3
+    count = len(refs) // 2
     part = own_ref.shape[1] // 2
     mine = ids[ids.shape[0] - 1]
     for k in range(count):
-        w, wd, out_ref = refs[k::count]
-        span = 2 * part
+        w, out_ref = refs[k::count]
+        span = w.shape[0] // 3
         at = lambda which, base, n: pl.ds(pl.multiple_of(which * span + base, LANES), n)
         gate = up = down = 0.0
         for half, rows in ((mine, own_ref), (1 - mine, mate_ref)):
@@ -161,7 +156,7 @@
             up += dot(rows[:, :part], w[at(1, base, part), :], ((1,), (0,)))
             for q in range(part // LANES):
                 cots = rows[:, part + q * LANES : part + (q + 1) * LANES]
-                down += dot(cots, wd[at(0, base + q * LANES, LANES), :], ((1,), (1,)))
+                down += dot(cots, w[at(2, base + q * LANES, LANES), :], ((1,), (1,)))
         out_ref[...] = jnp.concatenate([gate, up, down], axis=1).astype(BF)
 
 
@@ -189,7 +184,7 @@
     base = (mine if which == 0 else 1 - mine) * part
     for k in range(count):
         pair, w = refs[:-2][k::count]
-        at = lambda which: pl.ds(pl.multiple_of(which * 2 * part + base, LANES), part)
+        at = lambda which: pl.ds(pl.multiple_of(which * (w.shape[0] // 3) + base, LANES), part)
         total = dot(pair[:, :unit], w[at(0), :], ((1,), (1,)))
         total += dot(pair[:, unit:], w[at(1), :], ((1,), (1,)))
         if k == 0:
@@ -269,21 +264,22 @@
             ), 0,
         )
 
+    to_home, places = route(column)
+
+    cut = (jax.ShapeDtypeStruct((6 * part, hidden), BF),) * ring_len
+    sends = call(block_kernel, (after(sources, to_home),), (w_gate[0], w_up[0], w_down[0]), cut, 0)
     arrive = lambda sent: [sent[0]] + [flip(b, "dp", k, groups) for k, b in zip(turns, sent[1:])]
-    cut = lambda n: (jax.ShapeDtypeStruct((n * part, hidden), BF),) * ring_len
-    w_out = arrive(call(out_kernel, (after(sources, packed),), (w_down[0],), cut(2), 0))
-    to_home, places = route(column)
-    w_in = arrive(call(in_kernel, (after(sources, to_home),), (w_gate[0], w_up[0]), cut(4), 0))
+    blocks = arrive(sends)
 
     def exchange(x):
         return lax.all_to_all(x, "expert", split_axis=0, concat_axis=0, tiled=True)
 
-    arrived = exchange(after(to_home, *w_out[1:3]))
-    both = from_chunks(after(arrived, w_out[3], *w_in[1:3]), experts, low, 2 * parts)
+    arrived = exchange(to_home)
+    both = from_chunks(after(arrived, *blocks[1:3]), experts, low, 2 * parts)
     mate_both = flip(both, "dp", 1, groups)
     unit = 2 * slot_count * width * hidden
     sums = call(
-        partial_kernel, (sources,), (both, mate_both, *w_in, *w_out),
+        partial_kernel, (sources,), (both, mate_both, *blocks),
         (jax.ShapeDtypeStruct((slot_count, 3 * hidden), BF),) * ring_len, 3 * unit,
     )
     sums = arrive(sums)
@@ -302,19 +298,19 @@
 
     halves = [
         call(
-            functools.partial(share_kernel, which), (sources,), (*pairs, *w_in),
+            functools.partial(share_kernel, which), (sources,), (*pairs, *blocks),
             jax.ShapeDtypeStruct((slot_count, part), kind), unit,
             [pltpu.VMEM((slot_count, part), F32)],
         )
         for which, kind in ((1, BF), (0, F32))
     ]
     share = (flip(halves[0], "dp", 1, groups).astype(F32) + halves[1]).astype(BF)
-    share = after(share, there[1])
+    share = after(share, there[1], ring[2], ring[3])
     shapes = tuple(jax.ShapeDtypeStruct(w.shape[1:], BF) for w in (w_gate, w_up, w_down))
     grads = call(grad_kernel, (ids,), (*ring, trio, across(trio)), shapes, 3 * unit)
 
     back = exchange(to_chunks(share, experts, low))
-    back = from_chunks(back, experts, low, parts)
+    back = from_chunks(after(back, ring[4], ring[5]), experts, low, parts)
     total = dot(places, back, ((1,), (0,))).astype(BF)
     mine = lax.all_to_all(total.reshape(groups, stride, part), "dp", split_axis=0, concat_axis=0, tiled=True)
     grad_input = mine[:, :n_tok].transpose(1, 0, 2).reshape(1, 1, n_tok, width)

time: 239 us -> 218 us (0.912)
  waiting for transfers between devices: 116 us -> 98.6 us
  starting transfers between devices: 57.5 us -> 51.9 us
  Pallas kernels: 22.5 us -> 26.7 us
    all_to_all x1, waiting for transfers between devices: 25.6 us -> 0.01 us  [shards(): lax.all_to_all(total.reshape(groups, stride, part), 'dp', split_axis=0, c...]
    ppermute x17 -> x14, starting transfers between devices: 25.6 us -> 14.6 us  [flip(): return lax.ppermute(x, axis, [(i, i ^ bit) for i in range(size)])]
    ppermute x6, waiting for transfers between devices: 2.88 us -> 13.4 us  [hop(): return lax.ppermute(x, axis, [(i, (i + step) % size) for i in range(size)])]
    ppermute x6, starting transfers between devices: 5.75 us -> 10.3 us  [hop(): return lax.ppermute(x, axis, [(i, (i + step) % size) for i in range(size)])]
    pallas_call x9 -> x8, Pallas kernels: 22.5 us -> 26.7 us  [call(): pl.pallas_call(kernel, out_shape=outs, in_specs=[pl.BlockSpec(memory_spac...]
    unnamed x46 -> x34, local copies, waits for them, and re-layouts: 10.1 us -> 7.34 us
    ppermute x17 -> x14, waiting for transfers between devices: 77.7 us -> 76.7 us  [flip(): return lax.ppermute(x, axis, [(i, i ^ bit) for i in range(size)])]
  transfers between devices with their start and end apart: 26 -> 23, of which waited for: 11 -> 14; matrix products, arithmetic and copies ran while one was open for 4% -> 4% of each run, Pallas kernels for 5% -> 11%
where the time goes in v6:
time: 218 us; the launch traced here: 217 us
  waiting for transfers between devices  98.6 us (45%)
  starting transfers between devices  51.9 us (24%)
  Pallas kernels  26.7 us (12%)
  local copies, waits for them, and re-layouts  15.2 us (7%)
  blocking collectives  14.3 us (7%)
  other arithmetic  6.66 us (3%)
    ppermute x14, waiting for transfers between devices, flip(): return lax.ppermute(x, axis, [(i, i ^ bit) for i in range(size)])  76.7 us
    pallas_call x8, Pallas kernels, call(): pl.pallas_call(kernel, out_shape=outs, in_specs=[pl.BlockSpec(memory_spac...  26.7 us
    all_to_all x2, starting transfers between devices, exchange(): return lax.all_to_all(x, 'expert', split_axis=0, concat_axis=0, tiled=True)  22 us
    ppermute x14, starting transfers between devices, flip(): return lax.ppermute(x, axis, [(i, i ^ bit) for i in range(size)])  14.6 us
    all_to_all x1, blocking collectives, shards(): lax.all_to_all(packed, 'dp', split_axis=0, concat_axis=0, tiled=True)  14.3 us
    ppermute x6, waiting for transfers between devices, hop(): return lax.ppermute(x, axis, [(i, (i + step) % size) for i in range(size)])  13.4 us
    ppermute x6, starting transfers between devices, hop(): return lax.ppermute(x, axis, [(i, (i + step) % size) for i in range(size)])  10.3 us
    all_to_all x2, waiting for transfers between devices, exchange(): return lax.all_to_all(x, 'expert', split_axis=0, concat_axis=0, tiled=True)  8.49 us
  transfers between devices with their start and end apart: 23, of which 14 were waited for; matrix products, arithmetic and copies ran while one was open for 4% of the time, Pallas kernels for 11%

profile of v6, /device:TPU:6, one launch (start us, length us, event | category | flops | bytes accessed | tf_op | source)
XLA Modules:
  0.0 216.8 jit_solution(5341435952822500638)
XLA Ops:
  4.1 14.3 %all_to_all.20.rows_ref = bf16[8,16,1920]{2,1,0:T(8,128)(2,1)S(1)} all-to-all(bf16[8,16,1920]{2,1,0:T(8,128)(2,1)S(1)} %shard_map.111), channel_id=1, replica_groups=mesh['dp'=8,'expert'=32] {'dp'}, dimensions={0} | all-to-all | bytes 983040 | tf_op jit(solution)/shard_map/all_to_all | solution.py:252
  18.4 2.4 %shard_map.112 = (bf16[32,128,128]{2,1,0:T(8,128)(2,1)}, bf16[128,288]{1,0:T(8,128)(2,1)S(1)}) custom-call(bf16[8,16,1920]{2,1,0:T(8,128)(2,1)S(1)} %all_to_all.20.rows_ref), custom_call_target="tpu_custom_call" | custom-call | bytes 1613824 | tf_op jit(solution)/shard_map/pallas_call | solution.py:214
  21.5 11.7 %all-to-all-start.1 = ((bf16[32,128,128]{2,1,0:T(8,128)(2,1)}), bf16[32,128,128]{2,1,0:T(8,128)(2,1)}, u32[]{:S(2)}, u32[]{:S(2)}) async-start(bf16[32,128,128]{2,1,0:T(8,128)(2,1)} %get-tuple-element.31), calls=%async_computation.1 | async-start | bytes 2097152 | tf_op jit(solution)/shard_map/all_to_all | solution.py:275
  33.3 3.3 %shard_map.113 = (bf16[5376,128]{1,0:T(8,128)(2,1)S(1)}, bf16[5376,128]{1,0:T(8,128)(2,1)S(1)}, bf16[5376,128]{1,0:T(8,128)(2,1)S(1)}, bf16[5376,128]{1,0:T(8,128)(2,1)S(1)}) custom-call(s32[5]{0:T(128)S(1)} %stack.47.ids, bf16[7168,128]{1,0:T(8,128)(2,1)} %bitcast.57, bf16[7168,128]{1,0:T(8,128)(2,1)} %bitcast.58, bf16[128,7168]{1,0:T(8,128)(2,1)} %bitcast.59), custom_call_target="tpu_custom_call" | custom-call | bytes 11010048 | tf_op jit(solution)/shard_map/pallas_call | solution.py:214
  38.9 31.1 %collective-permute-done.refs_1_.refs_5_ = bf16[5376,128]{1,0:T(8,128)(2,1)S(1)} collective-permute-done((bf16[5376,128]{1,0:T(8,128)(2,1)S(1)}, bf16[5376,128]{1,0:T(8,128)(2,1)S(1)}, u32[]{:S(2)}, u32[]{:S(2)}) %collective-permute-start) | collective-permute-done | bytes 1376288 | tf_op jit(solution)/shard_map/ppermute | solution.py:24
  76.8 22.2 %collective-permute-done.2.mate_ref = bf16[288,1792]{1,0:T(8,128)(2,1)} collective-permute-done((bf16[288,1792]{1,0:T(8,128)(2,1)}, bf16[288,1792]{1,0:T(8,128)(2,1)}, u32[]{:S(2)}, u32[]{:S(2)}) %collective-permute-start.2) | collective-permute-done | bytes 1032224 | tf_op jit(solution)/shard_map/ppermute | solution.py:24
  99.5 8.9 %collective-permute-done.3.refs_3_.refs_7_ = bf16[5376,128]{1,0:T(8,128)(2,1)S(1)} collective-permute-done((bf16[5376,128]{1,0:T(8,128)(2,1)S(1)}, bf16[5376,128]{1,0:T(8,128)(2,1)S(1)}, u32[]{:S(2)}, u32[]{:S(2)}) %collective-permute-start.3) | collective-permute-done | bytes 1376288 | tf_op jit(solution)/shard_map/ppermute | solution.py:24
  109.4 5.8 %shard_map.114 = (bf16[288,384]{1,0:T(8,128)(2,1)S(1)}, bf16[288,384]{1,0:T(8,128)(2,1)S(1)}, bf16[288,384]{1,0:T(8,128)(2,1)S(1)}, bf16[288,384]{1,0:T(8,128)(2,1)S(1)}) custom-call(s32[5]{0:T(128)S(1)} %stack.47.ids, bf16[288,1792]{1,0:T(8,128)(2,1)} %pad_maximum_fusion.own_ref, bf16[288,1792]{1,0:T(8,128)(2,1)} %collective-permute-done.2.mate_ref, ...), custom_call_target="tpu_custom_call" | custom-call | flops 1585446912 | bytes 8454144 | tf_op jit(solution)/shard_map/pallas_call | solution.py:214
  116.8 2.6 %collective-permute-start.6 = (bf16[288,384]{1,0:T(8,128)(2,1)S(1)}, bf16[288,384]{1,0:T(8,128)(2,1)S(1)}, u32[]{:S(2)}, u32[]{:S(2)}) collective-permute-start(bf16[288,384]{1,0:T(8,128)(2,1)S(1)} %get-tuple-element.41), channel_id=1, source_target_pairs={{0,128},{32,160},{64,192},{96,224},{128,0},{160,32},{192,64},{224,... | collective-permute-start | bytes 663560 | tf_op jit(solution)/shard_map/ppermute | solution.py:24
  120.4 2.6 %collective-permute-done.4.refs_1_ = bf16[288,384]{1,0:T(8,128)(2,1)S(1)} collective-permute-done((bf16[288,384]{1,0:T(8,128)(2,1)S(1)}, bf16[288,384]{1,0:T(8,128)(2,1)S(1)}, u32[]{:S(2)}, u32[]{:S(2)}) %collective-permute-start.4) | collective-permute-done | bytes 221216 | tf_op jit(solution)/shard_map/ppermute | solution.py:24
  123.0 3.7 %collective-permute-done.5.refs_2_ = bf16[288,384]{1,0:T(8,128)(2,1)S(1)} collective-permute-done((bf16[288,384]{1,0:T(8,128)(2,1)S(1)}, bf16[288,384]{1,0:T(8,128)(2,1)S(1)}, u32[]{:S(2)}, u32[]{:S(2)}) %collective-permute-start.5) | collective-permute-done | bytes 221216 | tf_op jit(solution)/shard_map/ppermute | solution.py:24
  138.5 2.8 %collective-permute-start.14 = (bf16[288,1792]{1,0:T(8,128)(2,1)S(1)}, bf16[288,1792]{1,0:T(8,128)(2,1)S(1)}, u32[]{:S(2)}, u32[]{:S(2)}) collective-permute-start(bf16[288,1792]{1,0:T(8,128)(2,1)S(1)} %broadcast_select_fusion.1.refs_0_), channel_id=1, source_target_pairs={{0,192},{32,224},{64,0},{96,32},{128,64},{160,96},{192,128},{224,1... | collective-permute-start | bytes 3096584 | tf_op jit(solution)/shard_map/ppermute | solution.py:20
  141.4 3.0 %shard_map.116 = bf16[288,896]{1,0:T(8,128)(2,1)S(1)} custom-call(s32[5]{0:T(128)S(1)} %stack.47.ids, bf16[288,256]{1,0:T(8,128)(2,1)S(1)} %get-tuple-element.44.refs_0_, bf16[288,256]{1,0:T(8,128)(2,1)S(1)} %collective-permute-done.7.refs_1_, bf16[288,256]{1,0:T(8,128)(2,1)S(1)} %collective-permute-done.8.refs_2_, ...), custom_call_target="tpu_custom_call" | custom-call | flops 528482304 | bytes 6610944 | tf_op jit(solution)/shard_map/pallas_call | solution.py:214
  145.3 3.1 %collective-permute-done.12 = bf16[288,1792]{1,0:T(8,128)(2,1)} collective-permute-done((bf16[288,1792]{1,0:T(8,128)(2,1)}, bf16[288,1792]{1,0:T(8,128)(2,1)}, u32[]{:S(2)}, u32[]{:S(2)}) %collective-permute-start.12) | collective-permute-done | bytes 1032224 | tf_op jit(solution)/shard_map/ppermute | solution.py:24
  148.4 2.3 %broadcast_select_fusion.refs_1_ = bf16[288,1792]{1,0:T(8,128)(2,1)} fusion(bf16[288,1792]{1,0:T(8,128)(2,1)} %collective-permute-done.12, bf16[288,1792]{1,0:T(8,128)(2,1)} %collective-permute-done.2.mate_ref, pred[]{:T(512)S(6)} %ne.65), kind=kLoop, calls=%fused_computation.3 | loop fusion | flops 516096 | bytes 3096577 | tf_op jit(solution)/shard_map/jit(_where)/select_n | solution.py:296
  150.8 3.1 %collective-permute-start.16 = (bf16[288,1792]{1,0:T(8,128)(2,1)}, bf16[288,1792]{1,0:T(8,128)(2,1)}, u32[]{:S(2)}, u32[]{:S(2)}) collective-permute-start(bf16[288,1792]{1,0:T(8,128)(2,1)} %broadcast_select_fusion.refs_1_), channel_id=1, source_target_pairs={{0,192},{32,224},{64,0},{96,32},{128,64},{160,96},{192,128},{224,1... | collective-permute-start | bytes 3096584 | tf_op jit(solution)/shard_map/ppermute | solution.py:20
  154.0 3.0 %shard_map.117 = f32[288,896]{1,0:T(8,128)S(1)} custom-call(s32[5]{0:T(128)S(1)} %stack.47.ids, bf16[288,256]{1,0:T(8,128)(2,1)S(1)} %get-tuple-element.44.refs_0_, bf16[288,256]{1,0:T(8,128)(2,1)S(1)} %collective-permute-done.7.refs_1_, bf16[288,256]{1,0:T(8,128)(2,1)S(1)} %collective-permute-done.8.refs_2_, ...), custom_call_target="tpu_custom_call" | custom-call | flops 528482304 | bytes 7127040 | tf_op jit(solution)/shard_map/pallas_call | solution.py:214
  157.1 7.9 %collective-permute-done.13.refs_2_ = bf16[288,1792]{1,0:T(8,128)(2,1)S(1)} collective-permute-done((bf16[288,1792]{1,0:T(8,128)(2,1)S(1)}, bf16[288,1792]{1,0:T(8,128)(2,1)S(1)}, u32[]{:S(2)}, u32[]{:S(2)}) %collective-permute-start.13) | collective-permute-done | bytes 1032224 | tf_op jit(solution)/shard_map/ppermute | solution.py:20
  168.1 10.3 %all-to-all-start.2 = ((bf16[32,64,128]{2,1,0:T(8,128)(2,1)}), bf16[32,64,128]{2,1,0:T(8,128)(2,1)}, u32[]{:S(2)}, u32[]{:S(2)}) async-start(bf16[32,64,128]{2,1,0:T(8,128)(2,1)} %maximum_maximum_fusion), calls=%async_computation.2 | async-start | bytes 1048576 | tf_op jit(solution)/shard_map/all_to_all | solution.py:275
  178.5 4.0 %collective-permute-done.16.refs_5_ = bf16[288,1792]{1,0:T(8,128)(2,1)} collective-permute-done((bf16[288,1792]{1,0:T(8,128)(2,1)}, bf16[288,1792]{1,0:T(8,128)(2,1)}, u32[]{:S(2)}, u32[]{:S(2)}) %collective-permute-start.16) | collective-permute-done | bytes 1032224 | tf_op jit(solution)/shard_map/ppermute | solution.py:20
  182.5 3.7 %collective-permute-start.18 = (bf16[288,1792]{1,0:T(8,128)(2,1)}, bf16[288,1792]{1,0:T(8,128)(2,1)}, u32[]{:S(2)}, u32[]{:S(2)}) collective-permute-start(bf16[288,1792]{1,0:T(8,128)(2,1)} %collective-permute-done.16.refs_5_), channel_id=1, source_target_pairs={{0,192},{32,224},{64,0},{96,32},{128,64},{160,96},{192,128},{224,1... | collective-permute-start | bytes 3096584 | tf_op jit(solution)/shard_map/ppermute | solution.py:20
  187.2 8.5 %all-to-all-done.2 = bf16[32,64,128]{2,1,0:T(8,128)(2,1)} async-done(((bf16[32,64,128]{2,1,0:T(8,128)(2,1)}), bf16[32,64,128]{2,1,0:T(8,128)(2,1)}, u32[]{:S(2)}, u32[]{:S(2)}) %all-to-all-start.2) | async-done | bytes 524320 | tf_op jit(solution)/shard_map/all_to_all | solution.py:275
  199.4 5.0 %all-to-all-start.3 = ((bf16[8,16,896]{2,1,0:T(8,128)(2,1)}), bf16[8,16,896]{2,1,0:T(8,128)(2,1)}, u32[]{:S(2)}, u32[]{:S(2)}) async-start(bf16[8,16,896]{2,1,0:T(8,128)(2,1)} %bitcast.64), calls=%async_computation.3 | async-start | bytes 458752 | tf_op jit(solution)/shard_map/all_to_all | solution.py:315
  206.1 8.9 %shard_map.118 = (bf16[7168,128]{1,0:T(8,128)(2,1)}, bf16[7168,128]{1,0:T(8,128)(2,1)}, bf16[128,7168]{1,0:T(8,128)(2,1)}) custom-call(s32[9]{0:T(128)S(1)} %concatenate.15.ids, bf16[288,1792]{1,0:T(8,128)(2,1)S(1)} %copy-done.1, bf16[288,1792]{1,0:T(8,128)(2,1)} %broadcast_select_fusion.refs_1_, bf16[288,1792]{1,0:T(8,128)(2,1)S(1)} %copy-done.3, ...), custom_call_target="tpu_custom_call" | custom-call | flops 1585446912 | bytes 14204928 | tf_op jit(solution)/shard_map/pallas_call | solution.py:214
  (87 shorter events, 41.2 us)
Async XLA Ops:
  21.5 50.0 %all-to-all-start.1 = ((bf16[32,128,128]{2,1,0:T(8,128)(2,1)}), bf16[32,128,128]{2,1,0:T(8,128)(2,1)}, u32[]{:S(2)}, u32[]{:S(2)}) async-start(bf16[32,128,128]{2,1,0:T(8,128)(2,1)} %get-tuple-element.31), calls=%async_computation.1 | async-start | bytes 2097152 | tf_op jit(solution)/shard_map/all_to_all | solution.py:275
  37.7 32.2 %collective-permute-start = (bf16[5376,128]{1,0:T(8,128)(2,1)S(1)}, bf16[5376,128]{1,0:T(8,128)(2,1)S(1)}, u32[]{:S(2)}, u32[]{:S(2)}) collective-permute-start(bf16[5376,128]{1,0:T(8,128)(2,1)S(1)} %get-tuple-element.33), channel_id=1, source_target_pairs={{0,64},{32,96},{64,0},{96,32},{128,192},{160,224},{192,128},{224,1... | collective-permute-start | bytes 4128776 | tf_op jit(solution)/shard_map/ppermute | solution.py:24
  38.3 33.3 %collective-permute-start.1 = (bf16[5376,128]{1,0:T(8,128)(2,1)S(1)}, bf16[5376,128]{1,0:T(8,128)(2,1)}, u32[]{:S(2)}, u32[]{:S(2)}) collective-permute-start(bf16[5376,128]{1,0:T(8,128)(2,1)S(1)} %get-tuple-element.34), channel_id=1, source_target_pairs={{0,192},{32,224},{64,128},{96,160},{128,64},{160,96},{192,0},{224,... | collective-permute-start | bytes 4128776 | tf_op jit(solution)/shard_map/ppermute | solution.py:24
  75.0 24.0 %collective-permute-start.2 = (bf16[288,1792]{1,0:T(8,128)(2,1)}, bf16[288,1792]{1,0:T(8,128)(2,1)}, u32[]{:S(2)}, u32[]{:S(2)}) collective-permute-start(bf16[288,1792]{1,0:T(8,128)(2,1)} %pad_maximum_fusion.own_ref), channel_id=1, source_target_pairs={{0,32},{32,0},{64,96},{96,64},{128,160},{160,128},{192,224},{224,1... | collective-permute-start | bytes 3096584 | tf_op jit(solution)/shard_map/ppermute | solution.py:24
  76.0 32.4 %collective-permute-start.3 = (bf16[5376,128]{1,0:T(8,128)(2,1)S(1)}, bf16[5376,128]{1,0:T(8,128)(2,1)S(1)}, u32[]{:S(2)}, u32[]{:S(2)}) collective-permute-start(bf16[5376,128]{1,0:T(8,128)(2,1)S(1)} %copy-done.11), channel_id=1, source_target_pairs={{0,128},{32,160},{64,192},{96,224},{128,0},{160,32},{192,64},{224,... | collective-permute-start | bytes 4128776 | tf_op jit(solution)/shard_map/ppermute | solution.py:24
  99.1 37.5 %collective-permute-start.10 = (bf16[288,1792]{1,0:T(8,128)(2,1)}, bf16[288,1792]{1,0:T(8,128)(2,1)}, u32[]{:S(2)}, u32[]{:S(2)}) collective-permute-start(bf16[288,1792]{1,0:T(8,128)(2,1)} %pad_maximum_fusion.own_ref), channel_id=1, source_target_pairs={{0,16},{1,17},{2,18},{3,19},{4,20},{5,21},{6,22},{7,23},{8,24},{9,... | collective-permute-start | bytes 3096584 | tf_op jit(solution)/shard_map/ppermute | solution.py:24
  115.3 7.8 %collective-permute-start.4 = (bf16[288,384]{1,0:T(8,128)(2,1)S(1)}, bf16[288,384]{1,0:T(8,128)(2,1)S(1)}, u32[]{:S(2)}, u32[]{:S(2)}) collective-permute-start(bf16[288,384]{1,0:T(8,128)(2,1)S(1)} %get-tuple-element.39), channel_id=1, source_target_pairs={{0,64},{32,96},{64,0},{96,32},{128,192},{160,224},{192,128},{224,1... | collective-permute-start | bytes 663560 | tf_op jit(solution)/shard_map/ppermute | solution.py:24
  115.8 10.9 %collective-permute-start.5 = (bf16[288,384]{1,0:T(8,128)(2,1)S(1)}, bf16[288,384]{1,0:T(8,128)(2,1)S(1)}, u32[]{:S(2)}, u32[]{:S(2)}) collective-permute-start(bf16[288,384]{1,0:T(8,128)(2,1)S(1)} %get-tuple-element.40), channel_id=1, source_target_pairs={{0,192},{32,224},{64,128},{96,160},{128,64},{160,96},{192,0},{224,... | collective-permute-start | bytes 663560 | tf_op jit(solution)/shard_map/ppermute | solution.py:24
  116.8 9.9 %collective-permute-start.6 = (bf16[288,384]{1,0:T(8,128)(2,1)S(1)}, bf16[288,384]{1,0:T(8,128)(2,1)S(1)}, u32[]{:S(2)}, u32[]{:S(2)}) collective-permute-start(bf16[288,384]{1,0:T(8,128)(2,1)S(1)} %get-tuple-element.41), channel_id=1, source_target_pairs={{0,128},{32,160},{64,192},{96,224},{128,0},{160,32},{192,64},{224,... | collective-permute-start | bytes 663560 | tf_op jit(solution)/shard_map/ppermute | solution.py:24
  119.4 29.0 %collective-permute-start.12 = (bf16[288,1792]{1,0:T(8,128)(2,1)}, bf16[288,1792]{1,0:T(8,128)(2,1)}, u32[]{:S(2)}, u32[]{:S(2)}) collective-permute-start(bf16[288,1792]{1,0:T(8,128)(2,1)} %collective-permute-done.2.mate_ref), channel_id=1, source_target_pairs={{0,16},{1,17},{2,18},{3,19},{4,20},{5,21},{6,22},{7,23},{8,24},{9,... | collective-permute-start | bytes 3096584 | tf_op jit(solution)/shard_map/ppermute | solution.py:24
  127.6 5.4 %collective-permute-start.7 = (bf16[288,256]{1,0:T(8,128)(2,1)S(1)}, bf16[288,256]{1,0:T(8,128)(2,1)S(1)}, u32[]{:S(2)}, u32[]{:S(2)}) collective-permute-start(bf16[288,256]{1,0:T(8,128)(2,1)S(1)} %get-tuple-element.44.refs_0_), channel_id=1, source_target_pairs={{0,64},{32,96},{64,0},{96,32},{128,192},{160,224},{192,128},{224,1... | collective-permute-start | bytes 442376 | tf_op jit(solution)/shard_map/ppermute | solution.py:24
  128.2 6.4 %collective-permute-start.8 = (bf16[288,256]{1,0:T(8,128)(2,1)S(1)}, bf16[288,256]{1,0:T(8,128)(2,1)S(1)}, u32[]{:S(2)}, u32[]{:S(2)}) collective-permute-start(bf16[288,256]{1,0:T(8,128)(2,1)S(1)} %get-tuple-element.44.refs_0_), channel_id=1, source_target_pairs={{0,192},{32,224},{64,128},{96,160},{128,64},{160,96},{192,0},{224,... | collective-permute-start | bytes 442376 | tf_op jit(solution)/shard_map/ppermute | solution.py:24
  129.9 6.6 %collective-permute-start.9 = (bf16[288,256]{1,0:T(8,128)(2,1)S(1)}, bf16[288,256]{1,0:T(8,128)(2,1)S(1)}, u32[]{:S(2)}, u32[]{:S(2)}) collective-permute-start(bf16[288,256]{1,0:T(8,128)(2,1)S(1)} %get-tuple-element.44.refs_0_), channel_id=1, source_target_pairs={{0,128},{32,160},{64,192},{96,224},{128,0},{160,32},{192,64},{224,... | collective-permute-start | bytes 442376 | tf_op jit(solution)/shard_map/ppermute | solution.py:24
  138.0 27.0 %collective-permute-start.13 = (bf16[288,1792]{1,0:T(8,128)(2,1)S(1)}, bf16[288,1792]{1,0:T(8,128)(2,1)S(1)}, u32[]{:S(2)}, u32[]{:S(2)}) collective-permute-start(bf16[288,1792]{1,0:T(8,128)(2,1)S(1)} %broadcast_select_fusion.1.refs_0_), channel_id=1, source_target_pairs={{0,64},{32,96},{64,128},{96,160},{128,192},{160,224},{192,0},{224,... | collective-permute-start | bytes 3096584 | tf_op jit(solution)/shard_map/ppermute | solution.py:20
  138.5 26.5 %collective-permute-start.14 = (bf16[288,1792]{1,0:T(8,128)(2,1)S(1)}, bf16[288,1792]{1,0:T(8,128)(2,1)S(1)}, u32[]{:S(2)}, u32[]{:S(2)}) collective-permute-start(bf16[288,1792]{1,0:T(8,128)(2,1)S(1)} %broadcast_select_fusion.1.refs_0_), channel_id=1, source_target_pairs={{0,192},{32,224},{64,0},{96,32},{128,64},{160,96},{192,128},{224,1... | collective-permute-start | bytes 3096584 | tf_op jit(solution)/shard_map/ppermute | solution.py:20
  144.4 12.6 %collective-permute-start.11 = (bf16[288,896]{1,0:T(8,128)(2,1)S(1)}, bf16[288,896]{1,0:T(8,128)(2,1)S(1)}, u32[]{:S(2)}, u32[]{:S(2)}) collective-permute-start(bf16[288,896]{1,0:T(8,128)(2,1)S(1)} %shard_map.116), channel_id=1, source_target_pairs={{0,32},{32,0},{64,96},{96,64},{128,160},{160,128},{192,224},{224,1... | collective-permute-start | bytes 1548296 | tf_op jit(solution)/shard_map/ppermute | solution.py:24
  150.7 36.4 %collective-permute-start.15 = (bf16[288,1792]{1,0:T(8,128)(2,1)}, bf16[288,1792]{1,0:T(8,128)(2,1)}, u32[]{:S(2)}, u32[]{:S(2)}) collective-permute-start(bf16[288,1792]{1,0:T(8,128)(2,1)} %broadcast_select_fusion.refs_1_), channel_id=1, source_target_pairs={{0,64},{32,96},{64,128},{96,160},{128,192},{160,224},{192,0},{224,... | collective-permute-start | bytes 3096584 | tf_op jit(solution)/shard_map/ppermute | solution.py:20
  150.8 31.6 %collective-permute-start.16 = (bf16[288,1792]{1,0:T(8,128)(2,1)}, bf16[288,1792]{1,0:T(8,128)(2,1)}, u32[]{:S(2)}, u32[]{:S(2)}) collective-permute-start(bf16[288,1792]{1,0:T(8,128)(2,1)} %broadcast_select_fusion.refs_1_), channel_id=1, source_target_pairs={{0,192},{32,224},{64,0},{96,32},{128,64},{160,96},{192,128},{224,1... | collective-permute-start | bytes 3096584 | tf_op jit(solution)/shard_map/ppermute | solution.py:20
  168.1 38.0 %copy-start.5 = (bf16[288,1792]{1,0:T(8,128)(2,1)S(1)}, bf16[288,1792]{1,0:T(8,128)(2,1)}, u32[]{:S(2)}) copy-start(bf16[288,1792]{1,0:T(8,128)(2,1)} %copy-done.4) | copy-start | bytes 3096580
  168.1 27.6 %all-to-all-start.2 = ((bf16[32,64,128]{2,1,0:T(8,128)(2,1)}), bf16[32,64,128]{2,1,0:T(8,128)(2,1)}, u32[]{:S(2)}, u32[]{:S(2)}) async-start(bf16[32,64,128]{2,1,0:T(8,128)(2,1)} %maximum_maximum_fusion), calls=%async_computation.2 | async-start | bytes 1048576 | tf_op jit(solution)/shard_map/all_to_all | solution.py:275
  178.4 26.9 %collective-permute-start.17 = (bf16[288,1792]{1,0:T(8,128)(2,1)S(1)}, bf16[288,1792]{1,0:T(8,128)(2,1)}, u32[]{:S(2)}, u32[]{:S(2)}) collective-permute-start(bf16[288,1792]{1,0:T(8,128)(2,1)S(1)} %copy-done.3), channel_id=1, source_target_pairs={{0,64},{32,96},{64,128},{96,160},{128,192},{160,224},{192,0},{224,... | collective-permute-start | bytes 3096584 | tf_op jit(solution)/shard_map/ppermute | solution.py:20
  182.5 23.6 %collective-permute-start.18 = (bf16[288,1792]{1,0:T(8,128)(2,1)}, bf16[288,1792]{1,0:T(8,128)(2,1)}, u32[]{:S(2)}, u32[]{:S(2)}) collective-permute-start(bf16[288,1792]{1,0:T(8,128)(2,1)} %collective-permute-done.16.refs_5_), channel_id=1, source_target_pairs={{0,192},{32,224},{64,0},{96,32},{128,64},{160,96},{192,128},{224,1... | collective-permute-start | bytes 3096584 | tf_op jit(solution)/shard_map/ppermute | solution.py:20
  186.2 18.4 %collective-permute-start.19 = (bf16[288,384]{1,0:T(8,128)(2,1)S(1)}, bf16[288,384]{1,0:T(8,128)(2,1)S(1)}, u32[]{:S(2)}, u32[]{:S(2)}) collective-permute-start(bf16[288,384]{1,0:T(8,128)(2,1)S(1)} %copy-done.9), channel_id=1, source_target_pairs={{0,16},{1,17},{2,18},{3,19},{4,20},{5,21},{6,22},{7,23},{8,24},{9,... | collective-permute-start | bytes 663560 | tf_op jit(solution)/shard_map/ppermute | solution.py:24
  199.4 15.6 %all-to-all-start.3 = ((bf16[8,16,896]{2,1,0:T(8,128)(2,1)}), bf16[8,16,896]{2,1,0:T(8,128)(2,1)}, u32[]{:S(2)}, u32[]{:S(2)}) async-start(bf16[8,16,896]{2,1,0:T(8,128)(2,1)} %bitcast.64), calls=%async_computation.3 | async-start | bytes 458752 | tf_op jit(solution)/shard_map/all_to_all | solution.py:315
  (15 other events, 152.6 us)

commit v7 on v6

--- a/solution.py
+++ b/solution.py
@@ -10,6 +10,7 @@
 LANES = 128
 BF = jnp.bfloat16
 F32 = jnp.float32
+SPAN_HINT = 14 * 10**9
 
 
 def dot(a, b, dims):
@@ -47,14 +48,15 @@
 
 
 def block_kernel(ids, wg, wu, wd, *outs):
-    span = outs[0].shape[0] // 3
+    span = outs[0].shape[0]
+    unit = wg.shape[1]
     for k, out in enumerate(outs):
         start = pl.multiple_of(ids[k] * span, span)
-        out[:span, :] = wg[pl.ds(start, span), :]
-        out[span : 2 * span, :] = wu[pl.ds(start, span), :]
+        out[:, :unit] = wg[pl.ds(start, span), :]
+        out[:, unit : 2 * unit] = wu[pl.ds(start, span), :]
         for q in range(span // LANES):
             at = pl.ds(pl.multiple_of(start + q * LANES, LANES), LANES)
-            out[2 * span + q * LANES : 2 * span + (q + 1) * LANES, :] = wd[:, at]
+            out[q * LANES : (q + 1) * LANES, 2 * unit :] = wd[:, at]
 
 
 def route_kernel(n_tok, topk, rows_ref, out_ref, place_ref):
@@ -147,17 +149,17 @@
     mine = ids[ids.shape[0] - 1]
     for k in range(count):
         w, out_ref = refs[k::count]
-        span = w.shape[0] // 3
-        at = lambda which, base, n: pl.ds(pl.multiple_of(which * span + base, LANES), n)
-        gate = up = down = 0.0
+        unit = w.shape[1] // 3
+        both = down = 0.0
         for half, rows in ((mine, own_ref), (1 - mine, mate_ref)):
             base = half * part
-            gate += dot(rows[:, :part], w[at(0, base, part), :], ((1,), (0,)))
-            up += dot(rows[:, :part], w[at(1, base, part), :], ((1,), (0,)))
+            at = pl.ds(pl.multiple_of(base, part), part)
+            both += dot(rows[:, :part], w[at, : 2 * unit], ((1,), (0,)))
             for q in range(part // LANES):
                 cots = rows[:, part + q * LANES : part + (q + 1) * LANES]
-                down += dot(cots, w[at(2, base + q * LANES, LANES), :], ((1,), (1,)))
-        out_ref[...] = jnp.concatenate([gate, up, down], axis=1).astype(BF)
+                at = pl.ds(pl.multiple_of(base + q * LANES, LANES), LANES)
+                down += dot(cots, w[at, 2 * unit :], ((1,), (1,)))
+        out_ref[...] = jnp.concatenate([both, down], axis=1).astype(BF)
 
 
 def point_kernel(*refs):
@@ -179,14 +181,11 @@
     out_ref, acc = refs[-2:]
     count = len(refs) // 2 - 1
     part = out_ref.shape[1]
-    unit = refs[0].shape[1] // 2
     mine = ids[ids.shape[0] - 1]
-    base = (mine if which == 0 else 1 - mine) * part
+    at = pl.ds(pl.multiple_of((mine if which == 0 else 1 - mine) * part, part), part)
     for k in range(count):
         pair, w = refs[:-2][k::count]
-        at = lambda which: pl.ds(pl.multiple_of(which * (w.shape[0] // 3) + base, LANES), part)
-        total = dot(pair[:, :unit], w[at(0), :], ((1,), (1,)))
-        total += dot(pair[:, unit:], w[at(1), :], ((1,), (1,)))
+        total = dot(pair[...], w[at, : pair.shape[1]], ((1,), (1,)))
         if k == 0:
             acc[...] = total
         else:
@@ -266,16 +265,23 @@
 
     to_home, places = route(column)
 
-    cut = (jax.ShapeDtypeStruct((6 * part, hidden), BF),) * ring_len
-    sends = call(block_kernel, (after(sources, to_home),), (w_gate[0], w_up[0], w_down[0]), cut, 0)
-    arrive = lambda sent: [sent[0]] + [flip(b, "dp", k, groups) for k, b in zip(turns, sent[1:])]
-    blocks = arrive(sends)
+    cut = jax.ShapeDtypeStruct((2 * part, 3 * hidden), BF)
+    near = after(sources, column)
+    weights = (w_gate[0], w_up[0], w_down[0])
+    far = lambda b, k: flip(b, "dp", k, groups)
+    first = call(block_kernel, (near[1:3],), weights, (cut,) * 2, 0)
+    middle = [far(b, k) for k, b in zip(turns, first)]
+    rest = call(
+        block_kernel, (after(near, *middle)[:: ring_len - 1],), weights, (cut,) * 2, SPAN_HINT
+    )
+    blocks = [rest[0], *middle, far(rest[1], turns[-1])]
+    arrive = lambda sent: [sent[0]] + [far(b, k) for k, b in zip(turns, sent[1:])]
 
     def exchange(x):
         return lax.all_to_all(x, "expert", split_axis=0, concat_axis=0, tiled=True)
 
     arrived = exchange(to_home)
-    both = from_chunks(after(arrived, *blocks[1:3]), experts, low, 2 * parts)
+    both = from_chunks(after(arrived, *rest), experts, low, 2 * parts)
     mate_both = flip(both, "dp", 1, groups)
     unit = 2 * slot_count * width * hidden
     sums = call(

time: 218 us -> 215 us (0.986)
  blocking collectives: 14.3 us -> 0 us
  starting transfers between devices: 51.9 us -> 59.3 us
  local copies, waits for them, and re-layouts: 15.2 us -> 18.8 us
    ppermute x14, waiting for transfers between devices: 76.7 us -> 58.3 us  [flip(): return lax.ppermute(x, axis, [(i, i ^ bit) for i in range(size)])]
    all_to_all x1 -> x0, blocking collectives: 14.3 us -> none  [shards(): lax.all_to_all(packed, 'dp', split_axis=0, concat_axis=0, tiled=True)]
    all_to_all x0 -> x1, waiting for transfers between devices: none -> 8.48 us  [shards(): lax.all_to_all(packed, 'dp', split_axis=0, concat_axis=0, tiled=True)]
    all_to_all x0 -> x1, starting transfers between devices: none -> 5.93 us  [shards(): lax.all_to_all(packed, 'dp', split_axis=0, concat_axis=0, tiled=True)]
    all_to_all x2, waiting for transfers between devices: 8.49 us -> 13.1 us  [exchange(): return lax.all_to_all(x, 'expert', split_axis=0, concat_axis=0, tiled=True)]
    ppermute x14, starting transfers between devices: 14.6 us -> 18.5 us  [flip(): return lax.ppermute(x, axis, [(i, i ^ bit) for i in range(size)])]
    ppermute x6, waiting for transfers between devices: 13.4 us -> 16.7 us  [hop(): return lax.ppermute(x, axis, [(i, (i + step) % size) for i in range(size)])]
    unnamed x34 -> x50, local copies, waits for them, and re-layouts: 7.34 us -> 10.5 us
  transfers between devices with their start and end apart: 23 -> 24, of which waited for: 14 -> 17; matrix products, arithmetic and copies ran while one was open for 4% -> 5% of each run, Pallas kernels for 11% -> 10%
where the time goes in v7:
time: 215 us; the launch traced here: 212 us
  waiting for transfers between devices  96.6 us (45%)
  starting transfers between devices  59.3 us (28%)
  Pallas kernels  27.3 us (13%)
  local copies, waits for them, and re-layouts  18.8 us (9%)
  other arithmetic  6.71 us (3%)
    ppermute x14, waiting for transfers between devices, flip(): return lax.ppermute(x, axis, [(i, i ^ bit) for i in range(size)])  58.3 us
    pallas_call x9, Pallas kernels, call(): pl.pallas_call(kernel, out_shape=outs, in_specs=[pl.BlockSpec(memory_spac...  27.3 us
    all_to_all x2, starting transfers between devices, exchange(): return lax.all_to_all(x, 'expert', split_axis=0, concat_axis=0, tiled=True)  21.1 us
    ppermute x14, starting transfers between devices, flip(): return lax.ppermute(x, axis, [(i, i ^ bit) for i in range(size)])  18.5 us
    ppermute x6, waiting for transfers between devices, hop(): return lax.ppermute(x, axis, [(i, (i + step) % size) for i in range(size)])  16.7 us
    all_to_all x2, waiting for transfers between devices, exchange(): return lax.all_to_all(x, 'expert', split_axis=0, concat_axis=0, tiled=True)  13.1 us
    unnamed x50, local copies, waits for them, and re-layouts  10.5 us
    ppermute x6, starting transfers between devices, hop(): return lax.ppermute(x, axis, [(i, (i + step) % size) for i in range(size)])  8.72 us
  transfers between devices with their start and end apart: 24, of which 17 were waited for; matrix products, arithmetic and copies ran while one was open for 5% of the time, Pallas kernels for 10%

profile of v7, /device:TPU:6, one launch (start us, length us, event | category | flops | bytes accessed | tf_op | source)
XLA Modules:
  0.0 212.1 jit_solution(13441395016762636378)
XLA Ops:
  5.1 5.9 %all-to-all-start = ((bf16[8,16,1920]{2,1,0:T(8,128)(2,1)}), bf16[8,16,1920]{2,1,0:T(8,128)(2,1)S(1)}, u32[]{:S(2)}, u32[]{:S(2)}) async-start(bf16[8,16,1920]{2,1,0:T(8,128)(2,1)} %shard_map.111), calls=%async_computation | async-start | bytes 983040 | tf_op jit(solution)/shard_map/all_to_all | solution.py:251
  11.1 8.5 %all-to-all-done.rows_ref = bf16[8,16,1920]{2,1,0:T(8,128)(2,1)S(1)} async-done(((bf16[8,16,1920]{2,1,0:T(8,128)(2,1)}), bf16[8,16,1920]{2,1,0:T(8,128)(2,1)S(1)}, u32[]{:S(2)}, u32[]{:S(2)}) %all-to-all-start) | async-done | bytes 491552 | tf_op jit(solution)/shard_map/all_to_all | solution.py:251
  19.6 4.1 %shard_map.113 = (bf16[1792,384]{1,0:T(8,128)(2,1)}, bf16[1792,384]{1,0:T(8,128)(2,1)}) custom-call(s32[2]{0:T(128)S(1)} %slice.27.ids, bf16[7168,128]{1,0:T(8,128)(2,1)S(1)} %bitcast.55, bf16[7168,128]{1,0:T(8,128)(2,1)} %bitcast.59, bf16[128,7168]{1,0:T(8,128)(2,1)} %bitcast.61), custom_call_target="tpu_custom_call" | custom-call | bytes 8257536 | tf_op jit(solution)/shard_map/pallas_call | solution.py:213
  27.4 11.6 %all-to-all-start.1 = ((bf16[32,128,128]{2,1,0:T(8,128)(2,1)}), bf16[32,128,128]{2,1,0:T(8,128)(2,1)}, u32[]{:S(2)}, u32[]{:S(2)}) async-start(bf16[32,128,128]{2,1,0:T(8,128)(2,1)} %copy-done.9), calls=%async_computation.1 | async-start | bytes 2097152 | tf_op jit(solution)/shard_map/all_to_all | solution.py:281
  39.1 15.3 %collective-permute-done.refs_1_.refs_5_ = bf16[1792,384]{1,0:T(8,128)(2,1)S(1)} collective-permute-done((bf16[1792,384]{1,0:T(8,128)(2,1)}, bf16[1792,384]{1,0:T(8,128)(2,1)S(1)}, u32[]{:S(2)}, u32[]{:S(2)}) %collective-permute-start) | collective-permute-done | bytes 1376288 | tf_op jit(solution)/shard_map/ppermute | solution.py:25
  57.9 2.6 %shard_map.114 = (bf16[1792,384]{1,0:T(8,128)(2,1)S(1)}, bf16[1792,384]{1,0:T(8,128)(2,1)S(1)}) custom-call(s32[2]{0:T(128)S(1)} %slice.28.ids, bf16[7168,128]{1,0:T(8,128)(2,1)S(1)} %bitcast.56, bf16[7168,128]{1,0:T(8,128)(2,1)} %bitcast.60, bf16[128,7168]{1,0:T(8,128)(2,1)} %bitcast.62), custom_call_target="tpu_custom_call" | custom-call | flops 14000000000 | bytes 8257536 | tf_op jit(solution)/shard_map/pallas_call | solution.py:213
  62.7 3.7 %all-to-all-done.1 = bf16[32,128,128]{2,1,0:T(8,128)(2,1)} async-done(((bf16[32,128,128]{2,1,0:T(8,128)(2,1)}), bf16[32,128,128]{2,1,0:T(8,128)(2,1)}, u32[]{:S(2)}, u32[]{:S(2)}) %all-to-all-start.1) | async-done | bytes 1048608 | tf_op jit(solution)/shard_map/all_to_all | solution.py:281
  71.3 2.7 %collective-permute-start.3 = (bf16[1792,384]{1,0:T(8,128)(2,1)S(1)}, bf16[1792,384]{1,0:T(8,128)(2,1)S(1)}, u32[]{:S(2)}, u32[]{:S(2)}) collective-permute-start(bf16[1792,384]{1,0:T(8,128)(2,1)S(1)} %copy-done.19), channel_id=1, source_target_pairs={{0,128},{32,160},{64,192},{96,224},{128,0},{160,32},{192,64},{224,... | collective-permute-start | bytes 4128776 | tf_op jit(solution)/shard_map/ppermute | solution.py:25
  74.0 20.3 %collective-permute-done.2.mate_ref = bf16[288,1792]{1,0:T(8,128)(2,1)} collective-permute-done((bf16[288,1792]{1,0:T(8,128)(2,1)}, bf16[288,1792]{1,0:T(8,128)(2,1)}, u32[]{:S(2)}, u32[]{:S(2)}) %collective-permute-start.2) | collective-permute-done | bytes 1032224 | tf_op jit(solution)/shard_map/ppermute | solution.py:25
  96.2 7.8 %collective-permute-done.3.refs_3_.refs_7_ = bf16[1792,384]{1,0:T(8,128)(2,1)S(1)} collective-permute-done((bf16[1792,384]{1,0:T(8,128)(2,1)S(1)}, bf16[1792,384]{1,0:T(8,128)(2,1)S(1)}, u32[]{:S(2)}, u32[]{:S(2)}) %collective-permute-start.3) | collective-permute-done | bytes 1376288 | tf_op jit(solution)/shard_map/ppermute | solution.py:25
  105.1 4.8 %shard_map.115 = (bf16[288,384]{1,0:T(8,128)(2,1)S(1)}, bf16[288,384]{1,0:T(8,128)(2,1)S(1)}, bf16[288,384]{1,0:T(8,128)(2,1)S(1)}, bf16[288,384]{1,0:T(8,128)(2,1)S(1)}) custom-call(s32[5]{0:T(128)S(1)} %stack.47.ids, bf16[288,1792]{1,0:T(8,128)(2,1)} %pad_maximum_fusion.own_ref, bf16[288,1792]{1,0:T(8,128)(2,1)} %collective-permute-done.2.mate_ref, ...), custom_call_target="tpu_custom_call" | custom-call | flops 1585446912 | bytes 8454144 | tf_op jit(solution)/shard_map/pallas_call | solution.py:213
  110.9 2.4 %collective-permute-start.5 = (bf16[288,384]{1,0:T(8,128)(2,1)S(1)}, bf16[288,384]{1,0:T(8,128)(2,1)S(1)}, u32[]{:S(2)}, u32[]{:S(2)}) collective-permute-start(bf16[288,384]{1,0:T(8,128)(2,1)S(1)} %get-tuple-element.42), channel_id=1, source_target_pairs={{0,192},{32,224},{64,128},{96,160},{128,64},{160,96},{192,0},{224,... | collective-permute-start | bytes 663560 | tf_op jit(solution)/shard_map/ppermute | solution.py:25
  114.1 2.2 %collective-permute-start.12 = (bf16[288,1792]{1,0:T(8,128)(2,1)}, bf16[288,1792]{1,0:T(8,128)(2,1)}, u32[]{:S(2)}, u32[]{:S(2)}) collective-permute-start(bf16[288,1792]{1,0:T(8,128)(2,1)} %collective-permute-done.2.mate_ref), channel_id=1, source_target_pairs={{0,16},{1,17},{2,18},{3,19},{4,20},{5,21},{6,22},{7,23},{8,24},{9,... | collective-permute-start | bytes 3096584 | tf_op jit(solution)/shard_map/ppermute | solution.py:25
  118.0 4.5 %collective-permute-done.5.refs_2_ = bf16[288,384]{1,0:T(8,128)(2,1)S(1)} collective-permute-done((bf16[288,384]{1,0:T(8,128)(2,1)S(1)}, bf16[288,384]{1,0:T(8,128)(2,1)S(1)}, u32[]{:S(2)}, u32[]{:S(2)}) %collective-permute-start.5) | collective-permute-done | bytes 221216 | tf_op jit(solution)/shard_map/ppermute | solution.py:25
  129.7 2.4 %collective-permute-done.9.refs_3_ = bf16[288,256]{1,0:T(8,128)(2,1)S(1)} collective-permute-done((bf16[288,256]{1,0:T(8,128)(2,1)S(1)}, bf16[288,256]{1,0:T(8,128)(2,1)S(1)}, u32[]{:S(2)}, u32[]{:S(2)}) %collective-permute-start.9) | collective-permute-done | bytes 147488 | tf_op jit(solution)/shard_map/ppermute | solution.py:25
  136.9 2.2 %shard_map.117 = bf16[288,896]{1,0:T(8,128)(2,1)S(1)} custom-call(s32[5]{0:T(128)S(1)} %stack.47.ids, bf16[288,256]{1,0:T(8,128)(2,1)S(1)} %get-tuple-element.46.refs_0_, bf16[288,256]{1,0:T(8,128)(2,1)S(1)} %collective-permute-done.7.refs_1_, bf16[288,256]{1,0:T(8,128)(2,1)S(1)} %collective-permute-done.8.refs_2_, ...), custom_call_target="tpu_custom_call" | custom-call | flops 528482304 | bytes 6610944 | tf_op jit(solution)/shard_map/pallas_call | solution.py:213
  140.0 4.0 %collective-permute-done.12 = bf16[288,1792]{1,0:T(8,128)(2,1)} collective-permute-done((bf16[288,1792]{1,0:T(8,128)(2,1)}, bf16[288,1792]{1,0:T(8,128)(2,1)}, u32[]{:S(2)}, u32[]{:S(2)}) %collective-permute-start.12) | collective-permute-done | bytes 1032224 | tf_op jit(solution)/shard_map/ppermute | solution.py:25
  144.0 2.3 %broadcast_select_fusion.refs_1_ = bf16[288,1792]{1,0:T(8,128)(2,1)} fusion(bf16[288,1792]{1,0:T(8,128)(2,1)} %collective-permute-done.12, bf16[288,1792]{1,0:T(8,128)(2,1)} %collective-permute-done.2.mate_ref, pred[]{:T(512)S(6)} %ne.65), kind=kLoop, calls=%fused_computation.3 | loop fusion | flops 516096 | bytes 3096577 | tf_op jit(solution)/shard_map/jit(_where)/select_n | solution.py:302
  151.9 8.7 %collective-permute-done.13.refs_2_ = bf16[288,1792]{1,0:T(8,128)(2,1)S(1)} collective-permute-done((bf16[288,1792]{1,0:T(8,128)(2,1)S(1)}, bf16[288,1792]{1,0:T(8,128)(2,1)S(1)}, u32[]{:S(2)}, u32[]{:S(2)}) %collective-permute-start.13) | collective-permute-done | bytes 1032224 | tf_op jit(solution)/shard_map/ppermute | solution.py:21
  163.6 9.5 %all-to-all-start.2 = ((bf16[32,64,128]{2,1,0:T(8,128)(2,1)}), bf16[32,64,128]{2,1,0:T(8,128)(2,1)}, u32[]{:S(2)}, u32[]{:S(2)}) async-start(bf16[32,64,128]{2,1,0:T(8,128)(2,1)} %maximum_maximum_fusion), calls=%async_computation.2 | async-start | bytes 1048576 | tf_op jit(solution)/shard_map/all_to_all | solution.py:281
  173.2 5.6 %collective-permute-done.16.refs_5_ = bf16[288,1792]{1,0:T(8,128)(2,1)} collective-permute-done((bf16[288,1792]{1,0:T(8,128)(2,1)}, bf16[288,1792]{1,0:T(8,128)(2,1)}, u32[]{:S(2)}, u32[]{:S(2)}) %collective-permute-start.16) | collective-permute-done | bytes 1032224 | tf_op jit(solution)/shard_map/ppermute | solution.py:21
  181.0 9.4 %all-to-all-done.2 = bf16[32,64,128]{2,1,0:T(8,128)(2,1)} async-done(((bf16[32,64,128]{2,1,0:T(8,128)(2,1)}), bf16[32,64,128]{2,1,0:T(8,128)(2,1)}, u32[]{:S(2)}, u32[]{:S(2)}) %all-to-all-start.2) | async-done | bytes 524320 | tf_op jit(solution)/shard_map/all_to_all | solution.py:281
  194.2 5.0 %all-to-all-start.3 = ((bf16[8,16,896]{2,1,0:T(8,128)(2,1)}), bf16[8,16,896]{2,1,0:T(8,128)(2,1)}, u32[]{:S(2)}, u32[]{:S(2)}) async-start(bf16[8,16,896]{2,1,0:T(8,128)(2,1)} %bitcast.67), calls=%async_computation.3 | async-start | bytes 458752 | tf_op jit(solution)/shard_map/all_to_all | solution.py:321
  201.4 8.9 %shard_map.119 = (bf16[7168,128]{1,0:T(8,128)(2,1)}, bf16[7168,128]{1,0:T(8,128)(2,1)}, bf16[128,7168]{1,0:T(8,128)(2,1)}) custom-call(s32[9]{0:T(128)S(1)} %concatenate.15.ids, bf16[288,1792]{1,0:T(8,128)(2,1)S(1)} %copy-done.6, bf16[288,1792]{1,0:T(8,128)(2,1)} %broadcast_select_fusion.refs_1_, bf16[288,1792]{1,0:T(8,128)(2,1)S(1)} %copy-done.11, ...), custom_call_target="tpu_custom_call" | custom-call | flops 1585446912 | bytes 14204928 | tf_op jit(solution)/shard_map/pallas_call | solution.py:213
  (107 shorter events, 56.1 us)
Async XLA Ops:
  5.1 14.5 %all-to-all-start = ((bf16[8,16,1920]{2,1,0:T(8,128)(2,1)}), bf16[8,16,1920]{2,1,0:T(8,128)(2,1)S(1)}, u32[]{:S(2)}, u32[]{:S(2)}) async-start(bf16[8,16,1920]{2,1,0:T(8,128)(2,1)} %shard_map.111), calls=%async_computation | async-start | bytes 983040 | tf_op jit(solution)/shard_map/all_to_all | solution.py:251
  23.8 30.6 %collective-permute-start = (bf16[1792,384]{1,0:T(8,128)(2,1)}, bf16[1792,384]{1,0:T(8,128)(2,1)S(1)}, u32[]{:S(2)}, u32[]{:S(2)}) collective-permute-start(bf16[1792,384]{1,0:T(8,128)(2,1)} %get-tuple-element.34), channel_id=1, source_target_pairs={{0,64},{32,96},{64,0},{96,32},{128,192},{160,224},{192,128},{224,1... | collective-permute-start | bytes 4128776 | tf_op jit(solution)/shard_map/ppermute | solution.py:25
  24.3 31.6 %collective-permute-start.1 = (bf16[1792,384]{1,0:T(8,128)(2,1)}, bf16[1792,384]{1,0:T(8,128)(2,1)S(1)}, u32[]{:S(2)}, u32[]{:S(2)}) collective-permute-start(bf16[1792,384]{1,0:T(8,128)(2,1)} %get-tuple-element.35), channel_id=1, source_target_pairs={{0,192},{32,224},{64,128},{96,160},{128,64},{160,96},{192,0},{224,... | collective-permute-start | bytes 4128776 | tf_op jit(solution)/shard_map/ppermute | solution.py:25
  27.4 39.0 %all-to-all-start.1 = ((bf16[32,128,128]{2,1,0:T(8,128)(2,1)}), bf16[32,128,128]{2,1,0:T(8,128)(2,1)}, u32[]{:S(2)}, u32[]{:S(2)}) async-start(bf16[32,128,128]{2,1,0:T(8,128)(2,1)} %copy-done.9), calls=%async_computation.1 | async-start | bytes 2097152 | tf_op jit(solution)/shard_map/all_to_all | solution.py:281
  69.9 24.4 %collective-permute-start.2 = (bf16[288,1792]{1,0:T(8,128)(2,1)}, bf16[288,1792]{1,0:T(8,128)(2,1)}, u32[]{:S(2)}, u32[]{:S(2)}) collective-permute-start(bf16[288,1792]{1,0:T(8,128)(2,1)} %pad_maximum_fusion.own_ref), channel_id=1, source_target_pairs={{0,32},{32,0},{64,96},{96,64},{128,160},{160,128},{192,224},{224,1... | collective-permute-start | bytes 3096584 | tf_op jit(solution)/shard_map/ppermute | solution.py:25
  71.3 32.7 %collective-permute-start.3 = (bf16[1792,384]{1,0:T(8,128)(2,1)S(1)}, bf16[1792,384]{1,0:T(8,128)(2,1)S(1)}, u32[]{:S(2)}, u32[]{:S(2)}) collective-permute-start(bf16[1792,384]{1,0:T(8,128)(2,1)S(1)} %copy-done.19), channel_id=1, source_target_pairs={{0,128},{32,160},{64,192},{96,224},{128,0},{160,32},{192,64},{224,... | collective-permute-start | bytes 4128776 | tf_op jit(solution)/shard_map/ppermute | solution.py:25
  94.3 37.8 %collective-permute-start.10 = (bf16[288,1792]{1,0:T(8,128)(2,1)}, bf16[288,1792]{1,0:T(8,128)(2,1)}, u32[]{:S(2)}, u32[]{:S(2)}) collective-permute-start(bf16[288,1792]{1,0:T(8,128)(2,1)} %pad_maximum_fusion.own_ref), channel_id=1, source_target_pairs={{0,16},{1,17},{2,18},{3,19},{4,20},{5,21},{6,22},{7,23},{8,24},{9,... | collective-permute-start | bytes 3096584 | tf_op jit(solution)/shard_map/ppermute | solution.py:25
  109.9 8.1 %collective-permute-start.4 = (bf16[288,384]{1,0:T(8,128)(2,1)S(1)}, bf16[288,384]{1,0:T(8,128)(2,1)S(1)}, u32[]{:S(2)}, u32[]{:S(2)}) collective-permute-start(bf16[288,384]{1,0:T(8,128)(2,1)S(1)} %get-tuple-element.41), channel_id=1, source_target_pairs={{0,64},{32,96},{64,0},{96,32},{128,192},{160,224},{192,128},{224,1... | collective-permute-start | bytes 663560 | tf_op jit(solution)/shard_map/ppermute | solution.py:25
  110.9 11.6 %collective-permute-start.5 = (bf16[288,384]{1,0:T(8,128)(2,1)S(1)}, bf16[288,384]{1,0:T(8,128)(2,1)S(1)}, u32[]{:S(2)}, u32[]{:S(2)}) collective-permute-start(bf16[288,384]{1,0:T(8,128)(2,1)S(1)} %get-tuple-element.42), channel_id=1, source_target_pairs={{0,192},{32,224},{64,128},{96,160},{128,64},{160,96},{192,0},{224,... | collective-permute-start | bytes 663560 | tf_op jit(solution)/shard_map/ppermute | solution.py:25
  113.3 9.2 %collective-permute-start.6 = (bf16[288,384]{1,0:T(8,128)(2,1)S(1)}, bf16[288,384]{1,0:T(8,128)(2,1)S(1)}, u32[]{:S(2)}, u32[]{:S(2)}) collective-permute-start(bf16[288,384]{1,0:T(8,128)(2,1)S(1)} %get-tuple-element.43), channel_id=1, source_target_pairs={{0,128},{32,160},{64,192},{96,224},{128,0},{160,32},{192,64},{224,... | collective-permute-start | bytes 663560 | tf_op jit(solution)/shard_map/ppermute | solution.py:25
  114.1 29.9 %collective-permute-start.12 = (bf16[288,1792]{1,0:T(8,128)(2,1)}, bf16[288,1792]{1,0:T(8,128)(2,1)}, u32[]{:S(2)}, u32[]{:S(2)}) collective-permute-start(bf16[288,1792]{1,0:T(8,128)(2,1)} %collective-permute-done.2.mate_ref), channel_id=1, source_target_pairs={{0,16},{1,17},{2,18},{3,19},{4,20},{5,21},{6,22},{7,23},{8,24},{9,... | collective-permute-start | bytes 3096584 | tf_op jit(solution)/shard_map/ppermute | solution.py:25
  123.4 5.5 %collective-permute-start.7 = (bf16[288,256]{1,0:T(8,128)(2,1)S(1)}, bf16[288,256]{1,0:T(8,128)(2,1)S(1)}, u32[]{:S(2)}, u32[]{:S(2)}) collective-permute-start(bf16[288,256]{1,0:T(8,128)(2,1)S(1)} %get-tuple-element.46.refs_0_), channel_id=1, source_target_pairs={{0,64},{32,96},{64,0},{96,32},{128,192},{160,224},{192,128},{224,1... | collective-permute-start | bytes 442376 | tf_op jit(solution)/shard_map/ppermute | solution.py:25
  123.4 6.4 %collective-permute-start.8 = (bf16[288,256]{1,0:T(8,128)(2,1)S(1)}, bf16[288,256]{1,0:T(8,128)(2,1)S(1)}, u32[]{:S(2)}, u32[]{:S(2)}) collective-permute-start(bf16[288,256]{1,0:T(8,128)(2,1)S(1)} %get-tuple-element.46.refs_0_), channel_id=1, source_target_pairs={{0,192},{32,224},{64,128},{96,160},{128,64},{160,96},{192,0},{224,... | collective-permute-start | bytes 442376 | tf_op jit(solution)/shard_map/ppermute | solution.py:25
  125.4 6.6 %collective-permute-start.9 = (bf16[288,256]{1,0:T(8,128)(2,1)S(1)}, bf16[288,256]{1,0:T(8,128)(2,1)S(1)}, u32[]{:S(2)}, u32[]{:S(2)}) collective-permute-start(bf16[288,256]{1,0:T(8,128)(2,1)S(1)} %get-tuple-element.46.refs_0_), channel_id=1, source_target_pairs={{0,128},{32,160},{64,192},{96,224},{128,0},{160,32},{192,64},{224,... | collective-permute-start | bytes 442376 | tf_op jit(solution)/shard_map/ppermute | solution.py:25
  133.5 27.0 %collective-permute-start.13 = (bf16[288,1792]{1,0:T(8,128)(2,1)S(1)}, bf16[288,1792]{1,0:T(8,128)(2,1)S(1)}, u32[]{:S(2)}, u32[]{:S(2)}) collective-permute-start(bf16[288,1792]{1,0:T(8,128)(2,1)S(1)} %broadcast_select_fusion.1.refs_0_), channel_id=1, source_target_pairs={{0,64},{32,96},{64,128},{96,160},{128,192},{160,224},{192,0},{224,... | collective-permute-start | bytes 3096584 | tf_op jit(solution)/shard_map/ppermute | solution.py:21
  135.0 25.7 %collective-permute-start.14 = (bf16[288,1792]{1,0:T(8,128)(2,1)S(1)}, bf16[288,1792]{1,0:T(8,128)(2,1)S(1)}, u32[]{:S(2)}, u32[]{:S(2)}) collective-permute-start(bf16[288,1792]{1,0:T(8,128)(2,1)S(1)} %broadcast_select_fusion.1.refs_0_), channel_id=1, source_target_pairs={{0,192},{32,224},{64,0},{96,32},{128,64},{160,96},{192,128},{224,1... | collective-permute-start | bytes 3096584 | tf_op jit(solution)/shard_map/ppermute | solution.py:21
  139.1 12.6 %collective-permute-start.11 = (bf16[288,896]{1,0:T(8,128)(2,1)S(1)}, bf16[288,896]{1,0:T(8,128)(2,1)S(1)}, u32[]{:S(2)}, u32[]{:S(2)}) collective-permute-start(bf16[288,896]{1,0:T(8,128)(2,1)S(1)} %shard_map.117), channel_id=1, source_target_pairs={{0,32},{32,0},{64,96},{96,64},{128,160},{160,128},{192,224},{224,1... | collective-permute-start | bytes 1548296 | tf_op jit(solution)/shard_map/ppermute | solution.py:25
  146.3 34.6 %collective-permute-start.15 = (bf16[288,1792]{1,0:T(8,128)(2,1)}, bf16[288,1792]{1,0:T(8,128)(2,1)}, u32[]{:S(2)}, u32[]{:S(2)}) collective-permute-start(bf16[288,1792]{1,0:T(8,128)(2,1)} %broadcast_select_fusion.refs_1_), channel_id=1, source_target_pairs={{0,64},{32,96},{64,128},{96,160},{128,192},{160,224},{192,0},{224,... | collective-permute-start | bytes 3096584 | tf_op jit(solution)/shard_map/ppermute | solution.py:21
  147.7 31.1 %collective-permute-start.16 = (bf16[288,1792]{1,0:T(8,128)(2,1)}, bf16[288,1792]{1,0:T(8,128)(2,1)}, u32[]{:S(2)}, u32[]{:S(2)}) collective-permute-start(bf16[288,1792]{1,0:T(8,128)(2,1)} %broadcast_select_fusion.refs_1_), channel_id=1, source_target_pairs={{0,192},{32,224},{64,0},{96,32},{128,64},{160,96},{192,128},{224,1... | collective-permute-start | bytes 3096584 | tf_op jit(solution)/shard_map/ppermute | solution.py:21
  163.6 26.7 %all-to-all-start.2 = ((bf16[32,64,128]{2,1,0:T(8,128)(2,1)}), bf16[32,64,128]{2,1,0:T(8,128)(2,1)}, u32[]{:S(2)}, u32[]{:S(2)}) async-start(bf16[32,64,128]{2,1,0:T(8,128)(2,1)} %maximum_maximum_fusion), calls=%async_computation.2 | async-start | bytes 1048576 | tf_op jit(solution)/shard_map/all_to_all | solution.py:281
  173.1 26.8 %collective-permute-start.17 = (bf16[288,1792]{1,0:T(8,128)(2,1)S(1)}, bf16[288,1792]{1,0:T(8,128)(2,1)}, u32[]{:S(2)}, u32[]{:S(2)}) collective-permute-start(bf16[288,1792]{1,0:T(8,128)(2,1)S(1)} %copy-done.11), channel_id=1, source_target_pairs={{0,64},{32,96},{64,128},{96,160},{128,192},{160,224},{192,0},{224,... | collective-permute-start | bytes 3096584 | tf_op jit(solution)/shard_map/ppermute | solution.py:21
  178.9 22.6 %collective-permute-start.18 = (bf16[288,1792]{1,0:T(8,128)(2,1)}, bf16[288,1792]{1,0:T(8,128)(2,1)}, u32[]{:S(2)}, u32[]{:S(2)}) collective-permute-start(bf16[288,1792]{1,0:T(8,128)(2,1)} %collective-permute-done.16.refs_5_), channel_id=1, source_target_pairs={{0,192},{32,224},{64,0},{96,32},{128,64},{160,96},{192,128},{224,1... | collective-permute-start | bytes 3096584 | tf_op jit(solution)/shard_map/ppermute | solution.py:21
  181.0 18.3 %collective-permute-start.19 = (bf16[288,384]{1,0:T(8,128)(2,1)S(1)}, bf16[288,384]{1,0:T(8,128)(2,1)S(1)}, u32[]{:S(2)}, u32[]{:S(2)}) collective-permute-start(bf16[288,384]{1,0:T(8,128)(2,1)S(1)} %copy-done.17), channel_id=1, source_target_pairs={{0,16},{1,17},{2,18},{3,19},{4,20},{5,21},{6,22},{7,23},{8,24},{9,... | collective-permute-start | bytes 663560 | tf_op jit(solution)/shard_map/ppermute | solution.py:25
  194.2 16.1 %all-to-all-start.3 = ((bf16[8,16,896]{2,1,0:T(8,128)(2,1)}), bf16[8,16,896]{2,1,0:T(8,128)(2,1)}, u32[]{:S(2)}, u32[]{:S(2)}) async-start(bf16[8,16,896]{2,1,0:T(8,128)(2,1)} %bitcast.67), calls=%async_computation.3 | async-start | bytes 458752 | tf_op jit(solution)/shard_map/all_to_all | solution.py:321
  (24 other events, 337.5 us)

commit v8 on v7

--- a/solution.py
+++ b/solution.py
@@ -50,13 +50,14 @@
 def block_kernel(ids, wg, wu, wd, *outs):
     span = outs[0].shape[0]
     unit = wg.shape[1]
-    for k, out in enumerate(outs):
+    for k, out in enumerate(outs[: ids.shape[0]]):
         start = pl.multiple_of(ids[k] * span, span)
         out[:, :unit] = wg[pl.ds(start, span), :]
         out[:, unit : 2 * unit] = wu[pl.ds(start, span), :]
+        down, base = (out, 2 * unit) if out.shape[1] > 2 * unit else (outs[-1], 0)
         for q in range(span // LANES):
             at = pl.ds(pl.multiple_of(start + q * LANES, LANES), LANES)
-            out[q * LANES : (q + 1) * LANES, 2 * unit :] = wd[:, at]
+            down[q * LANES : (q + 1) * LANES, base : base + unit] = wd[:, at]
 
 
 def route_kernel(n_tok, topk, rows_ref, out_ref, place_ref):
@@ -145,11 +146,13 @@
 
 def partial_kernel(ids, own_ref, mate_ref, *refs):
     count = len(refs) // 2
+    blocks, last, outs = refs[:count], refs[count], refs[count + 1 :]
     part = own_ref.shape[1] // 2
     mine = ids[ids.shape[0] - 1]
     for k in range(count):
-        w, out_ref = refs[k::count]
-        unit = w.shape[1] // 3
+        w, out_ref = blocks[k], outs[k]
+        unit = last.shape[1]
+        wd, first = (w, 2 * unit) if w.shape[1] > 2 * unit else (last, 0)
         both = down = 0.0
         for half, rows in ((mine, own_ref), (1 - mine, mate_ref)):
             base = half * part
@@ -158,7 +161,7 @@
             for q in range(part // LANES):
                 cots = rows[:, part + q * LANES : part + (q + 1) * LANES]
                 at = pl.ds(pl.multiple_of(base + q * LANES, LANES), LANES)
-                down += dot(cots, w[at, 2 * unit :], ((1,), (1,)))
+                down += dot(cots, wd[at, first : first + unit], ((1,), (1,)))
         out_ref[...] = jnp.concatenate([both, down], axis=1).astype(BF)
 
 
@@ -272,20 +275,22 @@
     first = call(block_kernel, (near[1:3],), weights, (cut,) * 2, 0)
     middle = [far(b, k) for k, b in zip(turns, first)]
     rest = call(
-        block_kernel, (after(near, *middle)[:: ring_len - 1],), weights, (cut,) * 2, SPAN_HINT
+        block_kernel, (after(near, *middle)[:: ring_len - 1],), weights,
+        (cut, *(jax.ShapeDtypeStruct((2 * part, n * hidden), BF) for n in (2, 1))), SPAN_HINT,
     )
     blocks = [rest[0], *middle, far(rest[1], turns[-1])]
+    last = far(rest[2], turns[-1])
     arrive = lambda sent: [sent[0]] + [far(b, k) for k, b in zip(turns, sent[1:])]
 
     def exchange(x):
         return lax.all_to_all(x, "expert", split_axis=0, concat_axis=0, tiled=True)
 
     arrived = exchange(to_home)
-    both = from_chunks(after(arrived, *rest), experts, low, 2 * parts)
+    both = from_chunks(after(arrived, last, *rest), experts, low, 2 * parts)
     mate_both = flip(both, "dp", 1, groups)
     unit = 2 * slot_count * width * hidden
     sums = call(
-        partial_kernel, (sources,), (both, mate_both, *blocks),
+        partial_kernel, (sources,), (both, mate_both, *blocks, last),
         (jax.ShapeDtypeStruct((slot_count, 3 * hidden), BF),) * ring_len, 3 * unit,
     )
     sums = arrive(sums)

time: 215 us -> 213 us (level)
  starting transfers between devices: 59.3 us -> 66.8 us
  waiting for transfers between devices: 96.6 us -> 89.2 us
    ppermute x6, waiting for transfers between devices: 16.7 us -> 2.14 us  [hop(): return lax.ppermute(x, axis, [(i, (i + step) % size) for i in range(size)])]
    ppermute x14 -> x15, waiting for transfers between devices: 58.3 us -> 66.7 us  [flip(): return lax.ppermute(x, axis, [(i, i ^ bit) for i in range(size)])]
    all_to_all x2, starting transfers between devices: 21.1 us -> 24.4 us  [exchange(): return lax.all_to_all(x, 'expert', split_axis=0, concat_axis=0, tiled=True)]
    ppermute x14 -> x15, starting transfers between devices: 18.5 us -> 21.6 us  [flip(): return lax.ppermute(x, axis, [(i, i ^ bit) for i in range(size)])]
    unnamed x50 -> x56, local copies, waits for them, and re-layouts: 10.5 us -> 12 us
  transfers between devices with their start and end apart: 24 -> 25, of which waited for: 17 -> 12; matrix products, arithmetic and copies ran while one was open for 5% -> 4% of each run, Pallas kernels for 10% -> 10%
where the time goes in v8:
time: 213 us; the launch traced here: 211 us
  waiting for transfers between devices  89.2 us (42%)
  starting transfers between devices  66.8 us (31%)
  Pallas kernels  26.5 us (12%)
  local copies, waits for them, and re-layouts  20.2 us (9%)
  other arithmetic  6.04 us (3%)
    ppermute x15, waiting for transfers between devices, flip(): return lax.ppermute(x, axis, [(i, i ^ bit) for i in range(size)])  66.7 us
    pallas_call x9, Pallas kernels, call(): pl.pallas_call(kernel, out_shape=outs, in_specs=[pl.BlockSpec(memory_spac...  26.5 us
    all_to_all x2, starting transfers between devices, exchange(): return lax.all_to_all(x, 'expert', split_axis=0, concat_axis=0, tiled=True)  24.4 us
    ppermute x15, starting transfers between devices, flip(): return lax.ppermute(x, axis, [(i, i ^ bit) for i in range(size)])  21.6 us
    unnamed x56, local copies, waits for them, and re-layouts  12 us
    all_to_all x2, waiting for transfers between devices, exchange(): return lax.all_to_all(x, 'expert', split_axis=0, concat_axis=0, tiled=True)  11.8 us
    ppermute x6, starting transfers between devices, hop(): return lax.ppermute(x, axis, [(i, (i + step) % size) for i in range(size)])  9.92 us
    all_to_all x1, waiting for transfers between devices, shards(): lax.all_to_all(packed, 'dp', split_axis=0, concat_axis=0, tiled=True)  8.48 us
  transfers between devices with their start and end apart: 25, of which 12 were waited for; matrix products, arithmetic and copies ran while one was open for 4% of the time, Pallas kernels for 10%

profile of v8, /device:TPU:6, one launch (start us, length us, event | category | flops | bytes accessed | tf_op | source)
XLA Modules:
  0.0 211.3 jit_solution(13780351412834899734)
XLA Ops:
  5.1 5.9 %all-to-all-start = ((bf16[8,16,1920]{2,1,0:T(8,128)(2,1)}), bf16[8,16,1920]{2,1,0:T(8,128)(2,1)S(1)}, u32[]{:S(2)}, u32[]{:S(2)}) async-start(bf16[8,16,1920]{2,1,0:T(8,128)(2,1)} %shard_map.111), calls=%async_computation | async-start | bytes 983040 | tf_op jit(solution)/shard_map/all_to_all | solution.py:254
  11.1 8.5 %all-to-all-done.rows_ref = bf16[8,16,1920]{2,1,0:T(8,128)(2,1)S(1)} async-done(((bf16[8,16,1920]{2,1,0:T(8,128)(2,1)}), bf16[8,16,1920]{2,1,0:T(8,128)(2,1)S(1)}, u32[]{:S(2)}, u32[]{:S(2)}) %all-to-all-start) | async-done | bytes 491552 | tf_op jit(solution)/shard_map/all_to_all | solution.py:254
  19.6 4.1 %shard_map.113 = (bf16[1792,384]{1,0:T(8,128)(2,1)}, bf16[1792,384]{1,0:T(8,128)(2,1)}) custom-call(s32[2]{0:T(128)S(1)} %slice.27.ids, bf16[7168,128]{1,0:T(8,128)(2,1)S(1)} %bitcast.55, bf16[7168,128]{1,0:T(8,128)(2,1)} %bitcast.59, bf16[128,7168]{1,0:T(8,128)(2,1)} %bitcast.61), custom_call_target="tpu_custom_call" | custom-call | bytes 8257536 | tf_op jit(solution)/shard_map/pallas_call | solution.py:216
  27.4 11.6 %all-to-all-start.1 = ((bf16[32,128,128]{2,1,0:T(8,128)(2,1)}), bf16[32,128,128]{2,1,0:T(8,128)(2,1)}, u32[]{:S(2)}, u32[]{:S(2)}) async-start(bf16[32,128,128]{2,1,0:T(8,128)(2,1)} %copy-done.13), calls=%async_computation.1 | async-start | bytes 2097152 | tf_op jit(solution)/shard_map/all_to_all | solution.py:286
  39.1 15.3 %collective-permute-done.refs_1_.refs_5_ = bf16[1792,384]{1,0:T(8,128)(2,1)S(1)} collective-permute-done((bf16[1792,384]{1,0:T(8,128)(2,1)}, bf16[1792,384]{1,0:T(8,128)(2,1)S(1)}, u32[]{:S(2)}, u32[]{:S(2)}) %collective-permute-start) | collective-permute-done | bytes 1376288 | tf_op jit(solution)/shard_map/ppermute | solution.py:25
  57.9 2.6 %shard_map.114 = (bf16[1792,384]{1,0:T(8,128)(2,1)S(1)}, bf16[1792,256]{1,0:T(8,128)(2,1)S(1)}, bf16[1792,128]{1,0:T(8,128)(2,1)S(1)}) custom-call(s32[2]{0:T(128)S(1)} %slice.28.ids, bf16[7168,128]{1,0:T(8,128)(2,1)S(1)} %bitcast.56, bf16[7168,128]{1,0:T(8,128)(2,1)} %bitcast.60, bf16[128,7168]{1,0:T(8,128)(2,1)} %bitcast.62), custom_call_target="tpu_custom_call" | custom-call | flops 14000000000 | bytes 8257536 | tf_op jit(solution)/shard_map/pallas_call | solution.py:216
  63.4 10.3 %collective-permute-done.2.refs_4_ = bf16[1792,128]{1,0:T(8,128)(2,1)S(1)} collective-permute-done((bf16[1792,128]{1,0:T(8,128)(2,1)S(1)}, bf16[1792,128]{1,0:T(8,128)(2,1)S(1)}, u32[]{:S(2)}, u32[]{:S(2)}) %collective-permute-start.2) | collective-permute-done | bytes 458784 | tf_op jit(solution)/shard_map/ppermute | solution.py:25
  79.7 20.2 %collective-permute-done.3.mate_ref = bf16[288,1792]{1,0:T(8,128)(2,1)} collective-permute-done((bf16[288,1792]{1,0:T(8,128)(2,1)}, bf16[288,1792]{1,0:T(8,128)(2,1)}, u32[]{:S(2)}, u32[]{:S(2)}) %collective-permute-start.3) | collective-permute-done | bytes 1032224 | tf_op jit(solution)/shard_map/ppermute | solution.py:25
  100.6 5.2 %shard_map.115 = (bf16[288,384]{1,0:T(8,128)(2,1)S(1)}, bf16[288,384]{1,0:T(8,128)(2,1)S(1)}, bf16[288,384]{1,0:T(8,128)(2,1)S(1)}, bf16[288,384]{1,0:T(8,128)(2,1)S(1)}) custom-call(s32[5]{0:T(128)S(1)} %stack.47.ids, bf16[288,1792]{1,0:T(8,128)(2,1)} %pad_maximum_fusion.own_ref, bf16[288,1792]{1,0:T(8,128)(2,1)} %collective-permute-done.3.mate_ref, ...), custom_call_target="tpu_custom_call" | custom-call | flops 1585446912 | bytes 8454144 | tf_op jit(solution)/shard_map/pallas_call | solution.py:216
  106.1 2.9 %collective-permute-start.6 = (bf16[288,384]{1,0:T(8,128)(2,1)S(1)}, bf16[288,384]{1,0:T(8,128)(2,1)S(1)}, u32[]{:S(2)}, u32[]{:S(2)}) collective-permute-start(bf16[288,384]{1,0:T(8,128)(2,1)S(1)} %get-tuple-element.44), channel_id=1, source_target_pairs={{0,192},{32,224},{64,128},{96,160},{128,64},{160,96},{192,0},{224,... | collective-permute-start | bytes 663560 | tf_op jit(solution)/shard_map/ppermute | solution.py:25
  110.3 3.5 %collective-permute-start.13 = (bf16[288,1792]{1,0:T(8,128)(2,1)}, bf16[288,1792]{1,0:T(8,128)(2,1)}, u32[]{:S(2)}, u32[]{:S(2)}) collective-permute-start(bf16[288,1792]{1,0:T(8,128)(2,1)} %collective-permute-done.3.mate_ref), channel_id=1, source_target_pairs={{0,16},{1,17},{2,18},{3,19},{4,20},{5,21},{6,22},{7,23},{8,24},{9,... | collective-permute-start | bytes 3096584 | tf_op jit(solution)/shard_map/ppermute | solution.py:25
  117.9 2.6 %collective-permute-start.8 = (bf16[288,256]{1,0:T(8,128)(2,1)S(1)}, bf16[288,256]{1,0:T(8,128)(2,1)S(1)}, u32[]{:S(2)}, u32[]{:S(2)}) collective-permute-start(bf16[288,256]{1,0:T(8,128)(2,1)S(1)} %get-tuple-element.48.refs_0_), channel_id=1, source_target_pairs={{0,64},{32,96},{64,0},{96,32},{128,192},{160,224},{192,128},{224,1... | collective-permute-start | bytes 442376 | tf_op jit(solution)/shard_map/ppermute | solution.py:25
  120.6 2.0 collective-permute-start.10
  123.9 5.8 %collective-permute-done.9.refs_2_ = bf16[288,256]{1,0:T(8,128)(2,1)S(1)} collective-permute-done((bf16[288,256]{1,0:T(8,128)(2,1)S(1)}, bf16[288,256]{1,0:T(8,128)(2,1)S(1)}, u32[]{:S(2)}, u32[]{:S(2)}) %collective-permute-start.9) | collective-permute-done | bytes 147488 | tf_op jit(solution)/shard_map/ppermute | solution.py:25
  131.6 3.2 %collective-permute-start.15 = (bf16[288,1792]{1,0:T(8,128)(2,1)S(1)}, bf16[288,1792]{1,0:T(8,128)(2,1)S(1)}, u32[]{:S(2)}, u32[]{:S(2)}) collective-permute-start(bf16[288,1792]{1,0:T(8,128)(2,1)S(1)} %broadcast_select_fusion.1.refs_0_), channel_id=1, source_target_pairs={{0,192},{32,224},{64,0},{96,32},{128,64},{160,96},{192,128},{224,1... | collective-permute-start | bytes 3096584 | tf_op jit(solution)/shard_map/ppermute | solution.py:21
  139.3 10.3 %collective-permute-done.13 = bf16[288,1792]{1,0:T(8,128)(2,1)} collective-permute-done((bf16[288,1792]{1,0:T(8,128)(2,1)}, bf16[288,1792]{1,0:T(8,128)(2,1)}, u32[]{:S(2)}, u32[]{:S(2)}) %collective-permute-start.13) | collective-permute-done | bytes 1032224 | tf_op jit(solution)/shard_map/ppermute | solution.py:25
  151.2 3.0 %collective-permute-start.17 = (bf16[288,1792]{1,0:T(8,128)(2,1)S(1)}, bf16[288,1792]{1,0:T(8,128)(2,1)}, u32[]{:S(2)}, u32[]{:S(2)}) collective-permute-start(bf16[288,1792]{1,0:T(8,128)(2,1)S(1)} %broadcast_select_fusion.refs_1_), channel_id=1, source_target_pairs={{0,192},{32,224},{64,0},{96,32},{128,64},{160,96},{192,128},{224,1... | collective-permute-start | bytes 3096584 | tf_op jit(solution)/shard_map/ppermute | solution.py:21
  154.2 2.1 %shard_map.118 = f32[288,896]{1,0:T(8,128)S(1)} custom-call(s32[5]{0:T(128)S(1)} %stack.47.ids, bf16[288,256]{1,0:T(8,128)(2,1)S(1)} %get-tuple-element.48.refs_0_, bf16[288,256]{1,0:T(8,128)(2,1)S(1)} %collective-permute-done.8.refs_1_, bf16[288,256]{1,0:T(8,128)(2,1)S(1)} %collective-permute-done.9.refs_2_, ...), custom_call_target="tpu_custom_call" | custom-call | flops 528482304 | bytes 6668288 | tf_op jit(solution)/shard_map/pallas_call | solution.py:216
  159.6 12.8 %all-to-all-start.2 = ((bf16[32,64,128]{2,1,0:T(8,128)(2,1)}), bf16[32,64,128]{2,1,0:T(8,128)(2,1)}, u32[]{:S(2)}, u32[]{:S(2)}) async-start(bf16[32,64,128]{2,1,0:T(8,128)(2,1)} %maximum_maximum_fusion), calls=%async_computation.2 | async-start | bytes 1048576 | tf_op jit(solution)/shard_map/all_to_all | solution.py:286
  172.5 3.2 %collective-permute-start.19 = (bf16[288,1792]{1,0:T(8,128)(2,1)}, bf16[288,1792]{1,0:T(8,128)(2,1)}, u32[]{:S(2)}, u32[]{:S(2)}) collective-permute-start(bf16[288,1792]{1,0:T(8,128)(2,1)} %collective-permute-done.17.refs_5_), channel_id=1, source_target_pairs={{0,192},{32,224},{64,0},{96,32},{128,64},{160,96},{192,128},{224,1... | collective-permute-start | bytes 3096584 | tf_op jit(solution)/shard_map/ppermute | solution.py:21
  175.7 2.1 collective-permute-start.20
  177.8 11.8 %all-to-all-done.2 = bf16[32,64,128]{2,1,0:T(8,128)(2,1)} async-done(((bf16[32,64,128]{2,1,0:T(8,128)(2,1)}), bf16[32,64,128]{2,1,0:T(8,128)(2,1)}, u32[]{:S(2)}, u32[]{:S(2)}) %all-to-all-start.2) | async-done | bytes 524320 | tf_op jit(solution)/shard_map/all_to_all | solution.py:286
  192.5 5.0 %all-to-all-start.3 = ((bf16[8,16,896]{2,1,0:T(8,128)(2,1)}), bf16[8,16,896]{2,1,0:T(8,128)(2,1)}, u32[]{:S(2)}, u32[]{:S(2)}) async-start(bf16[8,16,896]{2,1,0:T(8,128)(2,1)} %bitcast.67), calls=%async_computation.3 | async-start | bytes 458752 | tf_op jit(solution)/shard_map/all_to_all | solution.py:326
  200.9 8.6 %shard_map.119 = (bf16[7168,128]{1,0:T(8,128)(2,1)}, bf16[7168,128]{1,0:T(8,128)(2,1)}, bf16[128,7168]{1,0:T(8,128)(2,1)}) custom-call(s32[9]{0:T(128)S(1)} %concatenate.15.ids, bf16[288,1792]{1,0:T(8,128)(2,1)S(1)} %copy-done.10, bf16[288,1792]{1,0:T(8,128)(2,1)S(1)} %broadcast_select_fusion.refs_1_, bf16[288,1792]{1,0:T(8,128)(2,1)S(1)} %copy-done.15, ...), custom_call_target="tpu_custom_call" | custom-call | flops 1585446912 | bytes 14204928 | tf_op jit(solution)/shard_map/pallas_call | solution.py:216
  (115 shorter events, 46.9 us)
Async XLA Ops:
  5.1 14.5 %all-to-all-start = ((bf16[8,16,1920]{2,1,0:T(8,128)(2,1)}), bf16[8,16,1920]{2,1,0:T(8,128)(2,1)S(1)}, u32[]{:S(2)}, u32[]{:S(2)}) async-start(bf16[8,16,1920]{2,1,0:T(8,128)(2,1)} %shard_map.111), calls=%async_computation | async-start | bytes 983040 | tf_op jit(solution)/shard_map/all_to_all | solution.py:254
  23.8 30.6 %collective-permute-start = (bf16[1792,384]{1,0:T(8,128)(2,1)}, bf16[1792,384]{1,0:T(8,128)(2,1)S(1)}, u32[]{:S(2)}, u32[]{:S(2)}) collective-permute-start(bf16[1792,384]{1,0:T(8,128)(2,1)} %get-tuple-element.35), channel_id=1, source_target_pairs={{0,64},{32,96},{64,0},{96,32},{128,192},{160,224},{192,128},{224,1... | collective-permute-start | bytes 4128776 | tf_op jit(solution)/shard_map/ppermute | solution.py:25
  24.3 31.6 %collective-permute-start.1 = (bf16[1792,384]{1,0:T(8,128)(2,1)}, bf16[1792,384]{1,0:T(8,128)(2,1)S(1)}, u32[]{:S(2)}, u32[]{:S(2)}) collective-permute-start(bf16[1792,384]{1,0:T(8,128)(2,1)} %get-tuple-element.36), channel_id=1, source_target_pairs={{0,192},{32,224},{64,128},{96,160},{128,64},{160,96},{192,0},{224,... | collective-permute-start | bytes 4128776 | tf_op jit(solution)/shard_map/ppermute | solution.py:25
  27.4 46.3 %all-to-all-start.1 = ((bf16[32,128,128]{2,1,0:T(8,128)(2,1)}), bf16[32,128,128]{2,1,0:T(8,128)(2,1)}, u32[]{:S(2)}, u32[]{:S(2)}) async-start(bf16[32,128,128]{2,1,0:T(8,128)(2,1)} %copy-done.13), calls=%async_computation.1 | async-start | bytes 2097152 | tf_op jit(solution)/shard_map/all_to_all | solution.py:286
  62.6 11.2 %collective-permute-start.2 = (bf16[1792,128]{1,0:T(8,128)(2,1)S(1)}, bf16[1792,128]{1,0:T(8,128)(2,1)S(1)}, u32[]{:S(2)}, u32[]{:S(2)}) collective-permute-start(bf16[1792,128]{1,0:T(8,128)(2,1)S(1)} %get-tuple-element.38), channel_id=1, source_target_pairs={{0,128},{32,160},{64,192},{96,224},{128,0},{160,32},{192,64},{224,... | collective-permute-start | bytes 1376264 | tf_op jit(solution)/shard_map/ppermute | solution.py:25
  77.3 22.6 %collective-permute-start.3 = (bf16[288,1792]{1,0:T(8,128)(2,1)}, bf16[288,1792]{1,0:T(8,128)(2,1)}, u32[]{:S(2)}, u32[]{:S(2)}) collective-permute-start(bf16[288,1792]{1,0:T(8,128)(2,1)} %pad_maximum_fusion.own_ref), channel_id=1, source_target_pairs={{0,32},{32,0},{64,96},{96,64},{128,160},{160,128},{192,224},{224,1... | collective-permute-start | bytes 3096584 | tf_op jit(solution)/shard_map/ppermute | solution.py:25
  79.0 21.6 %collective-permute-start.4 = (bf16[1792,256]{1,0:T(8,128)(2,1)S(1)}, bf16[1792,256]{1,0:T(8,128)(2,1)S(1)}, u32[]{:S(2)}, u32[]{:S(2)}) collective-permute-start(bf16[1792,256]{1,0:T(8,128)(2,1)S(1)} %copy-done.23), channel_id=1, source_target_pairs={{0,128},{32,160},{64,192},{96,224},{128,0},{160,32},{192,64},{224,... | collective-permute-start | bytes 2752520 | tf_op jit(solution)/shard_map/ppermute | solution.py:25
  99.9 29.8 %collective-permute-start.11 = (bf16[288,1792]{1,0:T(8,128)(2,1)}, bf16[288,1792]{1,0:T(8,128)(2,1)}, u32[]{:S(2)}, u32[]{:S(2)}) collective-permute-start(bf16[288,1792]{1,0:T(8,128)(2,1)} %pad_maximum_fusion.own_ref), channel_id=1, source_target_pairs={{0,16},{1,17},{2,18},{3,19},{4,20},{5,21},{6,22},{7,23},{8,24},{9,... | collective-permute-start | bytes 3096584 | tf_op jit(solution)/shard_map/ppermute | solution.py:25
  105.8 8.1 %collective-permute-start.5 = (bf16[288,384]{1,0:T(8,128)(2,1)S(1)}, bf16[288,384]{1,0:T(8,128)(2,1)S(1)}, u32[]{:S(2)}, u32[]{:S(2)}) collective-permute-start(bf16[288,384]{1,0:T(8,128)(2,1)S(1)} %get-tuple-element.43), channel_id=1, source_target_pairs={{0,64},{32,96},{64,0},{96,32},{128,192},{160,224},{192,128},{224,1... | collective-permute-start | bytes 663560 | tf_op jit(solution)/shard_map/ppermute | solution.py:25
  106.1 9.0 %collective-permute-start.6 = (bf16[288,384]{1,0:T(8,128)(2,1)S(1)}, bf16[288,384]{1,0:T(8,128)(2,1)S(1)}, u32[]{:S(2)}, u32[]{:S(2)}) collective-permute-start(bf16[288,384]{1,0:T(8,128)(2,1)S(1)} %get-tuple-element.44), channel_id=1, source_target_pairs={{0,192},{32,224},{64,128},{96,160},{128,64},{160,96},{192,0},{224,... | collective-permute-start | bytes 663560 | tf_op jit(solution)/shard_map/ppermute | solution.py:25
  109.0 8.0 %collective-permute-start.7 = (bf16[288,384]{1,0:T(8,128)(2,1)S(1)}, bf16[288,384]{1,0:T(8,128)(2,1)S(1)}, u32[]{:S(2)}, u32[]{:S(2)}) collective-permute-start(bf16[288,384]{1,0:T(8,128)(2,1)S(1)} %get-tuple-element.45), channel_id=1, source_target_pairs={{0,128},{32,160},{64,192},{96,224},{128,0},{160,32},{192,64},{224,... | collective-permute-start | bytes 663560 | tf_op jit(solution)/shard_map/ppermute | solution.py:25
  110.3 39.3 %collective-permute-start.13 = (bf16[288,1792]{1,0:T(8,128)(2,1)}, bf16[288,1792]{1,0:T(8,128)(2,1)}, u32[]{:S(2)}, u32[]{:S(2)}) collective-permute-start(bf16[288,1792]{1,0:T(8,128)(2,1)} %collective-permute-done.3.mate_ref), channel_id=1, source_target_pairs={{0,16},{1,17},{2,18},{3,19},{4,20},{5,21},{6,22},{7,23},{8,24},{9,... | collective-permute-start | bytes 3096584 | tf_op jit(solution)/shard_map/ppermute | solution.py:25
  120.5 9.2 %collective-permute-start.9 = (bf16[288,256]{1,0:T(8,128)(2,1)S(1)}, bf16[288,256]{1,0:T(8,128)(2,1)S(1)}, u32[]{:S(2)}, u32[]{:S(2)}) collective-permute-start(bf16[288,256]{1,0:T(8,128)(2,1)S(1)} %get-tuple-element.48.refs_0_), channel_id=1, source_target_pairs={{0,192},{32,224},{64,128},{96,160},{128,64},{160,96},{192,0},{224,... | collective-permute-start | bytes 442376 | tf_op jit(solution)/shard_map/ppermute | solution.py:25
  120.6 9.1 %collective-permute-start.10 = (bf16[288,256]{1,0:T(8,128)(2,1)S(1)}, bf16[288,256]{1,0:T(8,128)(2,1)S(1)}, u32[]{:S(2)}, u32[]{:S(2)}) collective-permute-start(bf16[288,256]{1,0:T(8,128)(2,1)S(1)} %get-tuple-element.48.refs_0_), channel_id=1, source_target_pairs={{0,128},{32,160},{64,192},{96,224},{128,0},{160,32},{192,64},{224,... | collective-permute-start | bytes 442376 | tf_op jit(solution)/shard_map/ppermute | solution.py:25
  131.5 25.0 %collective-permute-start.14 = (bf16[288,1792]{1,0:T(8,128)(2,1)S(1)}, bf16[288,1792]{1,0:T(8,128)(2,1)S(1)}, u32[]{:S(2)}, u32[]{:S(2)}) collective-permute-start(bf16[288,1792]{1,0:T(8,128)(2,1)S(1)} %broadcast_select_fusion.1.refs_0_), channel_id=1, source_target_pairs={{0,64},{32,96},{64,128},{96,160},{128,192},{160,224},{192,0},{224,... | collective-permute-start | bytes 3096584 | tf_op jit(solution)/shard_map/ppermute | solution.py:21
  131.6 25.0 %collective-permute-start.15 = (bf16[288,1792]{1,0:T(8,128)(2,1)S(1)}, bf16[288,1792]{1,0:T(8,128)(2,1)S(1)}, u32[]{:S(2)}, u32[]{:S(2)}) collective-permute-start(bf16[288,1792]{1,0:T(8,128)(2,1)S(1)} %broadcast_select_fusion.1.refs_0_), channel_id=1, source_target_pairs={{0,192},{32,224},{64,0},{96,32},{128,64},{160,96},{192,128},{224,1... | collective-permute-start | bytes 3096584 | tf_op jit(solution)/shard_map/ppermute | solution.py:21
  137.6 18.8 %collective-permute-start.12 = (bf16[288,896]{1,0:T(8,128)(2,1)S(1)}, bf16[288,896]{1,0:T(8,128)(2,1)S(1)}, u32[]{:S(2)}, u32[]{:S(2)}) collective-permute-start(bf16[288,896]{1,0:T(8,128)(2,1)S(1)} %shard_map.117), channel_id=1, source_target_pairs={{0,32},{32,0},{64,96},{96,64},{128,160},{160,128},{192,224},{224,1... | collective-permute-start | bytes 1548296 | tf_op jit(solution)/shard_map/ppermute | solution.py:25
  150.9 26.9 %collective-permute-start.16 = (bf16[288,1792]{1,0:T(8,128)(2,1)S(1)}, bf16[288,1792]{1,0:T(8,128)(2,1)}, u32[]{:S(2)}, u32[]{:S(2)}) collective-permute-start(bf16[288,1792]{1,0:T(8,128)(2,1)S(1)} %broadcast_select_fusion.refs_1_), channel_id=1, source_target_pairs={{0,64},{32,96},{64,128},{96,160},{128,192},{160,224},{192,0},{224,... | collective-permute-start | bytes 3096584 | tf_op jit(solution)/shard_map/ppermute | solution.py:21
  151.2 21.3 %collective-permute-start.17 = (bf16[288,1792]{1,0:T(8,128)(2,1)S(1)}, bf16[288,1792]{1,0:T(8,128)(2,1)}, u32[]{:S(2)}, u32[]{:S(2)}) collective-permute-start(bf16[288,1792]{1,0:T(8,128)(2,1)S(1)} %broadcast_select_fusion.refs_1_), channel_id=1, source_target_pairs={{0,192},{32,224},{64,0},{96,32},{128,64},{160,96},{192,128},{224,1... | collective-permute-start | bytes 3096584 | tf_op jit(solution)/shard_map/ppermute | solution.py:21
  159.6 30.0 %all-to-all-start.2 = ((bf16[32,64,128]{2,1,0:T(8,128)(2,1)}), bf16[32,64,128]{2,1,0:T(8,128)(2,1)}, u32[]{:S(2)}, u32[]{:S(2)}) async-start(bf16[32,64,128]{2,1,0:T(8,128)(2,1)} %maximum_maximum_fusion), calls=%async_computation.2 | async-start | bytes 1048576 | tf_op jit(solution)/shard_map/all_to_all | solution.py:286
  172.4 26.3 %collective-permute-start.18 = (bf16[288,1792]{1,0:T(8,128)(2,1)S(1)}, bf16[288,1792]{1,0:T(8,128)(2,1)}, u32[]{:S(2)}, u32[]{:S(2)}) collective-permute-start(bf16[288,1792]{1,0:T(8,128)(2,1)S(1)} %copy-done.15), channel_id=1, source_target_pairs={{0,64},{32,96},{64,128},{96,160},{128,192},{160,224},{192,0},{224,... | collective-permute-start | bytes 3096584 | tf_op jit(solution)/shard_map/ppermute | solution.py:21
  172.5 27.2 %collective-permute-start.19 = (bf16[288,1792]{1,0:T(8,128)(2,1)}, bf16[288,1792]{1,0:T(8,128)(2,1)}, u32[]{:S(2)}, u32[]{:S(2)}) collective-permute-start(bf16[288,1792]{1,0:T(8,128)(2,1)} %collective-permute-done.17.refs_5_), channel_id=1, source_target_pairs={{0,192},{32,224},{64,0},{96,32},{128,64},{160,96},{192,128},{224,1... | collective-permute-start | bytes 3096584 | tf_op jit(solution)/shard_map/ppermute | solution.py:21
  175.7 21.9 %collective-permute-start.20 = (bf16[288,384]{1,0:T(8,128)(2,1)S(1)}, bf16[288,384]{1,0:T(8,128)(2,1)}, u32[]{:S(2)}, u32[]{:S(2)}) collective-permute-start(bf16[288,384]{1,0:T(8,128)(2,1)S(1)} %copy-done.21), channel_id=1, source_target_pairs={{0,16},{1,17},{2,18},{3,19},{4,20},{5,21},{6,22},{7,23},{8,24},{9,... | collective-permute-start | bytes 663560 | tf_op jit(solution)/shard_map/ppermute | solution.py:25
  192.5 17.0 %all-to-all-start.3 = ((bf16[8,16,896]{2,1,0:T(8,128)(2,1)}), bf16[8,16,896]{2,1,0:T(8,128)(2,1)}, u32[]{:S(2)}, u32[]{:S(2)}) async-start(bf16[8,16,896]{2,1,0:T(8,128)(2,1)} %bitcast.67), calls=%async_computation.3 | async-start | bytes 458752 | tf_op jit(solution)/shard_map/all_to_all | solution.py:326
  (28 other events, 336.3 us)
